TPU v7x, 128 devices: a whole 4x4x4 slice. The times are simulated.
128 devices in a mesh: img: 4 (over y_lo, core), tile: 32 (over x, y_hi, z).
Axes of the slice: x: 4, y: 4 (y_hi: 2, y_lo: 2; y = y_hi * 2 + y_lo), z: 4, core: 2. Of those that a mesh axis runs over, the one named last changes fastest.
Arguments:
- tiles: bfloat16 [32768, 1152], P(('img', 'tile')), may hold values from -6 to 6
- tile_image: int32 [128], P(('img', 'tile')), may hold values from 0 to 1
- guide: bfloat16 [8, 512, 1152], P('img', 'tile'), may hold values from -160 to 160
- gain: float32 [1152], replicated, may hold values from 0.5 to 1.5
- w_query: bfloat16 [1152, 1152], replicated, may hold values from -0.1875 to 0.1875
- w_key: bfloat16 [1152, 1152], replicated, may hold values from -0.1875 to 0.1875
- w_value: bfloat16 [1152, 1152], replicated, may hold values from -0.1875 to 0.1875
- w_out: bfloat16 [1152, 1152], replicated, may hold values from -0.1875 to 0.1875
- grad_out: bfloat16 [32768, 1152], P(('img', 'tile')), may hold values from -24 to 24
Outputs:
- grad_tiles: bfloat16 [32768, 1152], P(('img', 'tile'))
- grad_guide: bfloat16 [8, 512, 1152], P('img', 'tile')
- grad_weights: float32 [4, 1152, 1152], P(None, ('img', 'tile'))
- grad_gain: float32 [1152], replicated
Inputs may be any that keep to these rules, and one draw needn't show every extreme that they name: `tile_image`: image of each tile within its own img group of 2 images.
All inputs are finite; a program needn't handle non-finite values.
Results may differ from a plain program's by a relative error of at most 0.034.
The roundings to bfloat16 on the way count: a program that leaves them out, or rounds other values in their place, can miss the bound.
Values may be sent and summed in bfloat16 or wider, within the bound.
No kernel may reach another device: no remote copies, remote signals or barrier semaphores. Data moves between devices by JAX's collectives and lax.ppermute only.
A program may use at most 128 MiB of HBM per device.

v0:
```python
import jax
import jax.numpy as jnp
from jax import lax
from jax.experimental import pallas as pl
from jax.experimental.pallas import tpu as pltpu
from jax.sharding import Mesh, PartitionSpec as P

HEADS = 16
HD = 72
HP = 128
D = 1152
G = 512
F32 = jnp.float32
BF16 = jnp.bfloat16
TILE_AXES = ("x", "yh", "z")
CHIP_AXES = ("yl", "x", "yh", "z")
SWAP = [(0, 1), (1, 0)]
PER_STEP = 2


def dot(a, b, ca, cb):
    return lax.dot_general(a, b, (((ca,), (cb,)), ((), ())), preferred_element_type=F32)


def spread_heads_kernel(q_ref, d_ref, qo_ref, do_ref):
    for src, dst in ((q_ref, qo_ref), (d_ref, do_ref)):
        dst[...] = jnp.zeros_like(dst)
        for h in range(HEADS):
            dst[:, h * HP : h * HP + HD] = src[:, h * HD : (h + 1) * HD]


def spread_heads(q, d):
    rows = q.shape[0]
    return pl.pallas_call(
        spread_heads_kernel,
        out_shape=[jax.ShapeDtypeStruct((rows, HEADS * HP), BF16)] * 2,
        name="spread_heads",
    )(q, d)


def spread_weights_kernel(k_ref, v_ref, o_ref):
    o_ref[...] = jnp.zeros_like(o_ref)
    for h in range(HEADS):
        o_ref[:, 2 * h * HP : 2 * h * HP + HD] = k_ref[:, h * HD : (h + 1) * HD]
        o_ref[:, (2 * h + 1) * HP : (2 * h + 1) * HP + HD] = v_ref[:, h * HD : (h + 1) * HD]


def spread_weights(w_key, w_value):
    step = 128
    return pl.pallas_call(
        spread_weights_kernel,
        grid=(D // step,),
        in_specs=[pl.BlockSpec((step, D), lambda i: (i, 0))] * 2,
        out_specs=pl.BlockSpec((step, 2 * HEADS * HP), lambda i: (i, 0)),
        out_shape=jax.ShapeDtypeStruct((D, 2 * HEADS * HP), BF16),
        name="spread_weights",
    )(w_key, w_value)


def attention_kernel(img_ref, g_ref, w_ref, q_ref, d_ref, pay_ref, o_ref, dq_ref, o_scr, dq_scr):
    step = pl.program_id(0)
    scale = HD ** (-0.5)
    guide = g_ref[...].reshape(G, D)
    kv_all = dot(guide, w_ref[...], 1, 0).astype(BF16)
    flag = jnp.full((4, G), img_ref[0], jnp.int32).astype(F32)
    for n in range(PER_STEP):
        k = kv_all[:, 2 * n * HP : (2 * n + 1) * HP]
        v = kv_all[:, (2 * n + 1) * HP : (2 * n + 2) * HP]
        q, d = q_ref[:, n * HP : (n + 1) * HP], d_ref[:, n * HP : (n + 1) * HP]
        scores = dot(q, k, 1, 1) * scale
        dprob = dot(d, v, 1, 1)
        top = jnp.max(scores, axis=-1, keepdims=True)
        expo = jnp.exp(scores - top)
        probs = expo * (1.0 / jnp.sum(expo, axis=-1, keepdims=True))
        pb = probs.astype(BF16)
        weighted = probs * dprob
        delta = jnp.sum(weighted, axis=-1, keepdims=True)
        ds = ((weighted - probs * delta) * scale).astype(BF16)
        o_scr[step * PER_STEP + n] = dot(pb, v, 1, 0).astype(BF16)
        dq_scr[step * PER_STEP + n] = dot(ds, k, 1, 0).astype(BF16)
        dk = dot(q, ds, 0, 0)
        dv = dot(d, pb, 0, 0)
        for i in range(2):
            for j, part in enumerate((dk, dv)):
                rows = jnp.concatenate([part[36 * i : 36 * i + 36], flag], axis=0)
                pay_ref[2 * n + i, j] = rows.astype(BF16)

    @pl.when(step == HEADS // PER_STEP - 1)
    def _():
        for n in range(HEADS):
            o_ref[:, n * HD : (n + 1) * HD] = o_scr[n][:, :HD]
            dq_ref[:, n * HD : (n + 1) * HD] = dq_scr[n][:, :HD]


def attention(img, whole, w_kv, q, d):
    t = q.shape[0]
    grid_spec = pltpu.PrefetchScalarGridSpec(
        num_scalar_prefetch=1,
        grid=(HEADS // PER_STEP,),
        in_specs=[
            pl.BlockSpec((32, pl.Squeezed(), 16, D), lambda h, i: (0, i[0], 0, 0)),
            pl.BlockSpec((D, 2 * PER_STEP * HP), lambda h, i: (0, h)),
            pl.BlockSpec((t, PER_STEP * HP), lambda h, i: (0, h)),
            pl.BlockSpec((t, PER_STEP * HP), lambda h, i: (0, h)),
        ],
        out_specs=[
            pl.BlockSpec((2 * PER_STEP, 2, 40, G), lambda h, i: (h, 0, 0, 0)),
            pl.BlockSpec((t, D), lambda h, i: (0, 0)),
            pl.BlockSpec((t, D), lambda h, i: (0, 0)),
        ],
        scratch_shapes=[pltpu.VMEM((HEADS, t, HP), BF16), pltpu.VMEM((HEADS, t, HP), BF16)],
    )
    return pl.pallas_call(
        attention_kernel,
        grid_spec=grid_spec,
        out_shape=[
            jax.ShapeDtypeStruct((32, 2, 40, G), BF16),
            jax.ShapeDtypeStruct((t, D), BF16),
            jax.ShapeDtypeStruct((t, D), BF16),
        ],
        name="attention",
    )(img, whole, w_kv, q, d)


RING_AXES = ("x", ("yl", "yh"), "z")
ROWS = 576


def ring_send(block, axis, distance):
    at = (0, 2, 1, 3) if isinstance(axis, tuple) else (0, 1, 2, 3)
    return lax.ppermute(block, axis, [(at[i], at[(i + distance) % 4]) for i in range(4)])


def eight_and_one(rows):
    return jnp.where(rows < 512, rows // 8 * 9 + rows % 8, (rows - 512) * 9 + 8)


def wanted_rows(core):
    row = eight_and_one(jnp.arange(ROWS, dtype=jnp.int32))
    return (row // 288 * 576 + core * 288 + row % 288)[:, None]


def one_hot(want, width):
    return (want == lax.broadcasted_iota(jnp.int32, (want.shape[0], width), 1)).astype(BF16)


def weight_parts_kernel(
    want_ref, hid_ref, o_ref, o2_ref, dq_ref, dq2_ref, g_ref, g2_ref, send_ref, ninth_ref
):
    o = jnp.concatenate([o_ref[...], o2_ref[...]], axis=0)
    dq = jnp.concatenate([dq_ref[...], dq2_ref[...]], axis=0)
    g = jnp.concatenate([g_ref[...], g2_ref[...]], axis=0)
    o_rows = dot(one_hot(want_ref[...], D), o, 1, 1).astype(BF16)
    parts = (dot(hid_ref[...], dq, 1, 0), dot(o_rows, g, 1, 0))
    for m, part in enumerate(parts):
        send_ref[:, m] = part[:512].reshape(64, 8, D).astype(BF16)
        ninth_ref[:, m * D : (m + 1) * D] = part[512:]


def weight_parts(*args):
    vmem = pl.BlockSpec(memory_space=pltpu.VMEM)
    return pl.pallas_call(
        weight_parts_kernel,
        grid=(1,),
        in_specs=[vmem] * 8,
        out_specs=[
            pl.BlockSpec((64, 2, 8, D), lambda i: (0, 0, 0, 0)),
            pl.BlockSpec((64, 2 * D), lambda i: (0, 0)),
        ],
        out_shape=[
            jax.ShapeDtypeStruct((64, 3, 8, D), BF16),
            jax.ShapeDtypeStruct((64, 2 * D), F32),
        ],
        name="weight_parts",
    )(*args)


def image_sums_kernel(core_ref, got_ref, g_ref, mine_ref, theirs_ref, tok_ref, scr):
    def add(s, sums):
        terms = got_ref[s].astype(F32)
        first = terms[:, 36:37, :] == 0.0
        zero = jnp.zeros_like(terms)
        return sums[0] + jnp.where(first, terms, zero), sums[1] + jnp.where(first, zero, terms)

    zero = jnp.zeros((2, 40, G), F32)
    sums = lax.fori_loop(0, 32, add, (zero, zero))
    rounded = [x.reshape(80, G).astype(BF16) for x in sums]
    prod = dot(rounded[0], g_ref[:, 0].reshape(G, D), 1, 0)
    prod = prod + dot(rounded[1], g_ref[:, 1].reshape(G, D), 1, 0)
    scr[...] = jnp.concatenate([prod, jnp.zeros((48, D), F32)], axis=0).T
    core = core_ref[0]
    for n in range(2):
        for out, c in ((mine_ref, core), (theirs_ref, 1 - core)):
            start = pl.multiple_of(n * 576 + c * 288, 32)
            out[n * 288 : n * 288 + 288] = scr[pl.ds(start, 288), :]
    both = jnp.concatenate([x.astype(F32) for x in rounded] + [jnp.zeros((96, G), F32)], axis=0)
    tok_ref[...] = both.T


def image_sums(core, got, whole):
    vmem = pl.BlockSpec(memory_space=pltpu.VMEM)
    return pl.pallas_call(
        image_sums_kernel,
        in_specs=[pl.BlockSpec(memory_space=pltpu.SMEM), vmem, vmem],
        out_specs=[vmem] * 3,
        out_shape=[
            jax.ShapeDtypeStruct((ROWS, 128), F32),
            jax.ShapeDtypeStruct((ROWS, 128), F32),
            jax.ShapeDtypeStruct((G, 256), F32),
        ],
        scratch_shapes=[pltpu.VMEM((D, 128), F32)],
        name="image_sums",
    )(core, got, whole)


SLOTS = [(r, 256) for r in range(1, 8)] + [(r, 384) for r in range(1, 8)]
SLOTS += [(r, 1024) for r in range(4)]


def fill_rest_kernel(send_ref, mine_ref, got_ref, tok_ref, ninth_ref, out_ref, scr):
    scr[...] = jnp.zeros_like(scr)
    total = mine_ref[...] + got_ref[...]
    high = total.astype(BF16)
    low = (total - high.astype(F32)).astype(BF16)
    want = eight_and_one(lax.broadcasted_iota(jnp.int32, (ROWS, ROWS), 0))
    order = (want == lax.broadcasted_iota(jnp.int32, (ROWS, ROWS), 1)).astype(BF16)
    moved = dot(order, jnp.concatenate([high, low], axis=1), 1, 0)
    scr[:, :, :256] = moved[:512].reshape(64, 8, 256)
    scr[:, 0, 256:512] = moved[512:]
    tok = tok_ref[...].reshape(32, 16, 256)
    for n in range(2):
        scr[32 * n : 32 * n + 32, :, 512:768] = tok[:, :8]
        scr[32 * n : 32 * n + 32, :, 768:1024] = tok[:, 8:]
    for b, (row, lane) in enumerate(SLOTS):
        scr[:, row, lane : lane + 128] = ninth_ref[:, 128 * b : 128 * b + 128]
    out_ref[:, 0] = scr[...].astype(BF16)


def fill_rest(send, mine, got, tok, ninth):
    vmem = pl.BlockSpec(memory_space=pltpu.VMEM)
    return pl.pallas_call(
        fill_rest_kernel,
        grid=(1,),
        in_specs=[pl.BlockSpec(memory_space=pl.ANY)] + [vmem] * 4,
        out_specs=pl.BlockSpec((64, 1, 8, D), lambda i: (0, 2, 0, 0)),
        out_shape=jax.ShapeDtypeStruct((64, 3, 8, D), BF16),
        scratch_shapes=[pltpu.VMEM((64, 8, D), F32)],
        input_output_aliases={0: 0},
        name="fill_rest",
    )(send, mine, got, tok, ninth)


def finish_kernel(yl_ref, recv_ref, wk_ref, wv_ref, gw_ref, gg_ref, scr):
    def add(j, sums):
        return tuple(s + recv_ref[j, n].astype(F32) for n, s in enumerate(sums))

    sums = lax.fori_loop(0, 64, add, tuple(jnp.zeros((8, D), F32) for _ in range(3)))
    gw_ref[0, :8] = sums[0]
    gw_ref[3, :8] = sums[1]
    for b, (row, lane) in enumerate(SLOTS):
        at = 128 * (b % 9)
        gw_ref[3 * (b // 9), 8:9, at : at + 128] = sums[2][row : row + 1, lane : lane + 128]
    base = yl_ref[0] * 32
    for t in range(32):
        cols = slice(36 * t, 36 * t + 36)
        x = recv_ref[t, 2, :, :512].astype(F32) + recv_ref[32 + t, 2, :, :512].astype(F32)
        eight = x[:, :128] + x[:, 128:256]
        one = x[:1, 256:384] + x[:1, 384:512]
        for n in range(2):
            gw_ref[1 + n, :8, cols] = eight[:, 40 * n : 40 * n + 36]
            gw_ref[1 + n, 8:9, cols] = one[:, 40 * n : 40 * n + 36]
        near = recv_ref[base + t, 2, :, 512:1024].astype(F32)
        for half in range(2):
            for m in range(2):
                for n in range(2):
                    lane = 256 * half + 80 * m + 40 * n
                    row = 16 * m + 8 * half
                    scr[n, row : row + 8, cols] = near[:, lane : lane + 36]
    grad = dot(scr[0].astype(BF16), wk_ref[...], 1, 1) + dot(scr[1].astype(BF16), wv_ref[...], 1, 1)
    gg_ref[...] = grad.astype(BF16)


def finish(yl, recv, w_key, w_value):
    vmem = pl.BlockSpec(memory_space=pltpu.VMEM)
    return pl.pallas_call(
        finish_kernel,
        in_specs=[pl.BlockSpec(memory_space=pltpu.SMEM), vmem, vmem, vmem],
        out_specs=[vmem] * 2,
        out_shape=[jax.ShapeDtypeStruct((4, 9, D), F32), jax.ShapeDtypeStruct((32, D), BF16)],
        scratch_shapes=[pltpu.VMEM((2, 32, D), F32)],
        name="finish",
    )(yl, recv, w_key, w_value)


def all_sum(x):
    x = x + lax.ppermute(x, "c", SWAP)
    for axes in RING_AXES:
        one, two, three = (ring_send(x, axes, n) for n in (1, 2, 3))
        x = (x + two) + (one + three)
    return x


def on_device(tiles, tile_image, guide, gain, w_query, w_key, w_value, w_out, grad_out):
    core = lax.axis_index("c")
    yl = lax.axis_index("yl")
    whole = lax.all_to_all(
        jnp.broadcast_to(guide, (32, *guide.shape)), TILE_AXES, 0, 0, tiled=True
    )
    xf = tiles.astype(F32)
    rstd = lax.rsqrt(jnp.mean(xf * xf, axis=-1, keepdims=True) + 1e-06)
    normed = xf * rstd
    hidden = (normed * gain).astype(BF16)
    query = dot(hidden, w_query, 1, 0).astype(BF16)
    dout = dot(grad_out, w_out, 1, 1).astype(BF16)
    q_wide, d_wide = spread_heads(query, dout)
    w_kv = spread_weights(w_key, w_value)
    want = wanted_rows(core)
    hid_both = jnp.concatenate([hidden, lax.ppermute(hidden, "c", SWAP)], axis=0)
    hid_rows = dot(one_hot(want, D), hid_both, 1, 1).astype(BF16)
    grad_got = lax.ppermute(grad_out, "c", SWAP)
    q_wide, hid_rows = lax.optimization_barrier((q_wide, hid_rows))

    pay, outv, dq = attention(tile_image, whole, w_kv, q_wide, d_wide)
    got = lax.all_to_all(pay, TILE_AXES, 0, 0, tiled=True)

    dq_got = lax.ppermute(dq, "c", SWAP)
    out_got = lax.ppermute(outv, "c", SWAP)
    send, ninth = weight_parts(want, hid_rows, outv, out_got, dq, dq_got, grad_out, grad_got)
    dh = dot(dq, w_query, 1, 1)
    gain_part = jnp.sum(dh * normed, axis=0)
    dn = dh * gain
    grad_tiles = (rstd * (dn - normed * jnp.mean(dn * normed, axis=-1, keepdims=True))).astype(BF16)

    got, ninth, gain_part = lax.optimization_barrier((got, ninth, gain_part))
    mine, theirs, tok = image_sums(core[None], got, whole)
    send = fill_rest(send, mine, lax.ppermute(theirs, "c", SWAP), tok, ninth)
    send, gain_part = lax.optimization_barrier((send, gain_part))
    recv = lax.all_to_all(send, CHIP_AXES, 0, 0, tiled=True)
    grad_gain = all_sum(gain_part)
    grad_weights, grad_guide = finish(yl[None], recv, w_key, w_value)
    return (grad_tiles, grad_guide.reshape(guide.shape), grad_weights, grad_gain)


def solution(mesh):
    fine = Mesh(mesh.devices.reshape(2, 2, 4, 2, 4), ("yl", "c", "x", "yh", "z"))
    every = ("yl", "c", "x", "yh", "z")
    return jax.shard_map(
        on_device,
        mesh=fine,
        in_specs=(
            P(every, None),
            P(every),
            P(("yl", "c"), TILE_AXES, None),
            P(),
            P(),
            P(),
            P(),
            P(),
            P(every, None),
        ),
        out_specs=(
            P(every, None),
            P(("yl", "c"), TILE_AXES, None),
            P(None, every, None),
            P(),
        ),
        check_vma=False,
    )
```

profile of v0, /device:TPU:2, one launch (start us, length us, event | category | flops | bytes accessed | tf_op | source)
XLA Modules:
  0.0 203.3 jit_solution(10619553027215276962)
XLA Ops:
  0.6 0.0 copy-start
  0.6 2.6 %broadcast_in_dim.6 = bf16[32,2,16,1152]{3,2,1,0:T(8,128)(2,1)} broadcast(bf16[2,16,1152]{2,1,0:T(8,128)(2,1)} %param.11), dimensions={1,2,3} | broadcast | bytes 2433024 | tf_op jit(solution)/shard_map/broadcast_in_dim | solution.py:307
  3.2 0.0 copy-start.1
  3.2 0.0 copy-start.3
  3.2 11.3 %all-to-all-start = ((bf16[32,2,16,1152]{3,2,1,0:T(8,128)(2,1)}), bf16[32,2,16,1152]{3,2,1,0:T(8,128)(2,1)}, u32[]{:S(2)}, u32[]{:S(2)}) async-start(bf16[32,2,16,1152]{3,2,1,0:T(8,128)(2,1)} %broadcast_in_dim.6), calls=%async_computation | async-start | bytes 4718592 | tf_op jit(solution)/shard_map/all_to_all | solution.py:306
  14.5 0.0 copy-done.1
  14.5 0.2 fusion.13
  14.7 0.0 copy-done.3
  14.7 1.0 fusion.7
  15.8 0.0 collective-permute-start
  15.8 0.0 copy-done
  15.8 2.9 %convolution_convert_fusion.1.q_ref = bf16[256,1152]{1,0:T(8,128)(2,1)} fusion(bf16[256,1152]{1,0:T(8,128)(2,1)} %fusion.7, bf16[1152,1152]{1,0:T(8,128)(2,1)S(1)} %copy-done), kind=kOutput, calls=%fused_computation.3 | convolution fusion | flops 679772160 | bytes 3833856 | tf_op jit(solution)/shard_map/dot_general | solution.py:22
  19.3 3.8 %convolution_convert_fusion.d_ref = bf16[256,1152]{1,0:T(8,128)(2,1)} fusion(bf16[256,1152]{1,0:T(8,128)(2,1)} %g_ref.1, bf16[1152,1152]{1,0:T(8,128)(2,1)} %param.16), kind=kOutput, calls=%fused_computation.2 | convolution fusion | flops 679772160 | bytes 3833856 | tf_op jit(solution)/shard_map/dot_general | solution.py:22
  23.1 3.4 %spread_heads.1 = (bf16[256,2048]{1,0:T(8,128)(2,1)}, bf16[256,2048]{1,0:T(8,128)(2,1)}) custom-call(bf16[256,1152]{1,0:T(8,128)(2,1)} %convolution_convert_fusion.1.q_ref, bf16[256,1152]{1,0:T(8,128)(2,1)} %convolution_convert_fusion.d_ref), custom_call_target="tpu_custom_call" | custom-call | tf_op jit(solution)/shard_map/spread_heads/pallas_call | solution.py:34
  26.5 10.8 %spread_weights.1.w_ref = bf16[1152,4096]{1,0:T(8,128)(2,1)} custom-call(bf16[1152,1152]{1,0:T(8,128)(2,1)} %wk_ref.1, bf16[1152,1152]{1,0:T(8,128)(2,1)} %wv_ref.1), custom_call_target="tpu_custom_call" | custom-call | tf_op jit(solution)/shard_map/spread_weights/pallas_call | solution.py:50
  37.3 0.0 collective-permute-done
  37.3 3.0 %fusion.6.hid_ref = bf16[576,512]{1,0:T(8,128)(2,1)} fusion(s32[576]{0:T(1024)S(1)} %fusion.44, bf16[256,1152]{1,0:T(8,128)(2,1)} %collective-permute-done, bf16[256,1152]{1,0:T(8,128)(2,1)} %fusion.7), kind=kOutput, calls=%fused_computation.11 | convolution fusion | flops 682795008 | bytes 1771776 | tf_op jit(solution)/shard_map/dot_general | solution.py:22
  40.4 4.2 %all-to-all-done.g_ref = bf16[32,2,16,1152]{3,2,1,0:T(8,128)(2,1)} async-done(((bf16[32,2,16,1152]{3,2,1,0:T(8,128)(2,1)}), bf16[32,2,16,1152]{3,2,1,0:T(8,128)(2,1)}, u32[]{:S(2)}, u32[]{:S(2)}) %all-to-all-start) | async-done | bytes 2359328 | tf_op jit(solution)/shard_map/all_to_all | solution.py:306
  44.6 22.2 %attention.1 = (bf16[32,2,40,512]{3,2,1,0:T(8,128)(2,1)}, bf16[256,1152]{1,0:T(8,128)(2,1)}, bf16[256,1152]{1,0:T(8,128)(2,1)}) custom-call(s32[1]{0:T(128)S(6)} %copy.16.img_ref, bf16[32,2,16,1152]{3,2,1,0:T(8,128)(2,1)} %all-to-all-done.g_ref, bf16[1152,4096]{1,0:T(8,128)(2,1)} %spread_weights.1.w_ref, bf16[256,2048]{1,0:T(8,128)(2,1)} %get-tuple-element.24.q_ref, ...), custom_call_target="tpu_custom_call" | custom-call | tf_op jit(solution)/shard_map/attention/pallas_call | solution.py:113
  66.9 8.3 %all-to-all-start.1 = ((bf16[32,2,40,512]{3,2,1,0:T(8,128)(2,1)}), bf16[32,2,40,512]{3,2,1,0:T(8,128)(2,1)}, u32[]{:S(2)}, u32[]{:S(2)}) async-start(bf16[32,2,40,512]{3,2,1,0:T(8,128)(2,1)} %get-tuple-element.30), calls=%async_computation.1 | async-start | bytes 5242880 | tf_op jit(solution)/shard_map/all_to_all | solution.py:324
  75.2 0.1 collective-permute-start.3
  75.3 0.5 collective-permute-start.2
  75.8 0.1 collective-permute-start.1
  75.9 1.1 fusion.28.want_ref
  77.0 3.8 %fusion.12 = (f32[1152]{0:T(1024)}, f32[256]{0:T(256)S(1)}, f32[256,1152]{1,0:T(8,128)}) fusion(bf16[256,1152]{1,0:T(8,128)(2,1)S(1)} %copy-done.1, f32[256]{0:T(256)S(1)} %add_rsqrt_fusion, f32[1152]{0:T(1024)S(1)} %copy-done.3, bf16[256,1152]{1,0:T(8,128)(2,1)} %get-tuple-element.26.dq_ref, bf16[1152,1152]{1,0:T(8,128)(2,1)S(1)} %copy-done), kind=kOutput, calls=%fused_computation.17 | convolution fusion | flops 681540224 | bytes 5024768 | tf_op jit(solution)/shard_map/dot_general | solution.py:22
  80.7 0.0 collective-permute-done.3.g2_ref
  80.7 0.0 collective-permute-done.2.dq2_ref
  80.7 0.0 collective-permute-done.1.o2_ref
  80.7 6.4 %weight_parts.1 = (bf16[64,3,8,1152]{3,2,1,0:T(8,128)(2,1)}, f32[64,2304]{1,0:T(8,128)}) custom-call(s32[576,1]{1,0:T(8,128)} %fusion.28.want_ref, bf16[576,512]{1,0:T(8,128)(2,1)} %fusion.6.hid_ref, bf16[256,1152]{1,0:T(8,128)(2,1)} %get-tuple-element.28.o_ref, bf16[256,1152]{1,0:T(8,128)(2,1)} %collective-permute-done.1.o2_ref, ...), custom_call_target="tpu_custom_call" | custom-call | tf_op jit(solution)/shard_map/weight_parts/pallas_call | solution.py:162
  87.2 21.1 %all-to-all-done.1.got_ref = bf16[32,2,40,512]{3,2,1,0:T(8,128)(2,1)} async-done(((bf16[32,2,40,512]{3,2,1,0:T(8,128)(2,1)}), bf16[32,2,40,512]{3,2,1,0:T(8,128)(2,1)}, u32[]{:S(2)}, u32[]{:S(2)}) %all-to-all-start.1) | async-done | bytes 2621472 | tf_op jit(solution)/shard_map/all_to_all | solution.py:324
  108.3 6.3 %image_sums.1 = (f32[576,128]{1,0:T(8,128)}, f32[576,128]{1,0:T(8,128)}, f32[512,256]{1,0:T(8,128)}) custom-call(s32[1]{0:T(128)} %bitcast.1.core_ref, bf16[32,2,40,512]{3,2,1,0:T(8,128)(2,1)} %all-to-all-done.1.got_ref, bf16[32,2,16,1152]{3,2,1,0:T(8,128)(2,1)} %all-to-all-done.g_ref), custom_call_target="tpu_custom_call" | custom-call | tf_op jit(solution)/shard_map/image_sums/pallas_call | solution.py:202
  114.5 0.0 collective-permute-start.4
  114.5 1.8 collective-permute-done.4.got_ref
  116.3 0.0 copy-start.2
  116.3 0.7 copy-done.2
  117.1 3.3 %fill_rest.1 = bf16[64,3,8,1152]{3,2,1,0:T(8,128)(2,1)} custom-call(bf16[64,3,8,1152]{3,2,1,0:T(8,128)(2,1)} %get-tuple-element.29.send_ref, f32[576,128]{1,0:T(8,128)} %get-tuple-element.33.mine_ref, f32[576,128]{1,0:T(8,128)} %copy-done.2, f32[512,256]{1,0:T(8,128)} %get-tuple-element.35.tok_ref, ...), custom_call_target="tpu_custom_call", output_to_operand_aliasing={{}: (0, {})} | custom-call | tf_op jit(solution)/shard_map/fill_rest/pallas_call | solution.py:241
  120.4 0.0 copy-start.4
  120.4 9.3 %all-to-all-start.2 = ((bf16[64,3,8,1152]{3,2,1,0:T(8,128)(2,1)}), bf16[64,3,8,1152]{3,2,1,0:T(8,128)(2,1)}, u32[]{:S(2)}, u32[]{:S(2)}) async-start(bf16[64,3,8,1152]{3,2,1,0:T(8,128)(2,1)} %fill_rest.1), calls=%async_computation.2 | async-start | bytes 7077888 | tf_op jit(solution)/shard_map/all_to_all | solution.py:338
  129.7 0.0 copy-done.4
  129.7 0.1 collective-permute-start.5
  129.8 1.2 collective-permute-done.5
  130.9 2.1 %collective-permute-start.6 = (f32[1152]{0:T(1024)S(1)}, f32[1152]{0:T(1024)S(1)}, u32[]{:S(2)}, u32[]{:S(2)}) collective-permute-start(f32[1152]{0:T(1024)S(1)} %add.184), channel_id=1, source_target_pairs={{0,16},{8,24},{16,0},{24,8},{1,17},{9,25},{17,1},{25,9},{2,18},{10... | collective-permute-start | bytes 13832 | tf_op jit(solution)/shard_map/ppermute | solution.py:131
  133.1 0.0 collective-permute-start.7
  133.1 2.0 collective-permute-start.8
  135.1 41.7 %collective-permute-done.6 = f32[1152]{0:T(1024)S(1)} collective-permute-done((f32[1152]{0:T(1024)S(1)}, f32[1152]{0:T(1024)S(1)}, u32[]{:S(2)}, u32[]{:S(2)}) %collective-permute-start.6) | collective-permute-done | bytes 4640 | tf_op jit(solution)/shard_map/ppermute | solution.py:131
  176.7 0.0 collective-permute-done.7
  176.7 0.0 collective-permute-done.8
  176.8 1.4 collective-permute-start.10
  178.1 1.9 collective-permute-start.11
  180.1 0.2 collective-permute-start.9
  180.3 1.4 collective-permute-done.10
  181.7 0.1 collective-permute-done.11
  181.8 3.4 %collective-permute-done.9 = f32[1152]{0:T(1024)S(1)} collective-permute-done((f32[1152]{0:T(1024)S(1)}, f32[1152]{0:T(1024)S(1)}, u32[]{:S(2)}, u32[]{:S(2)}) %collective-permute-start.9) | collective-permute-done | bytes 4640 | tf_op jit(solution)/shard_map/ppermute | solution.py:131
  185.2 3.4 %collective-permute-start.12 = (f32[1152]{0:T(1024)S(1)}, f32[1152]{0:T(1024)S(1)}, u32[]{:S(2)}, u32[]{:S(2)}) collective-permute-start(f32[1152]{0:T(1024)S(1)} %add_add_fusion.1), channel_id=1, source_target_pairs={{0,2},{1,3},{2,0},{3,1},{4,6},{5,7},{6,4},{7,5},{8,10},{9,11},{10,... | collective-permute-start | bytes 13832 | tf_op jit(solution)/shard_map/ppermute | solution.py:131
  188.7 0.0 collective-permute-start.13
  188.7 3.2 %collective-permute-start.14 = (f32[1152]{0:T(1024)S(1)}, f32[1152]{0:T(1024)S(1)}, u32[]{:S(2)}, u32[]{:S(2)}) collective-permute-start(f32[1152]{0:T(1024)S(1)} %add_add_fusion.1), channel_id=1, source_target_pairs={{0,3},{1,0},{2,1},{3,2},{4,7},{5,4},{6,5},{7,6},{8,11},{9,8},{10,9... | collective-permute-start | bytes 13832 | tf_op jit(solution)/shard_map/ppermute | solution.py:131
  191.9 2.4 %fusion.11 = bf16[256,1152]{1,0:T(8,128)(2,1)} fusion(bf16[256,1152]{1,0:T(8,128)(2,1)S(1)} %copy-done.1, f32[256,1152]{1,0:T(8,128)} %get-tuple-element.48, f32[256]{0:T(256)S(1)} %broadcast_multiply_fusion, f32[1152]{0:T(1024)S(1)} %copy-done.3, f32[256]{0:T(256)S(1)} %add_rsqrt_fusion), kind=kLoop, calls=%fused_computation.16 | loop fusion | flops 2064384 | bytes 2365952 | tf_op jit(solution)/shard_map/convert_element_type | solution.py:332
  194.3 0.0 collective-permute-done.12
  194.3 0.0 collective-permute-done.13
  194.3 0.0 collective-permute-done.14
  194.3 0.6 add_add_fusion
  194.9 0.0 all-to-all-done.2.recv_ref
  194.9 6.6 %finish.1 = (f32[4,9,1152]{2,1,0:T(8,128)}, bf16[32,1152]{1,0:T(8,128)(2,1)}) custom-call(s32[1]{0:T(128)} %bitcast.yl_ref, bf16[64,3,8,1152]{3,2,1,0:T(8,128)(2,1)} %all-to-all-done.2.recv_ref, bf16[1152,1152]{1,0:T(8,128)(2,1)} %wk_ref.1, bf16[1152,1152]{1,0:T(8,128)(2,1)} %wv_ref.1), custom_call_target="tpu_custom_call" | custom-call | tf_op jit(solution)/shard_map/finish/pallas_call | solution.py:285
  201.6 1.7 copy.14
  (6 shorter events, 0.0 us)
Async XLA Ops:
  0.6 15.1 %copy-start = (bf16[1152,1152]{1,0:T(8,128)(2,1)S(1)}, bf16[1152,1152]{1,0:T(8,128)(2,1)}, u32[]{:S(2)}) copy-start(bf16[1152,1152]{1,0:T(8,128)(2,1)} %param.13) | copy-start | bytes 7962628
  3.2 11.3 %copy-start.1 = (bf16[256,1152]{1,0:T(8,128)(2,1)S(1)}, bf16[256,1152]{1,0:T(8,128)(2,1)}, u32[]{:S(2)}) copy-start(bf16[256,1152]{1,0:T(8,128)(2,1)} %param.9) | copy-start | bytes 1769476
  3.2 11.5 %copy-start.3 = (f32[1152]{0:T(1024)S(1)}, f32[1152]{0:T(1024)}, u32[]{:S(2)}) copy-start(f32[1152]{0:T(1024)} %param.12) | copy-start | bytes 13828
  3.2 41.4 %all-to-all-start = ((bf16[32,2,16,1152]{3,2,1,0:T(8,128)(2,1)}), bf16[32,2,16,1152]{3,2,1,0:T(8,128)(2,1)}, u32[]{:S(2)}, u32[]{:S(2)}) async-start(bf16[32,2,16,1152]{3,2,1,0:T(8,128)(2,1)} %broadcast_in_dim.6), calls=%async_computation | async-start | bytes 4718592 | tf_op jit(solution)/shard_map/all_to_all | solution.py:306
  15.8 21.5 %collective-permute-start = (bf16[256,1152]{1,0:T(8,128)(2,1)}, bf16[256,1152]{1,0:T(8,128)(2,1)}, u32[]{:S(2)}, u32[]{:S(2)}) collective-permute-start(bf16[256,1152]{1,0:T(8,128)(2,1)} %fusion.7), channel_id=1, source_target_pairs={{0,32},{32,0},{1,33},{33,1},{2,34},{34,2},{3,35},{35,3},{4,36},{36... | collective-permute-start | bytes 1769480 | tf_op jit(solution)/shard_map/ppermute | solution.py:318
  66.9 41.4 %all-to-all-start.1 = ((bf16[32,2,40,512]{3,2,1,0:T(8,128)(2,1)}), bf16[32,2,40,512]{3,2,1,0:T(8,128)(2,1)}, u32[]{:S(2)}, u32[]{:S(2)}) async-start(bf16[32,2,40,512]{3,2,1,0:T(8,128)(2,1)} %get-tuple-element.30), calls=%async_computation.1 | async-start | bytes 5242880 | tf_op jit(solution)/shard_map/all_to_all | solution.py:324
  75.2 5.5 %collective-permute-start.3 = (bf16[256,1152]{1,0:T(8,128)(2,1)}, bf16[256,1152]{1,0:T(8,128)(2,1)}, u32[]{:S(2)}, u32[]{:S(2)}) collective-permute-start(bf16[256,1152]{1,0:T(8,128)(2,1)} %g_ref.1), channel_id=1, source_target_pairs={{0,32},{32,0},{1,33},{33,1},{2,34},{34,2},{3,35},{35,3},{4,36},{36... | collective-permute-start | bytes 1769480 | tf_op jit(solution)/shard_map/ppermute | solution.py:320
  75.3 5.4 %collective-permute-start.2 = (bf16[256,1152]{1,0:T(8,128)(2,1)}, bf16[256,1152]{1,0:T(8,128)(2,1)}, u32[]{:S(2)}, u32[]{:S(2)}) collective-permute-start(bf16[256,1152]{1,0:T(8,128)(2,1)} %get-tuple-element.26.dq_ref), channel_id=1, source_target_pairs={{0,32},{32,0},{1,33},{33,1},{2,34},{34,2},{3,35},{35,3},{4,36},{36... | collective-permute-start | bytes 1769480 | tf_op jit(solution)/shard_map/ppermute | solution.py:326
  75.8 4.9 %collective-permute-start.1 = (bf16[256,1152]{1,0:T(8,128)(2,1)}, bf16[256,1152]{1,0:T(8,128)(2,1)}, u32[]{:S(2)}, u32[]{:S(2)}) collective-permute-start(bf16[256,1152]{1,0:T(8,128)(2,1)} %get-tuple-element.28.o_ref), channel_id=1, source_target_pairs={{0,32},{32,0},{1,33},{33,1},{2,34},{34,2},{3,35},{35,3},{4,36},{36... | collective-permute-start | bytes 1769480 | tf_op jit(solution)/shard_map/ppermute | solution.py:327
  114.5 1.8 collective-permute-start.4
  116.3 0.7 copy-start.2
  120.4 9.3 %copy-start.4 = (f32[1152]{0:T(1024)S(1)}, f32[1152]{0:T(1024)}, u32[]{:S(2)}) copy-start(f32[1152]{0:T(1024)} %get-tuple-element.41) | copy-start | bytes 13828
  120.4 74.5 %all-to-all-start.2 = ((bf16[64,3,8,1152]{3,2,1,0:T(8,128)(2,1)}), bf16[64,3,8,1152]{3,2,1,0:T(8,128)(2,1)}, u32[]{:S(2)}, u32[]{:S(2)}) async-start(bf16[64,3,8,1152]{3,2,1,0:T(8,128)(2,1)} %fill_rest.1), calls=%async_computation.2 | async-start | bytes 7077888 | tf_op jit(solution)/shard_map/all_to_all | solution.py:338
  129.7 1.3 collective-permute-start.5
  130.9 45.8 %collective-permute-start.6 = (f32[1152]{0:T(1024)S(1)}, f32[1152]{0:T(1024)S(1)}, u32[]{:S(2)}, u32[]{:S(2)}) collective-permute-start(f32[1152]{0:T(1024)S(1)} %add.184), channel_id=1, source_target_pairs={{0,16},{8,24},{16,0},{24,8},{1,17},{9,25},{17,1},{25,9},{2,18},{10... | collective-permute-start | bytes 13832 | tf_op jit(solution)/shard_map/ppermute | solution.py:131
  133.1 43.7 %collective-permute-start.7 = (f32[1152]{0:T(1024)S(1)}, f32[1152]{0:T(1024)S(1)}, u32[]{:S(2)}, u32[]{:S(2)}) collective-permute-start(f32[1152]{0:T(1024)S(1)} %add.184), channel_id=1, source_target_pairs={{0,8},{8,16},{16,24},{24,0},{1,9},{9,17},{17,25},{25,1},{2,10},{10... | collective-permute-start | bytes 13832 | tf_op jit(solution)/shard_map/ppermute | solution.py:131
  133.1 43.7 %collective-permute-start.8 = (f32[1152]{0:T(1024)S(1)}, f32[1152]{0:T(1024)S(1)}, u32[]{:S(2)}, u32[]{:S(2)}) collective-permute-start(f32[1152]{0:T(1024)S(1)} %add.184), channel_id=1, source_target_pairs={{0,24},{8,0},{16,8},{24,16},{1,25},{9,1},{17,9},{25,17},{2,26},{10... | collective-permute-start | bytes 13832 | tf_op jit(solution)/shard_map/ppermute | solution.py:131
  176.8 4.9 %collective-permute-start.10 = (f32[1152]{0:T(1024)S(1)}, f32[1152]{0:T(1024)S(1)}, u32[]{:S(2)}, u32[]{:S(2)}) collective-permute-start(f32[1152]{0:T(1024)S(1)} %add_add_fusion.2), channel_id=1, source_target_pairs={{0,64},{64,4},{4,68},{68,0},{1,65},{65,5},{5,69},{69,1},{2,66},{66... | collective-permute-start | bytes 13832 | tf_op jit(solution)/shard_map/ppermute | solution.py:131
  178.1 3.7 %collective-permute-start.11 = (f32[1152]{0:T(1024)S(1)}, f32[1152]{0:T(1024)S(1)}, u32[]{:S(2)}, u32[]{:S(2)}) collective-permute-start(f32[1152]{0:T(1024)S(1)} %add_add_fusion.2), channel_id=1, source_target_pairs={{0,68},{64,0},{4,64},{68,4},{1,69},{65,1},{5,65},{69,5},{2,70},{66... | collective-permute-start | bytes 13832 | tf_op jit(solution)/shard_map/ppermute | solution.py:131
  180.1 5.2 %collective-permute-start.9 = (f32[1152]{0:T(1024)S(1)}, f32[1152]{0:T(1024)S(1)}, u32[]{:S(2)}, u32[]{:S(2)}) collective-permute-start(f32[1152]{0:T(1024)S(1)} %add_add_fusion.2), channel_id=1, source_target_pairs={{0,4},{64,68},{4,0},{68,64},{1,5},{65,69},{5,1},{69,65},{2,6},{66,... | collective-permute-start | bytes 13832 | tf_op jit(solution)/shard_map/ppermute | solution.py:131
  185.2 9.1 %collective-permute-start.12 = (f32[1152]{0:T(1024)S(1)}, f32[1152]{0:T(1024)S(1)}, u32[]{:S(2)}, u32[]{:S(2)}) collective-permute-start(f32[1152]{0:T(1024)S(1)} %add_add_fusion.1), channel_id=1, source_target_pairs={{0,2},{1,3},{2,0},{3,1},{4,6},{5,7},{6,4},{7,5},{8,10},{9,11},{10,... | collective-permute-start | bytes 13832 | tf_op jit(solution)/shard_map/ppermute | solution.py:131
  188.7 5.6 %collective-permute-start.13 = (f32[1152]{0:T(1024)S(1)}, f32[1152]{0:T(1024)S(1)}, u32[]{:S(2)}, u32[]{:S(2)}) collective-permute-start(f32[1152]{0:T(1024)S(1)} %add_add_fusion.1), channel_id=1, source_target_pairs={{0,1},{1,2},{2,3},{3,0},{4,5},{5,6},{6,7},{7,4},{8,9},{9,10},{10,1... | collective-permute-start | bytes 13832 | tf_op jit(solution)/shard_map/ppermute | solution.py:131
  188.7 5.6 %collective-permute-start.14 = (f32[1152]{0:T(1024)S(1)}, f32[1152]{0:T(1024)S(1)}, u32[]{:S(2)}, u32[]{:S(2)}) collective-permute-start(f32[1152]{0:T(1024)S(1)} %add_add_fusion.1), channel_id=1, source_target_pairs={{0,3},{1,0},{2,1},{3,2},{4,7},{5,4},{6,5},{7,6},{8,11},{9,8},{10,9... | collective-permute-start | bytes 13832 | tf_op jit(solution)/shard_map/ppermute | solution.py:131
where the time goes:
time: 204 us; the launch traced here: 203 us
  waiting for transfers between devices  75 us (37%)
  Pallas kernels  59.1 us (29%)
  starting transfers between devices  44 us (22%)
  matrix products  13.5 us (7%)
  other arithmetic  5.33 us (3%)
  local copies, waits for them, and re-layouts  5.01 us (2%)
    ppermute x9, waiting for transfers between devices, ring_send(): lax.ppermute(block, axis, [(at[i], at[(i + distance) % 4]) for i in range...  46.6 us
    pallas_call x1, Pallas kernels, attention(): pl.pallas_call(attention_kernel, grid_spec=grid_spec, out_shape=[jax.Shap...  22.2 us
    all_to_all x1, waiting for transfers between devices, on_device(): got = lax.all_to_all(pay, TILE_AXES, 0, 0, tiled=True)  21.1 us
    ppermute x9, starting transfers between devices, ring_send(): lax.ppermute(block, axis, [(at[i], at[(i + distance) % 4]) for i in range...  14.3 us
    dot_general x4, matrix products, dot(): lax.dot_general(a, b, (((ca,), (cb,)), ((), ())), preferred_element_type=...  13.5 us
    all_to_all x1, starting transfers between devices, on_device(): lax.all_to_all(jnp.broadcast_to(guide, (32, *guide.shape)), TILE_AXES, 0,...  11.3 us
    pallas_call x1, Pallas kernels, spread_weights(): pl.pallas_call(spread_weights_kernel, grid=(D // step,), in_specs=[pl.Blo...  10.8 us
    all_to_all x1, starting transfers between devices, on_device(): recv = lax.all_to_all(send, CHIP_AXES, 0, 0, tiled=True)  9.27 us
  transfers between devices with their start and end apart: 18, of which 8 were waited for; matrix products, arithmetic and copies ran while one was open for 9% of the time, Pallas kernels for 10%

commit v1 on v0

--- a/solution.py
+++ b/solution.py
@@ -15,7 +15,7 @@
 TILE_AXES = ("x", "yh", "z")
 CHIP_AXES = ("yl", "x", "yh", "z")
 SWAP = [(0, 1), (1, 0)]
-PER_STEP = 2
+PER_STEP = 4
 
 
 def dot(a, b, ca, cb):
@@ -46,7 +46,7 @@
 
 
 def spread_weights(w_key, w_value):
-    step = 128
+    step = 384
     return pl.pallas_call(
         spread_weights_kernel,
         grid=(D // step,),
@@ -122,13 +122,7 @@
     )(img, whole, w_kv, q, d)
 
 
-RING_AXES = ("x", ("yl", "yh"), "z")
 ROWS = 576
-
-
-def ring_send(block, axis, distance):
-    at = (0, 2, 1, 3) if isinstance(axis, tuple) else (0, 1, 2, 3)
-    return lax.ppermute(block, axis, [(at[i], at[(i + distance) % 4]) for i in range(4)])
 
 
 def eight_and_one(rows):
@@ -213,91 +207,123 @@
     )(core, got, whole)
 
 
-SLOTS = [(r, 256) for r in range(1, 8)] + [(r, 384) for r in range(1, 8)]
-SLOTS += [(r, 1024) for r in range(4)]
-
-
-def fill_rest_kernel(send_ref, mine_ref, got_ref, tok_ref, ninth_ref, out_ref, scr):
-    scr[...] = jnp.zeros_like(scr)
+SLOTS = [(row, lane) for lane in range(512, D, 128) for row in range(8)]
+
+
+def fill_rest_kernel(send_ref, mine_ref, got_ref, tok_ref, ninth_ref, gain_ref, out_ref, scr):
+    scr[:, :, 384:512] = jnp.zeros((64, 8, 128), F32)
     total = mine_ref[...] + got_ref[...]
     high = total.astype(BF16)
     low = (total - high.astype(F32)).astype(BF16)
     want = eight_and_one(lax.broadcasted_iota(jnp.int32, (ROWS, ROWS), 0))
     order = (want == lax.broadcasted_iota(jnp.int32, (ROWS, ROWS), 1)).astype(BF16)
-    moved = dot(order, jnp.concatenate([high, low], axis=1), 1, 0)
-    scr[:, :, :256] = moved[:512].reshape(64, 8, 256)
-    scr[:, 0, 256:512] = moved[512:]
+    moved = [dot(order, x, 1, 0) for x in (high, low)]
     tok = tok_ref[...].reshape(32, 16, 256)
     for n in range(2):
-        scr[32 * n : 32 * n + 32, :, 512:768] = tok[:, :8]
-        scr[32 * n : 32 * n + 32, :, 768:1024] = tok[:, 8:]
+        scr[:, :, 80 * n : 80 * n + 80] = moved[n][:512].reshape(64, 8, 128)[:, :, :80]
+        for half in range(2):
+            lanes = slice(160 * half + 160, 160 * half + 320)
+            scr[32 * n : 32 * n + 32, :, lanes] = tok[:, 8 * half : 8 * half + 8, :160]
+    gain = gain_ref[...]
+    gain_high = gain.astype(BF16).astype(F32)
+    gains = jnp.concatenate([gain_high, gain - gain_high], axis=1)
     for b, (row, lane) in enumerate(SLOTS):
-        scr[:, row, lane : lane + 128] = ninth_ref[:, 128 * b : 128 * b + 128]
+        if b < 18:
+            block = ninth_ref[:, 128 * b : 128 * b + 128]
+        elif b < 20:
+            block = moved[b - 18][512:]
+        elif b < 38:
+            block = jnp.broadcast_to(gains[:, 128 * (b - 20) : 128 * (b - 20) + 128], (64, 128))
+        else:
+            block = jnp.zeros((64, 128), F32)
+        scr[:, row, lane : lane + 128] = block
     out_ref[:, 0] = scr[...].astype(BF16)
 
 
-def fill_rest(send, mine, got, tok, ninth):
+def fill_rest(send, mine, got, tok, ninth, gain):
     vmem = pl.BlockSpec(memory_space=pltpu.VMEM)
     return pl.pallas_call(
         fill_rest_kernel,
         grid=(1,),
-        in_specs=[pl.BlockSpec(memory_space=pl.ANY)] + [vmem] * 4,
+        in_specs=[pl.BlockSpec(memory_space=pl.ANY)] + [vmem] * 5,
         out_specs=pl.BlockSpec((64, 1, 8, D), lambda i: (0, 2, 0, 0)),
         out_shape=jax.ShapeDtypeStruct((64, 3, 8, D), BF16),
         scratch_shapes=[pltpu.VMEM((64, 8, D), F32)],
         input_output_aliases={0: 0},
         name="fill_rest",
-    )(send, mine, got, tok, ninth)
-
-
-def finish_kernel(yl_ref, recv_ref, wk_ref, wv_ref, gw_ref, gg_ref, scr):
+    )(send, mine, got, tok, ninth, gain)
+
+
+def finish_kernel(yl_ref, recv_ref, wk_hbm, wv_hbm, gw_ref, gg_ref, gain_ref, scr, wk, wv, sems):
+    copies = [
+        pltpu.make_async_copy(wk_hbm, wk, sems.at[0]),
+        pltpu.make_async_copy(wv_hbm, wv, sems.at[1]),
+    ]
+    for copy in copies:
+        copy.start()
+
     def add(j, sums):
         return tuple(s + recv_ref[j, n].astype(F32) for n, s in enumerate(sums))
 
     sums = lax.fori_loop(0, 64, add, tuple(jnp.zeros((8, D), F32) for _ in range(3)))
     gw_ref[0, :8] = sums[0]
     gw_ref[3, :8] = sums[1]
-    for b, (row, lane) in enumerate(SLOTS):
+
+    def slot(b):
+        row, lane = SLOTS[b]
+        return sums[2][row : row + 1, lane : lane + 128]
+
+    for b in range(18):
         at = 128 * (b % 9)
-        gw_ref[3 * (b // 9), 8:9, at : at + 128] = sums[2][row : row + 1, lane : lane + 128]
+        gw_ref[3 * (b // 9), 8:9, at : at + 128] = slot(b)
+    for b in range(9):
+        gain_ref[:, 128 * b : 128 * b + 128] = slot(20 + b) + slot(29 + b)
     base = yl_ref[0] * 32
+    nines = [SLOTS[18], SLOTS[19]]
     for t in range(32):
         cols = slice(36 * t, 36 * t + 36)
-        x = recv_ref[t, 2, :, :512].astype(F32) + recv_ref[32 + t, 2, :, :512].astype(F32)
-        eight = x[:, :128] + x[:, 128:256]
-        one = x[:1, 256:384] + x[:1, 384:512]
+        x = recv_ref[t, 2, :, :256].astype(F32) + recv_ref[32 + t, 2, :, :256].astype(F32)
+        eight = x[:, :80] + x[:, 80:160]
+        one = jnp.zeros((1, 128), F32)
+        for row, lane in nines:
+            for j in (t, 32 + t):
+                one = one + recv_ref[j, 2, :, lane : lane + 128].astype(F32)[row : row + 1]
         for n in range(2):
             gw_ref[1 + n, :8, cols] = eight[:, 40 * n : 40 * n + 36]
             gw_ref[1 + n, 8:9, cols] = one[:, 40 * n : 40 * n + 36]
-        near = recv_ref[base + t, 2, :, 512:1024].astype(F32)
+        near = recv_ref[base + t, 2, :, 128:512].astype(F32)
         for half in range(2):
             for m in range(2):
                 for n in range(2):
-                    lane = 256 * half + 80 * m + 40 * n
+                    lane = 32 + 160 * half + 80 * m + 40 * n
                     row = 16 * m + 8 * half
                     scr[n, row : row + 8, cols] = near[:, lane : lane + 36]
-    grad = dot(scr[0].astype(BF16), wk_ref[...], 1, 1) + dot(scr[1].astype(BF16), wv_ref[...], 1, 1)
+    for copy in copies:
+        copy.wait()
+    grad = dot(scr[0].astype(BF16), wk[...], 1, 1) + dot(scr[1].astype(BF16), wv[...], 1, 1)
     gg_ref[...] = grad.astype(BF16)
 
 
 def finish(yl, recv, w_key, w_value):
     vmem = pl.BlockSpec(memory_space=pltpu.VMEM)
+    hbm = pl.BlockSpec(memory_space=pl.ANY)
     return pl.pallas_call(
         finish_kernel,
-        in_specs=[pl.BlockSpec(memory_space=pltpu.SMEM), vmem, vmem, vmem],
-        out_specs=[vmem] * 2,
-        out_shape=[jax.ShapeDtypeStruct((4, 9, D), F32), jax.ShapeDtypeStruct((32, D), BF16)],
-        scratch_shapes=[pltpu.VMEM((2, 32, D), F32)],
+        in_specs=[pl.BlockSpec(memory_space=pltpu.SMEM), vmem, hbm, hbm],
+        out_specs=[vmem] * 3,
+        out_shape=[
+            jax.ShapeDtypeStruct((4, 9, D), F32),
+            jax.ShapeDtypeStruct((32, D), BF16),
+            jax.ShapeDtypeStruct((1, D), F32),
+        ],
+        scratch_shapes=[
+            pltpu.VMEM((2, 32, D), F32),
+            pltpu.VMEM((D, D), BF16),
+            pltpu.VMEM((D, D), BF16),
+            pltpu.SemaphoreType.DMA((2,)),
+        ],
         name="finish",
     )(yl, recv, w_key, w_value)
-
-
-def all_sum(x):
-    x = x + lax.ppermute(x, "c", SWAP)
-    for axes in RING_AXES:
-        one, two, three = (ring_send(x, axes, n) for n in (1, 2, 3))
-        x = (x + two) + (one + three)
-    return x
 
 
 def on_device(tiles, tile_image, guide, gain, w_query, w_key, w_value, w_out, grad_out):
@@ -327,18 +353,17 @@
     out_got = lax.ppermute(outv, "c", SWAP)
     send, ninth = weight_parts(want, hid_rows, outv, out_got, dq, dq_got, grad_out, grad_got)
     dh = dot(dq, w_query, 1, 1)
-    gain_part = jnp.sum(dh * normed, axis=0)
+    gain_part = jnp.sum(dh * normed, axis=0, keepdims=True)
+    gain_part = gain_part + lax.ppermute(gain_part, "c", SWAP)
     dn = dh * gain
     grad_tiles = (rstd * (dn - normed * jnp.mean(dn * normed, axis=-1, keepdims=True))).astype(BF16)
 
     got, ninth, gain_part = lax.optimization_barrier((got, ninth, gain_part))
     mine, theirs, tok = image_sums(core[None], got, whole)
-    send = fill_rest(send, mine, lax.ppermute(theirs, "c", SWAP), tok, ninth)
-    send, gain_part = lax.optimization_barrier((send, gain_part))
+    send = fill_rest(send, mine, lax.ppermute(theirs, "c", SWAP), tok, ninth, gain_part)
     recv = lax.all_to_all(send, CHIP_AXES, 0, 0, tiled=True)
-    grad_gain = all_sum(gain_part)
-    grad_weights, grad_guide = finish(yl[None], recv, w_key, w_value)
-    return (grad_tiles, grad_guide.reshape(guide.shape), grad_weights, grad_gain)
+    grad_weights, grad_guide, grad_gain = finish(yl[None], recv, w_key, w_value)
+    return (grad_tiles, grad_guide.reshape(guide.shape), grad_weights, grad_gain.reshape(D))
 
 
 def solution(mesh):

time: 204 us -> 187 us (0.917)
  starting transfers between devices: 44 us -> 29.9 us
  waiting for transfers between devices: 75 us -> 72.2 us
    ppermute x11 -> x2, waiting for transfers between devices: 49.6 us -> 1.79 us  [the longest x1 1.79 us: on_device(): lax.ppermute(theirs, 'c', SWAP)]
    all_to_all x1, waiting for transfers between devices: 0.01 us -> 43.8 us  [on_device(): recv = lax.all_to_all(send, CHIP_AXES, 0, 0, tiled=True)]
    ppermute x11 -> x2, starting transfers between devices: 14.4 us -> 0.42 us  [the longest x1 0.42 us: on_device(): gain_part = gain_part + lax.ppermute(gain_part, 'c', SWAP)]
  transfers between devices with their start and end apart: 18 -> 9, of which waited for: 8 -> 4; matrix products, arithmetic and copies ran while one was open for 9% -> 10% of each run, Pallas kernels for 10% -> 10%
where the time goes in v1:
time: 187 us; the launch traced here: 185 us
  waiting for transfers between devices  72.2 us (39%)
  Pallas kernels  57.3 us (31%)
  starting transfers between devices  29.9 us (16%)
  matrix products  12.9 us (7%)
  other arithmetic  6.62 us (4%)
  local copies, waits for them, and re-layouts  5.02 us (3%)
    all_to_all x1, waiting for transfers between devices, on_device(): recv = lax.all_to_all(send, CHIP_AXES, 0, 0, tiled=True)  43.8 us
    pallas_call x1, Pallas kernels, attention(): pl.pallas_call(attention_kernel, grid_spec=grid_spec, out_shape=[jax.Shap...  21 us
    all_to_all x1, waiting for transfers between devices, on_device(): got = lax.all_to_all(pay, TILE_AXES, 0, 0, tiled=True)  20.8 us
    dot_general x4, matrix products, dot(): lax.dot_general(a, b, (((ca,), (cb,)), ((), ())), preferred_element_type=...  12.9 us
    all_to_all x1, starting transfers between devices, on_device(): lax.all_to_all(jnp.broadcast_to(guide, (32, *guide.shape)), TILE_AXES, 0,...  11.3 us
    all_to_all x1, starting transfers between devices, on_device(): recv = lax.all_to_all(send, CHIP_AXES, 0, 0, tiled=True)  9.19 us
    pallas_call x1, Pallas kernels, spread_weights(): pl.pallas_call(spread_weights_kernel, grid=(D // step,), in_specs=[pl.Blo...  9.19 us
    all_to_all x1, starting transfers between devices, on_device(): got = lax.all_to_all(pay, TILE_AXES, 0, 0, tiled=True)  8.31 us
  transfers between devices with their start and end apart: 9, of which 4 were waited for; matrix products, arithmetic and copies ran while one was open for 10% of the time, Pallas kernels for 10%

profile of v1, /device:TPU:2, one launch (start us, length us, event | category | flops | bytes accessed | tf_op | source)
XLA Modules:
  0.0 185.3 jit_solution(5272922066759484681)
XLA Ops:
  0.6 0.0 copy-start
  0.6 2.6 %broadcast_in_dim.8 = bf16[32,2,16,1152]{3,2,1,0:T(8,128)(2,1)} broadcast(bf16[2,16,1152]{2,1,0:T(8,128)(2,1)} %param.11), dimensions={1,2,3} | broadcast | bytes 2433024 | tf_op jit(solution)/shard_map/broadcast_in_dim | solution.py:333
  3.2 0.0 copy-start.1
  3.2 0.0 copy-start.3
  3.2 11.3 %all-to-all-start = ((bf16[32,2,16,1152]{3,2,1,0:T(8,128)(2,1)}), bf16[32,2,16,1152]{3,2,1,0:T(8,128)(2,1)}, u32[]{:S(2)}, u32[]{:S(2)}) async-start(bf16[32,2,16,1152]{3,2,1,0:T(8,128)(2,1)} %broadcast_in_dim.8), calls=%async_computation | async-start | bytes 4718592 | tf_op jit(solution)/shard_map/all_to_all | solution.py:332
  14.5 0.0 copy-done.1
  14.5 0.2 fusion.13
  14.7 0.0 copy-done.3
  14.8 1.0 fusion.7
  15.8 0.0 collective-permute-start
  15.8 0.0 copy-done
  15.8 2.9 %convolution_convert_fusion.1.q_ref = bf16[256,1152]{1,0:T(8,128)(2,1)} fusion(bf16[256,1152]{1,0:T(8,128)(2,1)} %fusion.7, bf16[1152,1152]{1,0:T(8,128)(2,1)S(1)} %copy-done), kind=kOutput, calls=%fused_computation.3 | convolution fusion | flops 679772160 | bytes 3833856 | tf_op jit(solution)/shard_map/dot_general | solution.py:22
  19.3 3.8 %convolution_convert_fusion.d_ref = bf16[256,1152]{1,0:T(8,128)(2,1)} fusion(bf16[256,1152]{1,0:T(8,128)(2,1)} %g_ref.1, bf16[1152,1152]{1,0:T(8,128)(2,1)} %param.16), kind=kOutput, calls=%fused_computation.2 | convolution fusion | flops 679772160 | bytes 3833856 | tf_op jit(solution)/shard_map/dot_general | solution.py:22
  23.1 3.4 %spread_heads.1 = (bf16[256,2048]{1,0:T(8,128)(2,1)}, bf16[256,2048]{1,0:T(8,128)(2,1)}) custom-call(bf16[256,1152]{1,0:T(8,128)(2,1)} %convolution_convert_fusion.1.q_ref, bf16[256,1152]{1,0:T(8,128)(2,1)} %convolution_convert_fusion.d_ref), custom_call_target="tpu_custom_call" | custom-call | tf_op jit(solution)/shard_map/spread_heads/pallas_call | solution.py:34
  26.6 9.2 %spread_weights.1.w_ref = bf16[1152,4096]{1,0:T(8,128)(2,1)} custom-call(bf16[1152,1152]{1,0:T(8,128)(2,1)} %wk_hbm.1, bf16[1152,1152]{1,0:T(8,128)(2,1)} %wv_hbm.1), custom_call_target="tpu_custom_call" | custom-call | tf_op jit(solution)/shard_map/spread_weights/pallas_call | solution.py:50
  35.8 0.0 collective-permute-done
  35.8 3.0 %fusion.6.hid_ref = bf16[576,512]{1,0:T(8,128)(2,1)} fusion(s32[576]{0:T(1024)S(1)} %fusion.44, bf16[256,1152]{1,0:T(8,128)(2,1)} %collective-permute-done, bf16[256,1152]{1,0:T(8,128)(2,1)} %fusion.7), kind=kOutput, calls=%fused_computation.11 | convolution fusion | flops 682795008 | bytes 1771776 | tf_op jit(solution)/shard_map/dot_general | solution.py:22
  38.8 5.8 %all-to-all-done.g_ref = bf16[32,2,16,1152]{3,2,1,0:T(8,128)(2,1)} async-done(((bf16[32,2,16,1152]{3,2,1,0:T(8,128)(2,1)}), bf16[32,2,16,1152]{3,2,1,0:T(8,128)(2,1)}, u32[]{:S(2)}, u32[]{:S(2)}) %all-to-all-start) | async-done | bytes 2359328 | tf_op jit(solution)/shard_map/all_to_all | solution.py:332
  44.6 21.0 %attention.1 = (bf16[32,2,40,512]{3,2,1,0:T(8,128)(2,1)}, bf16[256,1152]{1,0:T(8,128)(2,1)}, bf16[256,1152]{1,0:T(8,128)(2,1)}) custom-call(s32[1]{0:T(128)S(6)} %copy.16.img_ref, bf16[32,2,16,1152]{3,2,1,0:T(8,128)(2,1)} %all-to-all-done.g_ref, bf16[1152,4096]{1,0:T(8,128)(2,1)} %spread_weights.1.w_ref, bf16[256,2048]{1,0:T(8,128)(2,1)} %get-tuple-element.23.q_ref, ...), custom_call_target="tpu_custom_call" | custom-call | tf_op jit(solution)/shard_map/attention/pallas_call | solution.py:113
  65.6 8.3 %all-to-all-start.1 = ((bf16[32,2,40,512]{3,2,1,0:T(8,128)(2,1)}), bf16[32,2,40,512]{3,2,1,0:T(8,128)(2,1)}, u32[]{:S(2)}, u32[]{:S(2)}) async-start(bf16[32,2,40,512]{3,2,1,0:T(8,128)(2,1)} %get-tuple-element.29), calls=%async_computation.1 | async-start | bytes 5242880 | tf_op jit(solution)/shard_map/all_to_all | solution.py:350
  73.9 0.1 collective-permute-start.3
  74.0 0.5 collective-permute-start.2
  74.5 0.1 collective-permute-start.1
  74.6 3.1 %fusion.12 = (f32[1152]{0:T(1024)S(1)}, f32[256]{0:T(256)S(1)}, f32[256,1152]{1,0:T(8,128)}) fusion(bf16[256,1152]{1,0:T(8,128)(2,1)S(1)} %copy-done.1, f32[256]{0:T(256)S(1)} %add_rsqrt_fusion, f32[1152]{0:T(1024)S(1)} %copy-done.3, bf16[256,1152]{1,0:T(8,128)(2,1)} %get-tuple-element.25.dq_ref, bf16[1152,1152]{1,0:T(8,128)(2,1)S(1)} %copy-done), kind=kOutput, calls=%fused_computation.17 | convolution fusion | flops 681540224 | bytes 5024768 | tf_op jit(solution)/shard_map/dot_general | solution.py:22
  77.7 0.4 collective-permute-start.4
  78.1 1.1 fusion.28.want_ref
  79.2 0.0 collective-permute-done.4
  79.2 0.6 reshape_add_fusion.gain_ref
  79.8 0.0 collective-permute-done.3.g2_ref
  79.8 0.0 collective-permute-done.2.dq2_ref
  79.8 0.0 collective-permute-done.1.o2_ref
  79.8 6.4 %weight_parts.1 = (bf16[64,3,8,1152]{3,2,1,0:T(8,128)(2,1)}, f32[64,2304]{1,0:T(8,128)}) custom-call(s32[576,1]{1,0:T(8,128)} %fusion.28.want_ref, bf16[576,512]{1,0:T(8,128)(2,1)} %fusion.6.hid_ref, bf16[256,1152]{1,0:T(8,128)(2,1)} %get-tuple-element.27.o_ref, bf16[256,1152]{1,0:T(8,128)(2,1)} %collective-permute-done.1.o2_ref, ...), custom_call_target="tpu_custom_call" | custom-call | tf_op jit(solution)/shard_map/weight_parts/pallas_call | solution.py:156
  86.2 20.8 %all-to-all-done.1.got_ref = bf16[32,2,40,512]{3,2,1,0:T(8,128)(2,1)} async-done(((bf16[32,2,40,512]{3,2,1,0:T(8,128)(2,1)}), bf16[32,2,40,512]{3,2,1,0:T(8,128)(2,1)}, u32[]{:S(2)}, u32[]{:S(2)}) %all-to-all-start.1) | async-done | bytes 2621472 | tf_op jit(solution)/shard_map/all_to_all | solution.py:350
  107.0 6.3 %image_sums.1 = (f32[576,128]{1,0:T(8,128)}, f32[576,128]{1,0:T(8,128)}, f32[512,256]{1,0:T(8,128)}) custom-call(s32[1]{0:T(128)} %bitcast.1.core_ref, bf16[32,2,40,512]{3,2,1,0:T(8,128)(2,1)} %all-to-all-done.1.got_ref, bf16[32,2,16,1152]{3,2,1,0:T(8,128)(2,1)} %all-to-all-done.g_ref), custom_call_target="tpu_custom_call" | custom-call | tf_op jit(solution)/shard_map/image_sums/pallas_call | solution.py:196
  113.2 0.0 collective-permute-start.5
  113.2 1.8 collective-permute-done.5.got_ref
  115.0 0.0 copy-start.2
  115.0 0.7 copy-done.2
  115.7 3.9 %fill_rest.1 = bf16[64,3,8,1152]{3,2,1,0:T(8,128)(2,1)} custom-call(bf16[64,3,8,1152]{3,2,1,0:T(8,128)(2,1)} %get-tuple-element.28.send_ref, f32[576,128]{1,0:T(8,128)} %get-tuple-element.32.mine_ref, f32[576,128]{1,0:T(8,128)} %copy-done.2, f32[512,256]{1,0:T(8,128)} %get-tuple-element.34.tok_ref, ...), custom_call_target="tpu_custom_call", output_to_operand_aliasing={{}: (0, {})} | custom-call | tf_op jit(solution)/shard_map/fill_rest/pallas_call | solution.py:245
  119.6 9.2 %all-to-all-start.2 = ((bf16[64,3,8,1152]{3,2,1,0:T(8,128)(2,1)}), bf16[64,3,8,1152]{3,2,1,0:T(8,128)(2,1)}, u32[]{:S(2)}, u32[]{:S(2)}) async-start(bf16[64,3,8,1152]{3,2,1,0:T(8,128)(2,1)} %fill_rest.1), calls=%async_computation.2 | async-start | bytes 7077888 | tf_op jit(solution)/shard_map/all_to_all | solution.py:364
  128.9 2.4 %fusion.11 = bf16[256,1152]{1,0:T(8,128)(2,1)} fusion(bf16[256,1152]{1,0:T(8,128)(2,1)S(1)} %copy-done.1, f32[256,1152]{1,0:T(8,128)} %get-tuple-element.46, f32[256]{0:T(256)S(1)} %broadcast_multiply_fusion, f32[1152]{0:T(1024)S(1)} %copy-done.3, f32[256]{0:T(256)S(1)} %add_rsqrt_fusion), kind=kLoop, calls=%fused_computation.16 | loop fusion | flops 2064384 | bytes 2365952 | tf_op jit(solution)/shard_map/convert_element_type | solution.py:359
  131.2 43.8 %all-to-all-done.2.recv_ref = bf16[64,3,8,1152]{3,2,1,0:T(8,128)(2,1)} async-done(((bf16[64,3,8,1152]{3,2,1,0:T(8,128)(2,1)}), bf16[64,3,8,1152]{3,2,1,0:T(8,128)(2,1)}, u32[]{:S(2)}, u32[]{:S(2)}) %all-to-all-start.2) | async-done | bytes 3538976 | tf_op jit(solution)/shard_map/all_to_all | solution.py:364
  175.0 7.2 %finish.1 = (f32[4,9,1152]{2,1,0:T(8,128)}, bf16[32,1152]{1,0:T(8,128)(2,1)}, f32[1,1152]{1,0:T(1,128)}) custom-call(s32[1]{0:T(128)} %bitcast.yl_ref, bf16[64,3,8,1152]{3,2,1,0:T(8,128)(2,1)} %all-to-all-done.2.recv_ref, bf16[1152,1152]{1,0:T(8,128)(2,1)} %wk_hbm.1, bf16[1152,1152]{1,0:T(8,128)(2,1)} %wv_hbm.1), custom_call_target="tpu_custom_call" | custom-call | tf_op jit(solution)/shard_map/finish/pallas_call | solution.py:310
  182.3 1.7 copy.14
  184.0 1.3 reduce
  (4 shorter events, 0.0 us)
Async XLA Ops:
  0.6 15.1 %copy-start = (bf16[1152,1152]{1,0:T(8,128)(2,1)S(1)}, bf16[1152,1152]{1,0:T(8,128)(2,1)}, u32[]{:S(2)}) copy-start(bf16[1152,1152]{1,0:T(8,128)(2,1)} %param.13) | copy-start | bytes 7962628
  3.2 11.3 %copy-start.1 = (bf16[256,1152]{1,0:T(8,128)(2,1)S(1)}, bf16[256,1152]{1,0:T(8,128)(2,1)}, u32[]{:S(2)}) copy-start(bf16[256,1152]{1,0:T(8,128)(2,1)} %param.9) | copy-start | bytes 1769476
  3.2 11.5 %copy-start.3 = (f32[1152]{0:T(1024)S(1)}, f32[1152]{0:T(1024)}, u32[]{:S(2)}) copy-start(f32[1152]{0:T(1024)} %param.12) | copy-start | bytes 13828
  3.2 41.4 %all-to-all-start = ((bf16[32,2,16,1152]{3,2,1,0:T(8,128)(2,1)}), bf16[32,2,16,1152]{3,2,1,0:T(8,128)(2,1)}, u32[]{:S(2)}, u32[]{:S(2)}) async-start(bf16[32,2,16,1152]{3,2,1,0:T(8,128)(2,1)} %broadcast_in_dim.8), calls=%async_computation | async-start | bytes 4718592 | tf_op jit(solution)/shard_map/all_to_all | solution.py:332
  15.8 20.0 %collective-permute-start = (bf16[256,1152]{1,0:T(8,128)(2,1)}, bf16[256,1152]{1,0:T(8,128)(2,1)}, u32[]{:S(2)}, u32[]{:S(2)}) collective-permute-start(bf16[256,1152]{1,0:T(8,128)(2,1)} %fusion.7), channel_id=1, source_target_pairs={{0,32},{32,0},{1,33},{33,1},{2,34},{34,2},{3,35},{35,3},{4,36},{36... | collective-permute-start | bytes 1769480 | tf_op jit(solution)/shard_map/ppermute | solution.py:344
  65.6 41.4 %all-to-all-start.1 = ((bf16[32,2,40,512]{3,2,1,0:T(8,128)(2,1)}), bf16[32,2,40,512]{3,2,1,0:T(8,128)(2,1)}, u32[]{:S(2)}, u32[]{:S(2)}) async-start(bf16[32,2,40,512]{3,2,1,0:T(8,128)(2,1)} %get-tuple-element.29), calls=%async_computation.1 | async-start | bytes 5242880 | tf_op jit(solution)/shard_map/all_to_all | solution.py:350
  73.9 5.9 %collective-permute-start.3 = (bf16[256,1152]{1,0:T(8,128)(2,1)}, bf16[256,1152]{1,0:T(8,128)(2,1)}, u32[]{:S(2)}, u32[]{:S(2)}) collective-permute-start(bf16[256,1152]{1,0:T(8,128)(2,1)} %g_ref.1), channel_id=1, source_target_pairs={{0,32},{32,0},{1,33},{33,1},{2,34},{34,2},{3,35},{35,3},{4,36},{36... | collective-permute-start | bytes 1769480 | tf_op jit(solution)/shard_map/ppermute | solution.py:346
  74.0 5.8 %collective-permute-start.2 = (bf16[256,1152]{1,0:T(8,128)(2,1)}, bf16[256,1152]{1,0:T(8,128)(2,1)}, u32[]{:S(2)}, u32[]{:S(2)}) collective-permute-start(bf16[256,1152]{1,0:T(8,128)(2,1)} %get-tuple-element.25.dq_ref), channel_id=1, source_target_pairs={{0,32},{32,0},{1,33},{33,1},{2,34},{34,2},{3,35},{35,3},{4,36},{36... | collective-permute-start | bytes 1769480 | tf_op jit(solution)/shard_map/ppermute | solution.py:352
  74.5 5.3 %collective-permute-start.1 = (bf16[256,1152]{1,0:T(8,128)(2,1)}, bf16[256,1152]{1,0:T(8,128)(2,1)}, u32[]{:S(2)}, u32[]{:S(2)}) collective-permute-start(bf16[256,1152]{1,0:T(8,128)(2,1)} %get-tuple-element.27.o_ref), channel_id=1, source_target_pairs={{0,32},{32,0},{1,33},{33,1},{2,34},{34,2},{3,35},{35,3},{4,36},{36... | collective-permute-start | bytes 1769480 | tf_op jit(solution)/shard_map/ppermute | solution.py:353
  77.7 1.5 collective-permute-start.4
  113.2 1.8 collective-permute-start.5
  115.0 0.7 copy-start.2
  119.6 55.4 %all-to-all-start.2 = ((bf16[64,3,8,1152]{3,2,1,0:T(8,128)(2,1)}), bf16[64,3,8,1152]{3,2,1,0:T(8,128)(2,1)}, u32[]{:S(2)}, u32[]{:S(2)}) async-start(bf16[64,3,8,1152]{3,2,1,0:T(8,128)(2,1)} %fill_rest.1), calls=%async_computation.2 | async-start | bytes 7077888 | tf_op jit(solution)/shard_map/all_to_all | solution.py:364

commit v2 on v1

--- a/solution.py
+++ b/solution.py
@@ -7,7 +7,6 @@
 
 HEADS = 16
 HD = 72
-HP = 128
 D = 1152
 G = 512
 F32 = jnp.float32
@@ -15,58 +14,35 @@
 TILE_AXES = ("x", "yh", "z")
 CHIP_AXES = ("yl", "x", "yh", "z")
 SWAP = [(0, 1), (1, 0)]
-PER_STEP = 4
 
 
 def dot(a, b, ca, cb):
     return lax.dot_general(a, b, (((ca,), (cb,)), ((), ())), preferred_element_type=F32)
 
 
-def spread_heads_kernel(q_ref, d_ref, qo_ref, do_ref):
-    for src, dst in ((q_ref, qo_ref), (d_ref, do_ref)):
-        dst[...] = jnp.zeros_like(dst)
-        for h in range(HEADS):
-            dst[:, h * HP : h * HP + HD] = src[:, h * HD : (h + 1) * HD]
-
-
-def spread_heads(q, d):
-    rows = q.shape[0]
-    return pl.pallas_call(
-        spread_heads_kernel,
-        out_shape=[jax.ShapeDtypeStruct((rows, HEADS * HP), BF16)] * 2,
-        name="spread_heads",
-    )(q, d)
-
-
-def spread_weights_kernel(k_ref, v_ref, o_ref):
-    o_ref[...] = jnp.zeros_like(o_ref)
+def attention_kernel(
+    img_ref, g_hbm, wk_hbm, wv_hbm, q_ref, d_ref, pay_hbm, o_ref, dq_ref,
+    guide, wk, wv, k_scr, v_scr, pay, sems, out_sems,
+):
+    loads = [
+        pltpu.make_async_copy(g_hbm.at[:, img_ref[0]], guide, sems.at[0]),
+        pltpu.make_async_copy(wk_hbm, wk, sems.at[1]),
+        pltpu.make_async_copy(wv_hbm, wv, sems.at[2]),
+    ]
+    for copy in loads:
+        copy.start()
+    loads[0].wait()
+    tokens = guide[...].reshape(G, D)
+    loads[1].wait()
+    k_scr[...] = dot(tokens, wk[...], 1, 0).astype(BF16)
+    loads[2].wait()
+    v_scr[...] = dot(tokens, wv[...], 1, 0).astype(BF16)
+    scale = HD ** (-0.5)
+    flag = jnp.full((4, G), img_ref[0], jnp.int32).astype(F32)
+    stores = []
     for h in range(HEADS):
-        o_ref[:, 2 * h * HP : 2 * h * HP + HD] = k_ref[:, h * HD : (h + 1) * HD]
-        o_ref[:, (2 * h + 1) * HP : (2 * h + 1) * HP + HD] = v_ref[:, h * HD : (h + 1) * HD]
-
-
-def spread_weights(w_key, w_value):
-    step = 384
-    return pl.pallas_call(
-        spread_weights_kernel,
-        grid=(D // step,),
-        in_specs=[pl.BlockSpec((step, D), lambda i: (i, 0))] * 2,
-        out_specs=pl.BlockSpec((step, 2 * HEADS * HP), lambda i: (i, 0)),
-        out_shape=jax.ShapeDtypeStruct((D, 2 * HEADS * HP), BF16),
-        name="spread_weights",
-    )(w_key, w_value)
-
-
-def attention_kernel(img_ref, g_ref, w_ref, q_ref, d_ref, pay_ref, o_ref, dq_ref, o_scr, dq_scr):
-    step = pl.program_id(0)
-    scale = HD ** (-0.5)
-    guide = g_ref[...].reshape(G, D)
-    kv_all = dot(guide, w_ref[...], 1, 0).astype(BF16)
-    flag = jnp.full((4, G), img_ref[0], jnp.int32).astype(F32)
-    for n in range(PER_STEP):
-        k = kv_all[:, 2 * n * HP : (2 * n + 1) * HP]
-        v = kv_all[:, (2 * n + 1) * HP : (2 * n + 2) * HP]
-        q, d = q_ref[:, n * HP : (n + 1) * HP], d_ref[:, n * HP : (n + 1) * HP]
+        cols = slice(h * HD, (h + 1) * HD)
+        q, d, k, v = q_ref[:, cols], d_ref[:, cols], k_scr[:, cols], v_scr[:, cols]
         scores = dot(q, k, 1, 1) * scale
         dprob = dot(d, v, 1, 1)
         top = jnp.max(scores, axis=-1, keepdims=True)
@@ -76,50 +52,44 @@
         weighted = probs * dprob
         delta = jnp.sum(weighted, axis=-1, keepdims=True)
         ds = ((weighted - probs * delta) * scale).astype(BF16)
-        o_scr[step * PER_STEP + n] = dot(pb, v, 1, 0).astype(BF16)
-        dq_scr[step * PER_STEP + n] = dot(ds, k, 1, 0).astype(BF16)
-        dk = dot(q, ds, 0, 0)
-        dv = dot(d, pb, 0, 0)
-        for i in range(2):
-            for j, part in enumerate((dk, dv)):
+        o_ref[:, cols] = dot(pb, v, 1, 0).astype(BF16)
+        dq_ref[:, cols] = dot(ds, k, 1, 0).astype(BF16)
+        for j, part in enumerate((dot(q, ds, 0, 0), dot(d, pb, 0, 0))):
+            for i in range(2):
                 rows = jnp.concatenate([part[36 * i : 36 * i + 36], flag], axis=0)
-                pay_ref[2 * n + i, j] = rows.astype(BF16)
-
-    @pl.when(step == HEADS // PER_STEP - 1)
-    def _():
-        for n in range(HEADS):
-            o_ref[:, n * HD : (n + 1) * HD] = o_scr[n][:, :HD]
-            dq_ref[:, n * HD : (n + 1) * HD] = dq_scr[n][:, :HD]
-
-
-def attention(img, whole, w_kv, q, d):
+                pay[2 * h + i, j] = rows.astype(BF16)
+        two = pl.ds(2 * h, 2)
+        stores.append(pltpu.make_async_copy(pay.at[two], pay_hbm.at[two], out_sems.at[h]))
+        stores[-1].start()
+    for copy in stores:
+        copy.wait()
+
+
+def attention(img, whole, w_key, w_value, q, d):
     t = q.shape[0]
-    grid_spec = pltpu.PrefetchScalarGridSpec(
-        num_scalar_prefetch=1,
-        grid=(HEADS // PER_STEP,),
-        in_specs=[
-            pl.BlockSpec((32, pl.Squeezed(), 16, D), lambda h, i: (0, i[0], 0, 0)),
-            pl.BlockSpec((D, 2 * PER_STEP * HP), lambda h, i: (0, h)),
-            pl.BlockSpec((t, PER_STEP * HP), lambda h, i: (0, h)),
-            pl.BlockSpec((t, PER_STEP * HP), lambda h, i: (0, h)),
-        ],
-        out_specs=[
-            pl.BlockSpec((2 * PER_STEP, 2, 40, G), lambda h, i: (h, 0, 0, 0)),
-            pl.BlockSpec((t, D), lambda h, i: (0, 0)),
-            pl.BlockSpec((t, D), lambda h, i: (0, 0)),
-        ],
-        scratch_shapes=[pltpu.VMEM((HEADS, t, HP), BF16), pltpu.VMEM((HEADS, t, HP), BF16)],
-    )
+    vmem = pl.BlockSpec(memory_space=pltpu.VMEM)
+    hbm = pl.BlockSpec(memory_space=pl.ANY)
     return pl.pallas_call(
         attention_kernel,
-        grid_spec=grid_spec,
+        in_specs=[pl.BlockSpec(memory_space=pltpu.SMEM), hbm, hbm, hbm, vmem, vmem],
+        out_specs=[hbm, vmem, vmem],
         out_shape=[
             jax.ShapeDtypeStruct((32, 2, 40, G), BF16),
             jax.ShapeDtypeStruct((t, D), BF16),
             jax.ShapeDtypeStruct((t, D), BF16),
         ],
+        scratch_shapes=[
+            pltpu.VMEM((32, 16, D), BF16),
+            pltpu.VMEM((D, D), BF16),
+            pltpu.VMEM((D, D), BF16),
+            pltpu.VMEM((G, D), BF16),
+            pltpu.VMEM((G, D), BF16),
+            pltpu.VMEM((32, 2, 40, G), BF16),
+            pltpu.SemaphoreType.DMA((3,)),
+            pltpu.SemaphoreType.DMA((HEADS,)),
+        ],
         name="attention",
-    )(img, whole, w_kv, q, d)
+    )(img, whole, w_key, w_value, q, d)
 
 
 ROWS = 576
@@ -266,8 +236,8 @@
         return tuple(s + recv_ref[j, n].astype(F32) for n, s in enumerate(sums))
 
     sums = lax.fori_loop(0, 64, add, tuple(jnp.zeros((8, D), F32) for _ in range(3)))
-    gw_ref[0, :8] = sums[0]
-    gw_ref[3, :8] = sums[1]
+    gw_ref[:8, 0] = sums[0]
+    gw_ref[:8, 3] = sums[1]
 
     def slot(b):
         row, lane = SLOTS[b]
@@ -275,9 +245,9 @@
 
     for b in range(18):
         at = 128 * (b % 9)
-        gw_ref[3 * (b // 9), 8:9, at : at + 128] = slot(b)
+        gw_ref[8:9, 3 * (b // 9), at : at + 128] = slot(b)
     for b in range(9):
-        gain_ref[:, 128 * b : 128 * b + 128] = slot(20 + b) + slot(29 + b)
+        gain_ref[b : b + 1] = slot(20 + b) + slot(29 + b)
     base = yl_ref[0] * 32
     nines = [SLOTS[18], SLOTS[19]]
     for t in range(32):
@@ -289,8 +259,8 @@
             for j in (t, 32 + t):
                 one = one + recv_ref[j, 2, :, lane : lane + 128].astype(F32)[row : row + 1]
         for n in range(2):
-            gw_ref[1 + n, :8, cols] = eight[:, 40 * n : 40 * n + 36]
-            gw_ref[1 + n, 8:9, cols] = one[:, 40 * n : 40 * n + 36]
+            gw_ref[:8, 1 + n, cols] = eight[:, 40 * n : 40 * n + 36]
+            gw_ref[8:9, 1 + n, cols] = one[:, 40 * n : 40 * n + 36]
         near = recv_ref[base + t, 2, :, 128:512].astype(F32)
         for half in range(2):
             for m in range(2):
@@ -312,9 +282,9 @@
         in_specs=[pl.BlockSpec(memory_space=pltpu.SMEM), vmem, hbm, hbm],
         out_specs=[vmem] * 3,
         out_shape=[
-            jax.ShapeDtypeStruct((4, 9, D), F32),
+            jax.ShapeDtypeStruct((9, 4, D), F32),
             jax.ShapeDtypeStruct((32, D), BF16),
-            jax.ShapeDtypeStruct((1, D), F32),
+            jax.ShapeDtypeStruct((9, 128), F32),
         ],
         scratch_shapes=[
             pltpu.VMEM((2, 32, D), F32),
@@ -338,15 +308,13 @@
     hidden = (normed * gain).astype(BF16)
     query = dot(hidden, w_query, 1, 0).astype(BF16)
     dout = dot(grad_out, w_out, 1, 1).astype(BF16)
-    q_wide, d_wide = spread_heads(query, dout)
-    w_kv = spread_weights(w_key, w_value)
     want = wanted_rows(core)
     hid_both = jnp.concatenate([hidden, lax.ppermute(hidden, "c", SWAP)], axis=0)
     hid_rows = dot(one_hot(want, D), hid_both, 1, 1).astype(BF16)
     grad_got = lax.ppermute(grad_out, "c", SWAP)
-    q_wide, hid_rows = lax.optimization_barrier((q_wide, hid_rows))
-
-    pay, outv, dq = attention(tile_image, whole, w_kv, q_wide, d_wide)
+    query, hid_rows = lax.optimization_barrier((query, hid_rows))
+
+    pay, outv, dq = attention(tile_image, whole, w_key, w_value, query, dout)
     got = lax.all_to_all(pay, TILE_AXES, 0, 0, tiled=True)
 
     dq_got = lax.ppermute(dq, "c", SWAP)
@@ -363,6 +331,7 @@
     send = fill_rest(send, mine, lax.ppermute(theirs, "c", SWAP), tok, ninth, gain_part)
     recv = lax.all_to_all(send, CHIP_AXES, 0, 0, tiled=True)
     grad_weights, grad_guide, grad_gain = finish(yl[None], recv, w_key, w_value)
+    grad_weights = grad_weights.transpose(1, 0, 2)
     return (grad_tiles, grad_guide.reshape(guide.shape), grad_weights, grad_gain.reshape(D))
 
 

time: 187 us -> 186 us (level)
  waiting for transfers between devices: 72.2 us -> 86.5 us
  Pallas kernels: 57.3 us -> 46.3 us
    all_to_all x1, waiting for transfers between devices: 5.79 us -> 20.1 us  [on_device(): lax.all_to_all(jnp.broadcast_to(guide, (32, *guide.shape)), TILE_AXES, 0,...]
    pallas_call x3 -> x1, Pallas kernels: 33.6 us -> 21.6 us  [attention(): pl.pallas_call(attention_kernel, in_specs=[pl.BlockSpec(memory_space=pltp...]
  transfers between devices with their start and end apart: 9 -> 9, of which waited for: 4 -> 4; matrix products, arithmetic and copies ran while one was open for 10% -> 9% of each run, Pallas kernels for 10% -> 3%
where the time goes in v2:
time: 186 us; the launch traced here: 184 us
  waiting for transfers between devices  86.5 us (47%)
  Pallas kernels  46.3 us (25%)
  starting transfers between devices  29.8 us (16%)
  matrix products  11.1 us (6%)
  other arithmetic  5.3 us (3%)
  local copies, waits for them, and re-layouts  3.37 us (2%)
    all_to_all x1, waiting for transfers between devices, on_device(): recv = lax.all_to_all(send, CHIP_AXES, 0, 0, tiled=True)  43.7 us
    pallas_call x1, Pallas kernels, attention(): pl.pallas_call(attention_kernel, in_specs=[pl.BlockSpec(memory_space=pltp...  21.6 us
    all_to_all x1, waiting for transfers between devices, on_device(): got = lax.all_to_all(pay, TILE_AXES, 0, 0, tiled=True)  20.8 us
    all_to_all x1, waiting for transfers between devices, on_device(): lax.all_to_all(jnp.broadcast_to(guide, (32, *guide.shape)), TILE_AXES, 0,...  20.1 us
    all_to_all x1, starting transfers between devices, on_device(): lax.all_to_all(jnp.broadcast_to(guide, (32, *guide.shape)), TILE_AXES, 0,...  11.3 us
    dot_general x4, matrix products, dot(): lax.dot_general(a, b, (((ca,), (cb,)), ((), ())), preferred_element_type=...  11.1 us
    all_to_all x1, starting transfers between devices, on_device(): recv = lax.all_to_all(send, CHIP_AXES, 0, 0, tiled=True)  9.08 us
    all_to_all x1, starting transfers between devices, on_device(): got = lax.all_to_all(pay, TILE_AXES, 0, 0, tiled=True)  8.36 us
  transfers between devices with their start and end apart: 9, of which 4 were waited for; matrix products, arithmetic and copies ran while one was open for 9% of the time, Pallas kernels for 3%

profile of v2, /device:TPU:2, one launch (start us, length us, event | category | flops | bytes accessed | tf_op | source)
XLA Modules:
  0.0 183.9 jit_solution(16135252788966488760)
XLA Ops:
  0.6 0.0 copy-start
  0.6 2.6 %broadcast_in_dim.8 = bf16[32,2,16,1152]{3,2,1,0:T(8,128)(2,1)} broadcast(bf16[2,16,1152]{2,1,0:T(8,128)(2,1)} %param.11), dimensions={1,2,3} | broadcast | bytes 2433024 | tf_op jit(solution)/shard_map/broadcast_in_dim | solution.py:303
  3.3 0.0 copy-start.1
  3.3 0.0 copy-start.4
  3.3 11.3 %all-to-all-start = ((bf16[32,2,16,1152]{3,2,1,0:T(8,128)(2,1)}), bf16[32,2,16,1152]{3,2,1,0:T(8,128)(2,1)}, u32[]{:S(2)}, u32[]{:S(2)}) async-start(bf16[32,2,16,1152]{3,2,1,0:T(8,128)(2,1)} %broadcast_in_dim.8), calls=%async_computation | async-start | bytes 4718592 | tf_op jit(solution)/shard_map/all_to_all | solution.py:302
  14.6 0.0 copy-done.1
  14.6 0.2 fusion.13
  14.8 0.0 copy-done.4
  14.8 1.0 fusion.7
  15.8 0.0 collective-permute-start
  16.5 0.0 copy-done
  16.5 0.0 copy-start.2
  16.5 0.0 copy-start.5
  16.5 3.0 %convolution_convert_fusion.1.q_ref = bf16[256,1152]{1,0:T(8,128)(2,1)} fusion(bf16[256,1152]{1,0:T(8,128)(2,1)} %fusion.7, bf16[1152,1152]{1,0:T(8,128)(2,1)S(1)} %copy-done), kind=kOutput, calls=%fused_computation.3 | convolution fusion | flops 679772160 | bytes 3833856 | tf_op jit(solution)/shard_map/dot_general | solution.py:20
  19.6 0.0 copy-done.2
  19.6 0.0 copy-done.5
  19.6 1.9 %convolution_convert_fusion.d_ref = bf16[256,1152]{1,0:T(8,128)(2,1)} fusion(bf16[256,1152]{1,0:T(8,128)(2,1)S(1)} %copy-done.2, bf16[1152,1152]{1,0:T(8,128)(2,1)S(1)} %copy-done.5), kind=kOutput, calls=%fused_computation.2 | convolution fusion | flops 679772160 | bytes 3833856 | tf_op jit(solution)/shard_map/dot_general | solution.py:20
  21.5 0.0 collective-permute-done
  21.5 3.1 %fusion.6.hid_ref = bf16[576,512]{1,0:T(8,128)(2,1)} fusion(s32[576]{0:T(1024)S(1)} %fusion.44, bf16[256,1152]{1,0:T(8,128)(2,1)} %collective-permute-done, bf16[256,1152]{1,0:T(8,128)(2,1)} %fusion.7), kind=kOutput, calls=%fused_computation.11 | convolution fusion | flops 682795008 | bytes 1771776 | tf_op jit(solution)/shard_map/dot_general | solution.py:20
  24.5 20.1 %all-to-all-done.g_hbm.g_ref = bf16[32,2,16,1152]{3,2,1,0:T(8,128)(2,1)} async-done(((bf16[32,2,16,1152]{3,2,1,0:T(8,128)(2,1)}), bf16[32,2,16,1152]{3,2,1,0:T(8,128)(2,1)}, u32[]{:S(2)}, u32[]{:S(2)}) %all-to-all-start) | async-done | bytes 2359328 | tf_op jit(solution)/shard_map/all_to_all | solution.py:302
  44.7 21.6 %attention.1 = (bf16[32,2,40,512]{3,2,1,0:T(8,128)(2,1)}, bf16[256,1152]{1,0:T(8,128)(2,1)}, bf16[256,1152]{1,0:T(8,128)(2,1)}) custom-call(s32[1]{0:T(128)S(6)} %copy.15.img_ref, bf16[32,2,16,1152]{3,2,1,0:T(8,128)(2,1)} %all-to-all-done.g_hbm.g_ref, bf16[1152,1152]{1,0:T(8,128)(2,1)} %wk_hbm.3, bf16[1152,1152]{1,0:T(8,128)(2,1)} %wv_hbm.3, ...), custom_call_target="tpu_custom_call" | custom-call | tf_op jit(solution)/shard_map/attention/pallas_call | solution.py:72
  66.2 8.4 %all-to-all-start.1 = ((bf16[32,2,40,512]{3,2,1,0:T(8,128)(2,1)}), bf16[32,2,40,512]{3,2,1,0:T(8,128)(2,1)}, u32[]{:S(2)}, u32[]{:S(2)}) async-start(bf16[32,2,40,512]{3,2,1,0:T(8,128)(2,1)} %get-tuple-element.25), calls=%async_computation.1 | async-start | bytes 5242880 | tf_op jit(solution)/shard_map/all_to_all | solution.py:318
  74.6 0.1 collective-permute-start.3
  74.7 0.5 collective-permute-start.1
  75.2 0.1 collective-permute-start.2
  75.3 3.1 %fusion.12 = (f32[1152]{0:T(1024)S(1)}, f32[256]{0:T(256)S(1)}, f32[256,1152]{1,0:T(8,128)}) fusion(bf16[256,1152]{1,0:T(8,128)(2,1)S(1)} %copy-done.1, f32[256]{0:T(256)S(1)} %add_rsqrt_fusion, f32[1152]{0:T(1024)S(1)} %copy-done.4, bf16[256,1152]{1,0:T(8,128)(2,1)} %get-tuple-element.21.dq_ref, bf16[1152,1152]{1,0:T(8,128)(2,1)S(1)} %copy-done), kind=kOutput, calls=%fused_computation.17 | convolution fusion | flops 681540224 | bytes 5024768 | tf_op jit(solution)/shard_map/dot_general | solution.py:20
  78.4 0.4 collective-permute-start.4
  78.8 1.1 fusion.28.want_ref
  79.9 0.0 collective-permute-done.4
  79.9 0.6 reshape_add_fusion.gain_ref
  80.5 0.0 collective-permute-done.3.g2_ref
  80.5 0.0 collective-permute-done.1.o2_ref
  80.5 0.0 collective-permute-done.2.dq2_ref
  80.5 6.3 %weight_parts.1 = (bf16[64,3,8,1152]{3,2,1,0:T(8,128)(2,1)}, f32[64,2304]{1,0:T(8,128)}) custom-call(s32[576,1]{1,0:T(8,128)} %fusion.28.want_ref, bf16[576,512]{1,0:T(8,128)(2,1)} %fusion.6.hid_ref, bf16[256,1152]{1,0:T(8,128)(2,1)} %get-tuple-element.23.o_ref, bf16[256,1152]{1,0:T(8,128)(2,1)} %collective-permute-done.1.o2_ref, ...), custom_call_target="tpu_custom_call" | custom-call | tf_op jit(solution)/shard_map/weight_parts/pallas_call | solution.py:126
  86.8 20.8 %all-to-all-done.1.got_ref = bf16[32,2,40,512]{3,2,1,0:T(8,128)(2,1)} async-done(((bf16[32,2,40,512]{3,2,1,0:T(8,128)(2,1)}), bf16[32,2,40,512]{3,2,1,0:T(8,128)(2,1)}, u32[]{:S(2)}, u32[]{:S(2)}) %all-to-all-start.1) | async-done | bytes 2621472 | tf_op jit(solution)/shard_map/all_to_all | solution.py:318
  107.7 6.3 %image_sums.1 = (f32[576,128]{1,0:T(8,128)}, f32[576,128]{1,0:T(8,128)}, f32[512,256]{1,0:T(8,128)}) custom-call(s32[1]{0:T(128)} %bitcast.1.core_ref, bf16[32,2,40,512]{3,2,1,0:T(8,128)(2,1)} %all-to-all-done.1.got_ref, bf16[32,2,16,1152]{3,2,1,0:T(8,128)(2,1)} %all-to-all-done.g_hbm.g_ref), custom_call_target="tpu_custom_call" | custom-call | tf_op jit(solution)/shard_map/image_sums/pallas_call | solution.py:166
  113.9 0.0 collective-permute-start.5
  113.9 1.8 collective-permute-done.5.got_ref
  115.7 0.0 copy-start.3
  115.7 0.7 copy-done.3
  116.4 4.0 %fill_rest.1 = bf16[64,3,8,1152]{3,2,1,0:T(8,128)(2,1)} custom-call(bf16[64,3,8,1152]{3,2,1,0:T(8,128)(2,1)} %get-tuple-element.24.send_ref, f32[576,128]{1,0:T(8,128)} %get-tuple-element.28.mine_ref, f32[576,128]{1,0:T(8,128)} %copy-done.3, f32[512,256]{1,0:T(8,128)} %get-tuple-element.30.tok_ref, ...), custom_call_target="tpu_custom_call", output_to_operand_aliasing={{}: (0, {})} | custom-call | tf_op jit(solution)/shard_map/fill_rest/pallas_call | solution.py:215
  120.4 9.1 %all-to-all-start.2 = ((bf16[64,3,8,1152]{3,2,1,0:T(8,128)(2,1)}), bf16[64,3,8,1152]{3,2,1,0:T(8,128)(2,1)}, u32[]{:S(2)}, u32[]{:S(2)}) async-start(bf16[64,3,8,1152]{3,2,1,0:T(8,128)(2,1)} %fill_rest.1), calls=%async_computation.2 | async-start | bytes 7077888 | tf_op jit(solution)/shard_map/all_to_all | solution.py:332
  129.5 2.4 %fusion.11 = bf16[256,1152]{1,0:T(8,128)(2,1)} fusion(bf16[256,1152]{1,0:T(8,128)(2,1)S(1)} %copy-done.1, f32[256,1152]{1,0:T(8,128)} %get-tuple-element.38, f32[256]{0:T(256)S(1)} %broadcast_multiply_fusion, f32[1152]{0:T(1024)S(1)} %copy-done.4, f32[256]{0:T(256)S(1)} %add_rsqrt_fusion), kind=kLoop, calls=%fused_computation.16 | loop fusion | flops 2064384 | bytes 2365952 | tf_op jit(solution)/shard_map/convert_element_type | solution.py:327
  131.9 43.7 %all-to-all-done.2.recv_ref = bf16[64,3,8,1152]{3,2,1,0:T(8,128)(2,1)} async-done(((bf16[64,3,8,1152]{3,2,1,0:T(8,128)(2,1)}), bf16[64,3,8,1152]{3,2,1,0:T(8,128)(2,1)}, u32[]{:S(2)}, u32[]{:S(2)}) %all-to-all-start.2) | async-done | bytes 3538976 | tf_op jit(solution)/shard_map/all_to_all | solution.py:332
  175.7 8.1 %finish.1 = (f32[9,4,1152]{2,1,0:T(4,128)}, bf16[32,1152]{1,0:T(8,128)(2,1)}, f32[9,128]{1,0:T(8,128)}) custom-call(s32[1]{0:T(128)} %bitcast.yl_ref, bf16[64,3,8,1152]{3,2,1,0:T(8,128)(2,1)} %all-to-all-done.2.recv_ref, bf16[1152,1152]{1,0:T(8,128)(2,1)} %wk_hbm.3, bf16[1152,1152]{1,0:T(8,128)(2,1)} %wv_hbm.3), custom_call_target="tpu_custom_call" | custom-call | tf_op jit(solution)/shard_map/finish/pallas_call | solution.py:280
  (4 shorter events, 0.0 us)
Async XLA Ops:
  0.6 15.9 %copy-start = (bf16[1152,1152]{1,0:T(8,128)(2,1)S(1)}, bf16[1152,1152]{1,0:T(8,128)(2,1)}, u32[]{:S(2)}) copy-start(bf16[1152,1152]{1,0:T(8,128)(2,1)} %param.13) | copy-start | bytes 7962628
  3.3 11.3 %copy-start.1 = (bf16[256,1152]{1,0:T(8,128)(2,1)S(1)}, bf16[256,1152]{1,0:T(8,128)(2,1)}, u32[]{:S(2)}) copy-start(bf16[256,1152]{1,0:T(8,128)(2,1)} %param.9) | copy-start | bytes 1769476
  3.3 11.5 %copy-start.4 = (f32[1152]{0:T(1024)S(1)}, f32[1152]{0:T(1024)}, u32[]{:S(2)}) copy-start(f32[1152]{0:T(1024)} %param.12) | copy-start | bytes 13828
  3.3 41.4 %all-to-all-start = ((bf16[32,2,16,1152]{3,2,1,0:T(8,128)(2,1)}), bf16[32,2,16,1152]{3,2,1,0:T(8,128)(2,1)}, u32[]{:S(2)}, u32[]{:S(2)}) async-start(bf16[32,2,16,1152]{3,2,1,0:T(8,128)(2,1)} %broadcast_in_dim.8), calls=%async_computation | async-start | bytes 4718592 | tf_op jit(solution)/shard_map/all_to_all | solution.py:302
  15.8 5.6 %collective-permute-start = (bf16[256,1152]{1,0:T(8,128)(2,1)}, bf16[256,1152]{1,0:T(8,128)(2,1)}, u32[]{:S(2)}, u32[]{:S(2)}) collective-permute-start(bf16[256,1152]{1,0:T(8,128)(2,1)} %fusion.7), channel_id=1, source_target_pairs={{0,32},{32,0},{1,33},{33,1},{2,34},{34,2},{3,35},{35,3},{4,36},{36... | collective-permute-start | bytes 1769480 | tf_op jit(solution)/shard_map/ppermute | solution.py:312
  16.5 3.1 %copy-start.2 = (bf16[256,1152]{1,0:T(8,128)(2,1)S(1)}, bf16[256,1152]{1,0:T(8,128)(2,1)}, u32[]{:S(2)}) copy-start(bf16[256,1152]{1,0:T(8,128)(2,1)} %g_ref.1) | copy-start | bytes 1769476
  16.5 3.1 %copy-start.5 = (bf16[1152,1152]{1,0:T(8,128)(2,1)S(1)}, bf16[1152,1152]{1,0:T(8,128)(2,1)}, u32[]{:S(2)}) copy-start(bf16[1152,1152]{1,0:T(8,128)(2,1)} %param.16) | copy-start | bytes 7962628
  66.2 41.5 %all-to-all-start.1 = ((bf16[32,2,40,512]{3,2,1,0:T(8,128)(2,1)}), bf16[32,2,40,512]{3,2,1,0:T(8,128)(2,1)}, u32[]{:S(2)}, u32[]{:S(2)}) async-start(bf16[32,2,40,512]{3,2,1,0:T(8,128)(2,1)} %get-tuple-element.25), calls=%async_computation.1 | async-start | bytes 5242880 | tf_op jit(solution)/shard_map/all_to_all | solution.py:318
  74.6 5.9 %collective-permute-start.3 = (bf16[256,1152]{1,0:T(8,128)(2,1)}, bf16[256,1152]{1,0:T(8,128)(2,1)}, u32[]{:S(2)}, u32[]{:S(2)}) collective-permute-start(bf16[256,1152]{1,0:T(8,128)(2,1)} %g_ref.1), channel_id=1, source_target_pairs={{0,32},{32,0},{1,33},{33,1},{2,34},{34,2},{3,35},{35,3},{4,36},{36... | collective-permute-start | bytes 1769480 | tf_op jit(solution)/shard_map/ppermute | solution.py:314
  74.7 5.8 %collective-permute-start.1 = (bf16[256,1152]{1,0:T(8,128)(2,1)}, bf16[256,1152]{1,0:T(8,128)(2,1)}, u32[]{:S(2)}, u32[]{:S(2)}) collective-permute-start(bf16[256,1152]{1,0:T(8,128)(2,1)} %get-tuple-element.23.o_ref), channel_id=1, source_target_pairs={{0,32},{32,0},{1,33},{33,1},{2,34},{34,2},{3,35},{35,3},{4,36},{36... | collective-permute-start | bytes 1769480 | tf_op jit(solution)/shard_map/ppermute | solution.py:321
  75.2 5.3 %collective-permute-start.2 = (bf16[256,1152]{1,0:T(8,128)(2,1)}, bf16[256,1152]{1,0:T(8,128)(2,1)}, u32[]{:S(2)}, u32[]{:S(2)}) collective-permute-start(bf16[256,1152]{1,0:T(8,128)(2,1)} %get-tuple-element.21.dq_ref), channel_id=1, source_target_pairs={{0,32},{32,0},{1,33},{33,1},{2,34},{34,2},{3,35},{35,3},{4,36},{36... | collective-permute-start | bytes 1769480 | tf_op jit(solution)/shard_map/ppermute | solution.py:320
  78.4 1.5 collective-permute-start.4
  113.9 1.8 collective-permute-start.5
  115.7 0.7 copy-start.3
  120.4 55.2 %all-to-all-start.2 = ((bf16[64,3,8,1152]{3,2,1,0:T(8,128)(2,1)}), bf16[64,3,8,1152]{3,2,1,0:T(8,128)(2,1)}, u32[]{:S(2)}, u32[]{:S(2)}) async-start(bf16[64,3,8,1152]{3,2,1,0:T(8,128)(2,1)} %fill_rest.1), calls=%async_computation.2 | async-start | bytes 7077888 | tf_op jit(solution)/shard_map/all_to_all | solution.py:332

commit v3 on v2

--- a/solution.py
+++ b/solution.py
@@ -20,22 +20,89 @@
     return lax.dot_general(a, b, (((ca,), (cb,)), ((), ())), preferred_element_type=F32)
 
 
-def attention_kernel(
-    img_ref, g_hbm, wk_hbm, wv_hbm, q_ref, d_ref, pay_hbm, o_ref, dq_ref,
-    guide, wk, wv, k_scr, v_scr, pay, sems, out_sems,
-):
+def ring_send(block, axis, distance):
+    return lax.ppermute(block, axis, [(i, (i + distance) % 4) for i in range(4)])
+
+
+def ring_gather(block, axis):
+    half = block.shape[0] // 2
+    before = ring_send(block, axis, 1)
+    after = ring_send(block, axis, 3)
+    first = ring_send(before[:half], axis, 1)
+    second = ring_send(after[half:], axis, 3)
+    return [block, after, first, second, before]
+
+
+def gather_guide(guide):
+    other = lax.ppermute(guide, "yh", SWAP)
+    near = [ring_gather(jnp.stack([guide[m], other[m]]), "xz"[m]) for m in (0, 1)]
+    near = [jnp.concatenate(blocks).reshape(4, 2, 16, D) for blocks in near]
+    return [ring_gather(near[m], "zx"[m]) for m in (0, 1)]
+
+
+def guide_pieces(m, blocks, pos_ref):
+    x, yh, z = pos_ref[0], pos_ref[1], pos_ref[2]
+    places = ((0, 0, 4), (1, 0, 4), (2, 0, 2), (2, 2, 2), (3, 0, 4))
+    for block, (two, start, count) in zip(blocks, places):
+        for i in range(count):
+            one = start + i
+            dx, dz = (one, two) if m == 0 else (two, one)
+            for dy in range(2):
+                place = ((x + dx) & 3) * 8 + ((yh + dy) & 1) * 4 + ((z + dz) & 3)
+                yield block.at[i, dy], place
+
+
+def whole_guide_kernel(pos_ref, *refs):
+    out, sems = refs[10], refs[11]
+    copies = []
+    for m in range(2):
+        for i, (source, place) in enumerate(guide_pieces(m, refs[5 * m : 5 * m + 5], pos_ref)):
+            copies.append(pltpu.make_async_copy(source, out.at[place, m], sems.at[32 * m + i]))
+            copies[-1].start()
+    for copy in copies:
+        copy.wait()
+
+
+def whole_guide(pos, blocks):
+    hbm = pl.BlockSpec(memory_space=pl.ANY)
+    return pl.pallas_call(
+        whole_guide_kernel,
+        in_specs=[pl.BlockSpec(memory_space=pltpu.SMEM)] + [hbm] * 10,
+        out_specs=hbm,
+        out_shape=jax.ShapeDtypeStruct((32, 2, 16, D), BF16),
+        scratch_shapes=[pltpu.SemaphoreType.DMA((64,))],
+        name="whole_guide",
+    )(pos, *blocks)
+
+
+def attention_kernel(img_ref, pos_ref, *refs):
+    blocks, refs = refs[:10], refs[10:]
+    wk_hbm, wv_hbm, q_ref, d_ref, pay_hbm, o_ref, dq_ref = refs[:7]
+    guide, wk, wv, k_scr, v_scr, pay, sems, guide_sems, out_sems = refs[7:]
     loads = [
-        pltpu.make_async_copy(g_hbm.at[:, img_ref[0]], guide, sems.at[0]),
-        pltpu.make_async_copy(wk_hbm, wk, sems.at[1]),
-        pltpu.make_async_copy(wv_hbm, wv, sems.at[2]),
+        pltpu.make_async_copy(wk_hbm, wk, sems.at[0]),
+        pltpu.make_async_copy(wv_hbm, wv, sems.at[1]),
     ]
-    for copy in loads:
-        copy.start()
+    for m in range(2):
+
+        @pl.when(img_ref[0] == m)
+        def _(m=m):
+            pieces = guide_pieces(m, blocks[5 * m : 5 * m + 5], pos_ref)
+            copies = [
+                pltpu.make_async_copy(source, guide.at[place], guide_sems.at[i])
+                for i, (source, place) in enumerate(pieces)
+            ]
+            for copy in copies:
+                copy.start()
+            for copy in loads:
+                copy.start()
+            for copy in copies:
+                copy.wait()
+
+    tokens = guide[...].reshape(G, D)
     loads[0].wait()
-    tokens = guide[...].reshape(G, D)
+    k_scr[...] = dot(tokens, wk[...], 1, 0).astype(BF16)
     loads[1].wait()
-    k_scr[...] = dot(tokens, wk[...], 1, 0).astype(BF16)
-    loads[2].wait()
     v_scr[...] = dot(tokens, wv[...], 1, 0).astype(BF16)
     scale = HD ** (-0.5)
     flag = jnp.full((4, G), img_ref[0], jnp.int32).astype(F32)
@@ -65,13 +132,13 @@
         copy.wait()
 
 
-def attention(img, whole, w_key, w_value, q, d):
+def attention(img, pos, blocks, w_key, w_value, q, d):
     t = q.shape[0]
     vmem = pl.BlockSpec(memory_space=pltpu.VMEM)
     hbm = pl.BlockSpec(memory_space=pl.ANY)
     return pl.pallas_call(
         attention_kernel,
-        in_specs=[pl.BlockSpec(memory_space=pltpu.SMEM), hbm, hbm, hbm, vmem, vmem],
+        in_specs=[pl.BlockSpec(memory_space=pltpu.SMEM)] * 2 + [hbm] * 12 + [vmem] * 2,
         out_specs=[hbm, vmem, vmem],
         out_shape=[
             jax.ShapeDtypeStruct((32, 2, 40, G), BF16),
@@ -85,11 +152,12 @@
             pltpu.VMEM((G, D), BF16),
             pltpu.VMEM((G, D), BF16),
             pltpu.VMEM((32, 2, 40, G), BF16),
-            pltpu.SemaphoreType.DMA((3,)),
+            pltpu.SemaphoreType.DMA((2,)),
+            pltpu.SemaphoreType.DMA((32,)),
             pltpu.SemaphoreType.DMA((HEADS,)),
         ],
         name="attention",
-    )(img, whole, w_key, w_value, q, d)
+    )(img, pos, *blocks, w_key, w_value, q, d)
 
 
 ROWS = 576
@@ -299,9 +367,9 @@
 def on_device(tiles, tile_image, guide, gain, w_query, w_key, w_value, w_out, grad_out):
     core = lax.axis_index("c")
     yl = lax.axis_index("yl")
-    whole = lax.all_to_all(
-        jnp.broadcast_to(guide, (32, *guide.shape)), TILE_AXES, 0, 0, tiled=True
-    )
+    pos = jnp.stack([lax.axis_index(name) for name in ("x", "yh", "z")])
+    zero_blocks, one_blocks = gather_guide(guide)
+    blocks = zero_blocks + one_blocks
     xf = tiles.astype(F32)
     rstd = lax.rsqrt(jnp.mean(xf * xf, axis=-1, keepdims=True) + 1e-06)
     normed = xf * rstd
@@ -314,7 +382,7 @@
     grad_got = lax.ppermute(grad_out, "c", SWAP)
     query, hid_rows = lax.optimization_barrier((query, hid_rows))
 
-    pay, outv, dq = attention(tile_image, whole, w_key, w_value, query, dout)
+    pay, outv, dq = attention(tile_image, pos, blocks, w_key, w_value, query, dout)
     got = lax.all_to_all(pay, TILE_AXES, 0, 0, tiled=True)
 
     dq_got = lax.ppermute(dq, "c", SWAP)
@@ -326,7 +394,8 @@
     dn = dh * gain
     grad_tiles = (rstd * (dn - normed * jnp.mean(dn * normed, axis=-1, keepdims=True))).astype(BF16)
 
-    got, ninth, gain_part = lax.optimization_barrier((got, ninth, gain_part))
+    whole = whole_guide(pos, blocks)
+    got, ninth, gain_part, whole = lax.optimization_barrier((got, ninth, gain_part, whole))
     mine, theirs, tok = image_sums(core[None], got, whole)
     send = fill_rest(send, mine, lax.ppermute(theirs, "c", SWAP), tok, ninth, gain_part)
     recv = lax.all_to_all(send, CHIP_AXES, 0, 0, tiled=True)

time: 186 us -> 242 us (1.30)
  Pallas kernels: 46.3 us -> 120 us
  waiting for transfers between devices: 86.5 us -> 47.4 us
  starting transfers between devices: 29.8 us -> 47.4 us
  other arithmetic: 5.3 us -> 8.11 us
    pallas_call x0 -> x1, Pallas kernels: none -> 73.8 us  [whole_guide(): pl.pallas_call(whole_guide_kernel, in_specs=[pl.BlockSpec(memory_space=pl...]
    ppermute x0 -> x17, starting transfers between devices: none -> 28 us  [the longest x16 24.7 us: ring_send(): lax.ppermute(block, axis, [(i, (i + distance) % 4) for i in range(4)])]
    all_to_all x1, waiting for transfers between devices: 20.8 us -> 0.01 us  [on_device(): got = lax.all_to_all(pay, TILE_AXES, 0, 0, tiled=True)]
    all_to_all x1 -> x0, waiting for transfers between devices: 20.1 us -> none  [on_device(): lax.all_to_all(jnp.broadcast_to(guide, (32, *guide.shape)), TILE_AXES, 0,...]
    all_to_all x1 -> x0, starting transfers between devices: 11.3 us -> none  [on_device(): lax.all_to_all(jnp.broadcast_to(guide, (32, *guide.shape)), TILE_AXES, 0,...]
    broadcast_in_dim x1 -> x0, local copies, waits for them, and re-layouts: 2.63 us -> none  [on_device(): jnp.broadcast_to(guide, (32, *guide.shape))]
  transfers between devices with their start and end apart: 9 -> 25, of which waited for: 4 -> 3; matrix products, arithmetic and copies ran while one was open for 9% -> 9% of each run, Pallas kernels for 3% -> 33%
where the time goes in v3:
time: 242 us; the launch traced here: 240 us
  Pallas kernels  120 us (50%)
  starting transfers between devices  47.4 us (20%)
  waiting for transfers between devices  47.4 us (20%)
  matrix products  12.7 us (5%)
  other arithmetic  8.11 us (3%)
    pallas_call x1, Pallas kernels, whole_guide(): pl.pallas_call(whole_guide_kernel, in_specs=[pl.BlockSpec(memory_space=pl...  73.8 us
    all_to_all x1, waiting for transfers between devices, on_device(): recv = lax.all_to_all(send, CHIP_AXES, 0, 0, tiled=True)  43.7 us
    ppermute x16, starting transfers between devices, ring_send(): lax.ppermute(block, axis, [(i, (i + distance) % 4) for i in range(4)])  24.7 us
    pallas_call x1, Pallas kernels, attention(): pl.pallas_call(attention_kernel, in_specs=[pl.BlockSpec(memory_space=pltp...  22 us
    dot_general x4, matrix products, dot(): lax.dot_general(a, b, (((ca,), (cb,)), ((), ())), preferred_element_type=...  12.7 us
    all_to_all x1, starting transfers between devices, on_device(): recv = lax.all_to_all(send, CHIP_AXES, 0, 0, tiled=True)  10.4 us
    pallas_call x1, Pallas kernels, finish(): pl.pallas_call(finish_kernel, in_specs=[pl.BlockSpec(memory_space=pltpu.S...  8.1 us
    all_to_all x1, starting transfers between devices, on_device(): got = lax.all_to_all(pay, TILE_AXES, 0, 0, tiled=True)  7.79 us
  transfers between devices with their start and end apart: 25, of which 3 were waited for; matrix products, arithmetic and copies ran while one was open for 9% of the time, Pallas kernels for 33%

profile of v3, /device:TPU:2, one launch (start us, length us, event | category | flops | bytes accessed | tf_op | source)
XLA Modules:
  0.0 240.2 jit_solution(11659950414055979011)
XLA Ops:
  0.6 0.0 copy-start
  0.7 3.3 %collective-permute-start = (bf16[2,16,1152]{2,1,0:T(8,128)(2,1)}, bf16[2,16,1152]{2,1,0:T(8,128)(2,1)S(1)}, u32[]{:S(2)}, u32[]{:S(2)}) collective-permute-start(bf16[2,16,1152]{2,1,0:T(8,128)(2,1)} %param.11), channel_id=1, source_target_pairs={{0,4},{4,0},{1,5},{5,1},{2,6},{6,2},{3,7},{7,3},{8,12},{12,8},{9,1... | collective-permute-start | bytes 221192 | tf_op jit(solution)/shard_map/ppermute | solution.py:37
  3.9 1.3 fusion.13
  5.2 2.1 fusion.7
  8.0 2.9 %convolution_convert_fusion.1.refs_12_ = bf16[256,1152]{1,0:T(8,128)(2,1)} fusion(bf16[256,1152]{1,0:T(8,128)(2,1)} %fusion.7, bf16[1152,1152]{1,0:T(8,128)(2,1)S(1)} %copy-done), kind=kOutput, calls=%fused_computation.3 | convolution fusion | flops 679772160 | bytes 3833856 | tf_op jit(solution)/shard_map/dot_general | solution.py:20
  10.9 1.6 collective-permute-start.2
  12.5 0.5 collective-permute-start.1
  13.0 2.0 collective-permute-start.10
  15.0 2.2 collective-permute-start.9
  17.2 0.6 pad_add_fusion.pos_ref
  17.8 0.0 collective-permute-done.2
  17.8 1.5 collective-permute-start.3
  19.3 0.0 collective-permute-done.1
  19.3 0.5 collective-permute-start.4
  19.9 0.0 collective-permute-done.10
  19.9 0.0 collective-permute-start.11
  19.9 0.0 collective-permute-done.9
  19.9 3.2 %collective-permute-start.12 = (bf16[1,16,1152]{2,1,0:T(8,128)(2,1)S(1)}, bf16[1,16,1152]{2,1,0:T(8,128)(2,1)S(1)}, u32[]{:S(2)}, u32[]{:S(2)}) collective-permute-start(bf16[1,16,1152]{2,1,0:T(8,128)(2,1)S(1)} %slice.55), channel_id=1, source_target_pairs={{0,3},{1,0},{2,1},{3,2},{4,7},{5,4},{6,5},{7,6},{8,11},{9,8},{10,9... | collective-permute-start | bytes 110600 | tf_op jit(solution)/shard_map/ppermute | solution.py:24
  23.2 1.9 collective-permute-done.11
  25.1 0.0 collective-permute-done.12
  25.1 1.6 collective-permute-start.14
  26.7 1.5 collective-permute-start.13
  28.2 0.0 collective-permute-done.3
  28.2 0.0 collective-permute-done.4
  28.3 0.6 collective-permute-start.6
  28.9 2.8 %collective-permute-start.5 = (bf16[4,2,16,1152]{3,2,1,0:T(8,128)(2,1)S(1)}, bf16[4,2,16,1152]{3,2,1,0:T(8,128)(2,1)S(1)}, u32[]{:S(2)}, u32[]{:S(2)}) collective-permute-start(bf16[4,2,16,1152]{3,2,1,0:T(8,128)(2,1)S(1)} %bitcast.17), channel_id=1, source_target_pairs={{0,3},{1,0},{2,1},{3,2},{4,7},{5,4},{6,5},{7,6},{8,11},{9,8},{10,9... | collective-permute-start | bytes 884744 | tf_op jit(solution)/shard_map/ppermute | solution.py:24
  31.7 3.6 %convolution_convert_fusion.refs_13_ = bf16[256,1152]{1,0:T(8,128)(2,1)} fusion(bf16[256,1152]{1,0:T(8,128)(2,1)S(1)} %copy-done.8, bf16[1152,1152]{1,0:T(8,128)(2,1)} %param.16), kind=kOutput, calls=%fused_computation.2 | convolution fusion | flops 679772160 | bytes 3833856 | tf_op jit(solution)/shard_map/dot_general | solution.py:20
  35.3 0.0 collective-permute-done.14.refs_9_
  35.3 0.5 collective-permute-start.15
  35.9 0.0 collective-permute-done.13.refs_6_
  35.9 2.8 %collective-permute-start.16 = (bf16[2,2,16,1152]{3,2,1,0:T(8,128)(2,1)S(1)}, bf16[2,2,16,1152]{3,2,1,0:T(8,128)(2,1)S(1)}, u32[]{:S(2)}, u32[]{:S(2)}) collective-permute-start(bf16[2,2,16,1152]{3,2,1,0:T(8,128)(2,1)S(1)} %slice.57), channel_id=1, source_target_pairs={{0,24},{8,0},{16,8},{24,16},{1,25},{9,1},{17,9},{25,17},{2,26},{10... | collective-permute-start | bytes 442376 | tf_op jit(solution)/shard_map/ppermute | solution.py:24
  38.6 0.0 collective-permute-done.6.refs_4_
  38.7 0.1 collective-permute-start.7
  38.8 0.0 collective-permute-done.5.refs_1_
  38.8 3.3 %collective-permute-start.8 = (bf16[2,2,16,1152]{3,2,1,0:T(8,128)(2,1)S(1)}, bf16[2,2,16,1152]{3,2,1,0:T(8,128)(2,1)S(1)}, u32[]{:S(2)}, u32[]{:S(2)}) collective-permute-start(bf16[2,2,16,1152]{3,2,1,0:T(8,128)(2,1)S(1)} %slice.52), channel_id=1, source_target_pairs={{0,3},{1,0},{2,1},{3,2},{4,7},{5,4},{6,5},{7,6},{8,11},{9,8},{10,9... | collective-permute-start | bytes 442376 | tf_op jit(solution)/shard_map/ppermute | solution.py:24
  42.1 0.0 collective-permute-done.17
  42.1 3.1 %fusion.6.hid_ref = bf16[576,512]{1,0:T(8,128)(2,1)} fusion(s32[576]{0:T(1024)S(1)} %fusion.44, bf16[256,1152]{1,0:T(8,128)(2,1)} %collective-permute-done.17, bf16[256,1152]{1,0:T(8,128)(2,1)} %fusion.7), kind=kOutput, calls=%fused_computation.11 | convolution fusion | flops 682795008 | bytes 1771776 | tf_op jit(solution)/shard_map/dot_general | solution.py:20
  45.3 0.0 copy-start.11
  45.3 0.6 copy-done.9
  45.9 0.0 copy-done.10
  45.9 0.1 copy-done.11
  46.0 0.7 copy-done.12
  46.6 22.0 %attention.1 = (bf16[32,2,40,512]{3,2,1,0:T(8,128)(2,1)}, bf16[256,1152]{1,0:T(8,128)(2,1)}, bf16[256,1152]{1,0:T(8,128)(2,1)}) custom-call(s32[1]{0:T(128)S(6)} %copy.25.img_ref, s32[3]{0:T(128)} %pad_add_fusion.pos_ref, bf16[4,2,16,1152]{3,2,1,0:T(8,128)(2,1)} %bitcast.18, bf16[4,2,16,1152]{3,2,1,0:T(8,128)(2,1)} %copy-done.5, ...), custom_call_target="tpu_custom_call" | custom-call | tf_op jit(solution)/shard_map/attention/pallas_call | solution.py:139
  68.6 0.0 copy-start.1
  68.6 0.0 copy-start.15
  68.6 7.8 %all-to-all-start = ((bf16[32,2,40,512]{3,2,1,0:T(8,128)(2,1)}), bf16[32,2,40,512]{3,2,1,0:T(8,128)(2,1)}, u32[]{:S(2)}, u32[]{:S(2)}) async-start(bf16[32,2,40,512]{3,2,1,0:T(8,128)(2,1)} %get-tuple-element.26), calls=%async_computation | async-start | bytes 5242880 | tf_op jit(solution)/shard_map/all_to_all | solution.py:386
  76.4 0.1 collective-permute-start.20
  76.5 0.5 collective-permute-start.18
  77.0 0.1 collective-permute-start.19
  77.1 3.2 %fusion.12 = (f32[1152]{0:T(1024)S(1)}, f32[256]{0:T(256)S(1)}, f32[256,1152]{1,0:T(8,128)}) fusion(bf16[256,1152]{1,0:T(8,128)(2,1)S(1)} %copy-done.1, f32[256]{0:T(256)S(1)} %add_rsqrt_fusion, f32[1152]{0:T(1024)S(1)} %copy-done.15, bf16[256,1152]{1,0:T(8,128)(2,1)} %get-tuple-element.22.dq_ref, bf16[1152,1152]{1,0:T(8,128)(2,1)S(1)} %copy-done), kind=kOutput, calls=%fused_computation.17 | convolution fusion | flops 681540224 | bytes 5024768 | tf_op jit(solution)/shard_map/dot_general | solution.py:20
  80.3 0.4 collective-permute-start.21
  80.7 1.1 fusion.28.want_ref
  81.8 73.8 %whole_guide.1.g_ref = bf16[32,2,16,1152]{3,2,1,0:T(8,128)(2,1)} custom-call(s32[3]{0:T(128)} %pad_add_fusion.pos_ref, bf16[4,2,16,1152]{3,2,1,0:T(8,128)(2,1)} %bitcast.19, bf16[4,2,16,1152]{3,2,1,0:T(8,128)(2,1)} %copy-done.5, bf16[2,2,16,1152]{3,2,1,0:T(8,128)(2,1)} %copy-done.11, bf16[2,2,16,1152]{3,2,1,0:T(8,128)(2,1)} %copy-done.12, ...), custom_call_target="tpu_custom_call" | custom-call | tf_op jit(solution)/shard_map/whole_guide/pallas_call | solution.py:68
  155.6 0.6 reshape_add_fusion.gain_ref
  156.2 6.4 %weight_parts.1 = (bf16[64,3,8,1152]{3,2,1,0:T(8,128)(2,1)}, f32[64,2304]{1,0:T(8,128)}) custom-call(s32[576,1]{1,0:T(8,128)} %fusion.28.want_ref, bf16[576,512]{1,0:T(8,128)(2,1)} %fusion.6.hid_ref, bf16[256,1152]{1,0:T(8,128)(2,1)} %get-tuple-element.24.o_ref, bf16[256,1152]{1,0:T(8,128)(2,1)} %collective-permute-done.18.o2_ref, ...), custom_call_target="tpu_custom_call" | custom-call | tf_op jit(solution)/shard_map/weight_parts/pallas_call | solution.py:194
  162.6 6.3 %image_sums.1 = (f32[576,128]{1,0:T(8,128)}, f32[576,128]{1,0:T(8,128)}, f32[512,256]{1,0:T(8,128)}) custom-call(s32[1]{0:T(128)} %bitcast.6.core_ref, bf16[32,2,40,512]{3,2,1,0:T(8,128)(2,1)} %all-to-all-done.got_ref, bf16[32,2,16,1152]{3,2,1,0:T(8,128)(2,1)} %whole_guide.1.g_ref), custom_call_target="tpu_custom_call" | custom-call | tf_op jit(solution)/shard_map/image_sums/pallas_call | solution.py:234
  168.9 0.1 collective-permute-start.22
  169.0 1.7 collective-permute-done.22.got_ref
  170.7 0.7 copy-done.13
  171.4 3.9 %fill_rest.1 = bf16[64,3,8,1152]{3,2,1,0:T(8,128)(2,1)} custom-call(bf16[64,3,8,1152]{3,2,1,0:T(8,128)(2,1)} %get-tuple-element.25.send_ref, f32[576,128]{1,0:T(8,128)} %get-tuple-element.30.mine_ref, f32[576,128]{1,0:T(8,128)} %copy-done.13, f32[512,256]{1,0:T(8,128)} %get-tuple-element.32.tok_ref, ...), custom_call_target="tpu_custom_call", output_to_operand_aliasing={{}: (0, {})} | custom-call | tf_op jit(solution)/shard_map/fill_rest/pallas_call | solution.py:283
  175.3 10.4 %all-to-all-start.1 = ((bf16[64,3,8,1152]{3,2,1,0:T(8,128)(2,1)}), bf16[64,3,8,1152]{3,2,1,0:T(8,128)(2,1)}, u32[]{:S(2)}, u32[]{:S(2)}) async-start(bf16[64,3,8,1152]{3,2,1,0:T(8,128)(2,1)} %fill_rest.1), calls=%async_computation.1 | async-start | bytes 7077888 | tf_op jit(solution)/shard_map/all_to_all | solution.py:401
  185.8 2.4 fusion.11
  188.2 43.7 %all-to-all-done.1.recv_ref = bf16[64,3,8,1152]{3,2,1,0:T(8,128)(2,1)} async-done(((bf16[64,3,8,1152]{3,2,1,0:T(8,128)(2,1)}), bf16[64,3,8,1152]{3,2,1,0:T(8,128)(2,1)}, u32[]{:S(2)}, u32[]{:S(2)}) %all-to-all-start.1) | async-done | bytes 3538976 | tf_op jit(solution)/shard_map/all_to_all | solution.py:401
  231.9 8.1 %finish.1 = (f32[9,4,1152]{2,1,0:T(4,128)}, bf16[32,1152]{1,0:T(8,128)(2,1)}, f32[9,128]{1,0:T(8,128)}) custom-call(s32[1]{0:T(128)} %bitcast.5.yl_ref, bf16[64,3,8,1152]{3,2,1,0:T(8,128)(2,1)} %all-to-all-done.1.recv_ref, bf16[1152,1152]{1,0:T(8,128)(2,1)} %wk_hbm.1, bf16[1152,1152]{1,0:T(8,128)(2,1)} %wv_hbm.1), custom_call_target="tpu_custom_call" | custom-call | tf_op jit(solution)/shard_map/finish/pallas_call | solution.py:348
  (58 shorter events, 0.3 us)
Async XLA Ops:
  0.6 7.3 %copy-start = (bf16[1152,1152]{1,0:T(8,128)(2,1)S(1)}, bf16[1152,1152]{1,0:T(8,128)(2,1)}, u32[]{:S(2)}) copy-start(bf16[1152,1152]{1,0:T(8,128)(2,1)} %param.13) | copy-start | bytes 7962628
  0.6 6.6 %copy-start.14 = (bf16[2,16,1152]{2,1,0:T(8,128)(2,1)S(1)}, bf16[2,16,1152]{2,1,0:T(8,128)(2,1)}, u32[]{:S(2)}) copy-start(bf16[2,16,1152]{2,1,0:T(8,128)(2,1)} %param.11) | copy-start | bytes 221188
  0.7 10.2 %collective-permute-start = (bf16[2,16,1152]{2,1,0:T(8,128)(2,1)}, bf16[2,16,1152]{2,1,0:T(8,128)(2,1)S(1)}, u32[]{:S(2)}, u32[]{:S(2)}) collective-permute-start(bf16[2,16,1152]{2,1,0:T(8,128)(2,1)} %param.11), channel_id=1, source_target_pairs={{0,4},{4,0},{1,5},{5,1},{2,6},{6,2},{3,7},{7,3},{8,12},{12,8},{9,1... | collective-permute-start | bytes 221192 | tf_op jit(solution)/shard_map/ppermute | solution.py:37
  7.3 34.8 %collective-permute-start.17 = (bf16[256,1152]{1,0:T(8,128)(2,1)}, bf16[256,1152]{1,0:T(8,128)(2,1)}, u32[]{:S(2)}, u32[]{:S(2)}) collective-permute-start(bf16[256,1152]{1,0:T(8,128)(2,1)} %fusion.7), channel_id=1, source_target_pairs={{0,32},{32,0},{1,33},{33,1},{2,34},{34,2},{3,35},{35,3},{4,36},{36... | collective-permute-start | bytes 1769480 | tf_op jit(solution)/shard_map/ppermute | solution.py:380
  10.8 20.8 %copy-start.8 = (bf16[256,1152]{1,0:T(8,128)(2,1)S(1)}, bf16[256,1152]{1,0:T(8,128)(2,1)}, u32[]{:S(2)}) copy-start(bf16[256,1152]{1,0:T(8,128)(2,1)} %g_ref.1) | copy-start | bytes 1769476
  10.9 6.9 %collective-permute-start.2 = (bf16[2,16,1152]{2,1,0:T(8,128)(2,1)S(1)}, bf16[2,16,1152]{2,1,0:T(8,128)(2,1)S(1)}, u32[]{:S(2)}, u32[]{:S(2)}) collective-permute-start(bf16[2,16,1152]{2,1,0:T(8,128)(2,1)S(1)} %pad_maximum_fusion), channel_id=1, source_target_pairs={{0,8},{8,16},{16,24},{24,0},{1,9},{9,17},{17,25},{25,1},{2,10},{10... | collective-permute-start | bytes 221192 | tf_op jit(solution)/shard_map/ppermute | solution.py:24
  12.5 6.9 %collective-permute-start.1 = (bf16[2,16,1152]{2,1,0:T(8,128)(2,1)S(1)}, bf16[2,16,1152]{2,1,0:T(8,128)(2,1)S(1)}, u32[]{:S(2)}, u32[]{:S(2)}) collective-permute-start(bf16[2,16,1152]{2,1,0:T(8,128)(2,1)S(1)} %pad_maximum_fusion), channel_id=1, source_target_pairs={{0,24},{8,0},{16,8},{24,16},{1,25},{9,1},{17,9},{25,17},{2,26},{10... | collective-permute-start | bytes 221192 | tf_op jit(solution)/shard_map/ppermute | solution.py:24
  13.0 6.9 %collective-permute-start.10 = (bf16[2,16,1152]{2,1,0:T(8,128)(2,1)S(1)}, bf16[2,16,1152]{2,1,0:T(8,128)(2,1)S(1)}, u32[]{:S(2)}, u32[]{:S(2)}) collective-permute-start(bf16[2,16,1152]{2,1,0:T(8,128)(2,1)S(1)} %pad_maximum_fusion.1), channel_id=1, source_target_pairs={{0,1},{1,2},{2,3},{3,0},{4,5},{5,6},{6,7},{7,4},{8,9},{9,10},{10,1... | collective-permute-start | bytes 221192 | tf_op jit(solution)/shard_map/ppermute | solution.py:24
  15.0 4.9 %collective-permute-start.9 = (bf16[2,16,1152]{2,1,0:T(8,128)(2,1)S(1)}, bf16[2,16,1152]{2,1,0:T(8,128)(2,1)S(1)}, u32[]{:S(2)}, u32[]{:S(2)}) collective-permute-start(bf16[2,16,1152]{2,1,0:T(8,128)(2,1)S(1)} %pad_maximum_fusion.1), channel_id=1, source_target_pairs={{0,3},{1,0},{2,1},{3,2},{4,7},{5,4},{6,5},{7,6},{8,11},{9,8},{10,9... | collective-permute-start | bytes 221192 | tf_op jit(solution)/shard_map/ppermute | solution.py:24
  17.8 10.4 %collective-permute-start.3 = (bf16[1,16,1152]{2,1,0:T(8,128)(2,1)S(1)}, bf16[1,16,1152]{2,1,0:T(8,128)(2,1)S(1)}, u32[]{:S(2)}, u32[]{:S(2)}) collective-permute-start(bf16[1,16,1152]{2,1,0:T(8,128)(2,1)S(1)} %slice.49), channel_id=1, source_target_pairs={{0,8},{8,16},{16,24},{24,0},{1,9},{9,17},{17,25},{25,1},{2,10},{10... | collective-permute-start | bytes 110600 | tf_op jit(solution)/shard_map/ppermute | solution.py:24
  19.3 8.9 %collective-permute-start.4 = (bf16[1,16,1152]{2,1,0:T(8,128)(2,1)S(1)}, bf16[1,16,1152]{2,1,0:T(8,128)(2,1)S(1)}, u32[]{:S(2)}, u32[]{:S(2)}) collective-permute-start(bf16[1,16,1152]{2,1,0:T(8,128)(2,1)S(1)} %slice.50), channel_id=1, source_target_pairs={{0,24},{8,0},{16,8},{24,16},{1,25},{9,1},{17,9},{25,17},{2,26},{10... | collective-permute-start | bytes 110600 | tf_op jit(solution)/shard_map/ppermute | solution.py:24
  19.9 5.2 %collective-permute-start.11 = (bf16[1,16,1152]{2,1,0:T(8,128)(2,1)S(1)}, bf16[1,16,1152]{2,1,0:T(8,128)(2,1)S(1)}, u32[]{:S(2)}, u32[]{:S(2)}) collective-permute-start(bf16[1,16,1152]{2,1,0:T(8,128)(2,1)S(1)} %slice.54), channel_id=1, source_target_pairs={{0,1},{1,2},{2,3},{3,0},{4,5},{5,6},{6,7},{7,4},{8,9},{9,10},{10,1... | collective-permute-start | bytes 110600 | tf_op jit(solution)/shard_map/ppermute | solution.py:24
  19.9 5.2 %collective-permute-start.12 = (bf16[1,16,1152]{2,1,0:T(8,128)(2,1)S(1)}, bf16[1,16,1152]{2,1,0:T(8,128)(2,1)S(1)}, u32[]{:S(2)}, u32[]{:S(2)}) collective-permute-start(bf16[1,16,1152]{2,1,0:T(8,128)(2,1)S(1)} %slice.55), channel_id=1, source_target_pairs={{0,3},{1,0},{2,1},{3,2},{4,7},{5,4},{6,5},{7,6},{8,11},{9,8},{10,9... | collective-permute-start | bytes 110600 | tf_op jit(solution)/shard_map/ppermute | solution.py:24
  25.1 10.2 %copy-start.7 = (bf16[8,16,1152]{2,1,0:T(8,128)(2,1)}, bf16[8,16,1152]{2,1,0:T(8,128)(2,1)S(1)}, u32[]{:S(2)}) copy-start(bf16[8,16,1152]{2,1,0:T(8,128)(2,1)S(1)} %constant_dynamic-update-slice_fusion.6) | copy-start | bytes 884740
  25.1 10.2 %collective-permute-start.14 = (bf16[4,2,16,1152]{3,2,1,0:T(8,128)(2,1)S(1)}, bf16[4,2,16,1152]{3,2,1,0:T(8,128)(2,1)S(1)}, u32[]{:S(2)}, u32[]{:S(2)}) collective-permute-start(bf16[4,2,16,1152]{3,2,1,0:T(8,128)(2,1)S(1)} %bitcast.20), channel_id=1, source_target_pairs={{0,8},{8,16},{16,24},{24,0},{1,9},{9,17},{17,25},{25,1},{2,10},{10... | collective-permute-start | bytes 884744 | tf_op jit(solution)/shard_map/ppermute | solution.py:24
  26.7 9.2 %collective-permute-start.13 = (bf16[4,2,16,1152]{3,2,1,0:T(8,128)(2,1)S(1)}, bf16[4,2,16,1152]{3,2,1,0:T(8,128)(2,1)S(1)}, u32[]{:S(2)}, u32[]{:S(2)}) collective-permute-start(bf16[4,2,16,1152]{3,2,1,0:T(8,128)(2,1)S(1)} %bitcast.21), channel_id=1, source_target_pairs={{0,24},{8,0},{16,8},{24,16},{1,25},{9,1},{17,9},{25,17},{2,26},{10... | collective-permute-start | bytes 884744 | tf_op jit(solution)/shard_map/ppermute | solution.py:24
  28.3 16.9 %copy-start.6 = (bf16[8,16,1152]{2,1,0:T(8,128)(2,1)}, bf16[8,16,1152]{2,1,0:T(8,128)(2,1)S(1)}, u32[]{:S(2)}) copy-start(bf16[8,16,1152]{2,1,0:T(8,128)(2,1)S(1)} %constant_dynamic-update-slice_fusion) | copy-start | bytes 884740
  28.3 10.4 %collective-permute-start.6 = (bf16[4,2,16,1152]{3,2,1,0:T(8,128)(2,1)S(1)}, bf16[4,2,16,1152]{3,2,1,0:T(8,128)(2,1)S(1)}, u32[]{:S(2)}, u32[]{:S(2)}) collective-permute-start(bf16[4,2,16,1152]{3,2,1,0:T(8,128)(2,1)S(1)} %bitcast.16), channel_id=1, source_target_pairs={{0,1},{1,2},{2,3},{3,0},{4,5},{5,6},{6,7},{7,4},{8,9},{9,10},{10,1... | collective-permute-start | bytes 884744 | tf_op jit(solution)/shard_map/ppermute | solution.py:24
  28.9 9.9 %collective-permute-start.5 = (bf16[4,2,16,1152]{3,2,1,0:T(8,128)(2,1)S(1)}, bf16[4,2,16,1152]{3,2,1,0:T(8,128)(2,1)S(1)}, u32[]{:S(2)}, u32[]{:S(2)}) collective-permute-start(bf16[4,2,16,1152]{3,2,1,0:T(8,128)(2,1)S(1)} %bitcast.17), channel_id=1, source_target_pairs={{0,3},{1,0},{2,1},{3,2},{4,7},{5,4},{6,5},{7,6},{8,11},{9,8},{10,9... | collective-permute-start | bytes 884744 | tf_op jit(solution)/shard_map/ppermute | solution.py:24
  35.3 9.9 %copy-start.2 = (bf16[4,2,16,1152]{3,2,1,0:T(8,128)(2,1)}, bf16[4,2,16,1152]{3,2,1,0:T(8,128)(2,1)S(1)}, u32[]{:S(2)}) copy-start(bf16[4,2,16,1152]{3,2,1,0:T(8,128)(2,1)S(1)} %collective-permute-done.14.refs_9_) | copy-start | bytes 884740
  35.3 9.9 %collective-permute-start.15 = (bf16[2,2,16,1152]{3,2,1,0:T(8,128)(2,1)S(1)}, bf16[2,2,16,1152]{3,2,1,0:T(8,128)(2,1)S(1)}, u32[]{:S(2)}, u32[]{:S(2)}) collective-permute-start(bf16[2,2,16,1152]{3,2,1,0:T(8,128)(2,1)S(1)} %slice.56), channel_id=1, source_target_pairs={{0,8},{8,16},{16,24},{24,0},{1,9},{9,17},{17,25},{25,1},{2,10},{10... | collective-permute-start | bytes 442376 | tf_op jit(solution)/shard_map/ppermute | solution.py:24
  35.9 9.3 %copy-start.3 = (bf16[4,2,16,1152]{3,2,1,0:T(8,128)(2,1)}, bf16[4,2,16,1152]{3,2,1,0:T(8,128)(2,1)S(1)}, u32[]{:S(2)}) copy-start(bf16[4,2,16,1152]{3,2,1,0:T(8,128)(2,1)S(1)} %collective-permute-done.13.refs_6_) | copy-start | bytes 884740
  35.9 9.4 %collective-permute-start.16 = (bf16[2,2,16,1152]{3,2,1,0:T(8,128)(2,1)S(1)}, bf16[2,2,16,1152]{3,2,1,0:T(8,128)(2,1)S(1)}, u32[]{:S(2)}, u32[]{:S(2)}) collective-permute-start(bf16[2,2,16,1152]{3,2,1,0:T(8,128)(2,1)S(1)} %slice.57), channel_id=1, source_target_pairs={{0,24},{8,0},{16,8},{24,16},{1,25},{9,1},{17,9},{25,17},{2,26},{10... | collective-permute-start | bytes 442376 | tf_op jit(solution)/shard_map/ppermute | solution.py:24
  38.7 6.5 %copy-start.4 = (bf16[4,2,16,1152]{3,2,1,0:T(8,128)(2,1)}, bf16[4,2,16,1152]{3,2,1,0:T(8,128)(2,1)S(1)}, u32[]{:S(2)}) copy-start(bf16[4,2,16,1152]{3,2,1,0:T(8,128)(2,1)S(1)} %collective-permute-done.6.refs_4_) | copy-start | bytes 884740
  38.7 6.6 %collective-permute-start.7 = (bf16[2,2,16,1152]{3,2,1,0:T(8,128)(2,1)S(1)}, bf16[2,2,16,1152]{3,2,1,0:T(8,128)(2,1)S(1)}, u32[]{:S(2)}, u32[]{:S(2)}) collective-permute-start(bf16[2,2,16,1152]{3,2,1,0:T(8,128)(2,1)S(1)} %slice.51), channel_id=1, source_target_pairs={{0,1},{1,2},{2,3},{3,0},{4,5},{5,6},{6,7},{7,4},{8,9},{9,10},{10,1... | collective-permute-start | bytes 442376 | tf_op jit(solution)/shard_map/ppermute | solution.py:24
  38.8 6.4 %copy-start.5 = (bf16[4,2,16,1152]{3,2,1,0:T(8,128)(2,1)}, bf16[4,2,16,1152]{3,2,1,0:T(8,128)(2,1)S(1)}, u32[]{:S(2)}) copy-start(bf16[4,2,16,1152]{3,2,1,0:T(8,128)(2,1)S(1)} %collective-permute-done.5.refs_1_) | copy-start | bytes 884740
  38.8 6.5 %collective-permute-start.8 = (bf16[2,2,16,1152]{3,2,1,0:T(8,128)(2,1)S(1)}, bf16[2,2,16,1152]{3,2,1,0:T(8,128)(2,1)S(1)}, u32[]{:S(2)}, u32[]{:S(2)}) collective-permute-start(bf16[2,2,16,1152]{3,2,1,0:T(8,128)(2,1)S(1)} %slice.52), channel_id=1, source_target_pairs={{0,3},{1,0},{2,1},{3,2},{4,7},{5,4},{6,5},{7,6},{8,11},{9,8},{10,9... | collective-permute-start | bytes 442376 | tf_op jit(solution)/shard_map/ppermute | solution.py:24
  45.2 0.7 copy-start.9
  45.2 0.7 copy-start.10
  45.3 0.7 copy-start.11
  46.0 0.7 copy-start.12
  68.6 8.5 %copy-start.1 = (bf16[256,1152]{1,0:T(8,128)(2,1)S(1)}, bf16[256,1152]{1,0:T(8,128)(2,1)}, u32[]{:S(2)}) copy-start(bf16[256,1152]{1,0:T(8,128)(2,1)} %param.9) | copy-start | bytes 1769476
  68.6 8.5 %copy-start.15 = (f32[1152]{0:T(1024)S(1)}, f32[1152]{0:T(1024)}, u32[]{:S(2)}) copy-start(f32[1152]{0:T(1024)} %param.12) | copy-start | bytes 13828
  68.6 94.0 %all-to-all-start = ((bf16[32,2,40,512]{3,2,1,0:T(8,128)(2,1)}), bf16[32,2,40,512]{3,2,1,0:T(8,128)(2,1)}, u32[]{:S(2)}, u32[]{:S(2)}) async-start(bf16[32,2,40,512]{3,2,1,0:T(8,128)(2,1)} %get-tuple-element.26), calls=%async_computation | async-start | bytes 5242880 | tf_op jit(solution)/shard_map/all_to_all | solution.py:386
  76.4 79.8 %collective-permute-start.20 = (bf16[256,1152]{1,0:T(8,128)(2,1)}, bf16[256,1152]{1,0:T(8,128)(2,1)}, u32[]{:S(2)}, u32[]{:S(2)}) collective-permute-start(bf16[256,1152]{1,0:T(8,128)(2,1)} %g_ref.1), channel_id=1, source_target_pairs={{0,32},{32,0},{1,33},{33,1},{2,34},{34,2},{3,35},{35,3},{4,36},{36... | collective-permute-start | bytes 1769480 | tf_op jit(solution)/shard_map/ppermute | solution.py:382
  76.5 79.7 %collective-permute-start.18 = (bf16[256,1152]{1,0:T(8,128)(2,1)}, bf16[256,1152]{1,0:T(8,128)(2,1)}, u32[]{:S(2)}, u32[]{:S(2)}) collective-permute-start(bf16[256,1152]{1,0:T(8,128)(2,1)} %get-tuple-element.24.o_ref), channel_id=1, source_target_pairs={{0,32},{32,0},{1,33},{33,1},{2,34},{34,2},{3,35},{35,3},{4,36},{36... | collective-permute-start | bytes 1769480 | tf_op jit(solution)/shard_map/ppermute | solution.py:389
  77.0 79.2 %collective-permute-start.19 = (bf16[256,1152]{1,0:T(8,128)(2,1)}, bf16[256,1152]{1,0:T(8,128)(2,1)}, u32[]{:S(2)}, u32[]{:S(2)}) collective-permute-start(bf16[256,1152]{1,0:T(8,128)(2,1)} %get-tuple-element.22.dq_ref), channel_id=1, source_target_pairs={{0,32},{32,0},{1,33},{33,1},{2,34},{34,2},{3,35},{35,3},{4,36},{36... | collective-permute-start | bytes 1769480 | tf_op jit(solution)/shard_map/ppermute | solution.py:388
  80.3 75.3 %collective-permute-start.21 = (f32[1,1152]{1,0:T(1,128)S(1)}, f32[1,1152]{1,0:T(1,128)S(1)}, u32[]{:S(2)}, u32[]{:S(2)}) collective-permute-start(f32[1,1152]{1,0:T(1,128)S(1)} %broadcast_in_dim.16), channel_id=1, source_target_pairs={{0,32},{32,0},{1,33},{33,1},{2,34},{34,2},{3,35},{35,3},{4,36},{36... | collective-permute-start | bytes 13832 | tf_op jit(solution)/shard_map/ppermute | solution.py:393
  168.9 1.8 collective-permute-start.22
  170.7 0.7 copy-start.13
  175.3 56.6 %all-to-all-start.1 = ((bf16[64,3,8,1152]{3,2,1,0:T(8,128)(2,1)}), bf16[64,3,8,1152]{3,2,1,0:T(8,128)(2,1)}, u32[]{:S(2)}, u32[]{:S(2)}) async-start(bf16[64,3,8,1152]{3,2,1,0:T(8,128)(2,1)} %fill_rest.1), calls=%async_computation.1 | async-start | bytes 7077888 | tf_op jit(solution)/shard_map/all_to_all | solution.py:401

commit v4 on v2

--- a/solution.py
+++ b/solution.py
@@ -18,6 +18,25 @@
 
 def dot(a, b, ca, cb):
     return lax.dot_general(a, b, (((ca,), (cb,)), ((), ())), preferred_element_type=F32)
+
+
+def copies_kernel(g_ref, out, sems):
+    copies = [pltpu.make_async_copy(g_ref, out.at[i], sems.at[i]) for i in range(32)]
+    for copy in copies:
+        copy.start()
+    for copy in copies:
+        copy.wait()
+
+
+def copies_of(guide):
+    return pl.pallas_call(
+        copies_kernel,
+        in_specs=[pl.BlockSpec(memory_space=pltpu.VMEM)],
+        out_specs=pl.BlockSpec(memory_space=pl.ANY),
+        out_shape=jax.ShapeDtypeStruct((32, *guide.shape), guide.dtype),
+        scratch_shapes=[pltpu.SemaphoreType.DMA((32,))],
+        name="copies_of_guide",
+    )(guide)
 
 
 def attention_kernel(
@@ -108,8 +127,13 @@
     return (want == lax.broadcasted_iota(jnp.int32, (want.shape[0], width), 1)).astype(BF16)
 
 
+EARLY = 640
+SLOTS = [(row, lane) for lane in range(EARLY, D, 128) for row in range(8)]
+GAINS = SLOTS[18:] + [(row, 512) for row in range(1, 5)]
+
+
 def weight_parts_kernel(
-    want_ref, hid_ref, o_ref, o2_ref, dq_ref, dq2_ref, g_ref, g2_ref, send_ref, ninth_ref
+    want_ref, hid_ref, o_ref, o2_ref, dq_ref, dq2_ref, g_ref, g2_ref, gain_ref, send_ref, scr
 ):
     o = jnp.concatenate([o_ref[...], o2_ref[...]], axis=0)
     dq = jnp.concatenate([dq_ref[...], dq2_ref[...]], axis=0)
@@ -118,39 +142,58 @@
     parts = (dot(hid_ref[...], dq, 1, 0), dot(o_rows, g, 1, 0))
     for m, part in enumerate(parts):
         send_ref[:, m] = part[:512].reshape(64, 8, D).astype(BF16)
-        ninth_ref[:, m * D : (m + 1) * D] = part[512:]
+        for b in range(9):
+            row, lane = SLOTS[9 * m + b]
+            at = lane - EARLY
+            scr[:, row, at : at + 128] = part[512:, 128 * b : 128 * b + 128]
+    for b in range(14):
+        row, lane = GAINS[b]
+        at = lane - EARLY
+        block = gain_ref[:, 128 * b : 128 * b + 128]
+        scr[:, row, at : at + 128] = jnp.broadcast_to(block, (64, 128))
+    send_ref[:, 2, :, EARLY:] = scr[...].astype(BF16)
 
 
 def weight_parts(*args):
     vmem = pl.BlockSpec(memory_space=pltpu.VMEM)
     return pl.pallas_call(
         weight_parts_kernel,
-        grid=(1,),
-        in_specs=[vmem] * 8,
-        out_specs=[
-            pl.BlockSpec((64, 2, 8, D), lambda i: (0, 0, 0, 0)),
-            pl.BlockSpec((64, 2 * D), lambda i: (0, 0)),
-        ],
-        out_shape=[
-            jax.ShapeDtypeStruct((64, 3, 8, D), BF16),
-            jax.ShapeDtypeStruct((64, 2 * D), F32),
-        ],
+        in_specs=[vmem] * 9,
+        out_specs=vmem,
+        out_shape=jax.ShapeDtypeStruct((64, 3, 8, D), BF16),
+        scratch_shapes=[pltpu.VMEM((64, 8, D - EARLY), F32)],
         name="weight_parts",
     )(*args)
 
 
-def image_sums_kernel(core_ref, got_ref, g_ref, mine_ref, theirs_ref, tok_ref, scr):
-    def add(s, sums):
-        terms = got_ref[s].astype(F32)
-        first = terms[:, 36:37, :] == 0.0
-        zero = jnp.zeros_like(terms)
-        return sums[0] + jnp.where(first, terms, zero), sums[1] + jnp.where(first, zero, terms)
-
-    zero = jnp.zeros((2, 40, G), F32)
-    sums = lax.fori_loop(0, 32, add, (zero, zero))
-    rounded = [x.reshape(80, G).astype(BF16) for x in sums]
-    prod = dot(rounded[0], g_ref[:, 0].reshape(G, D), 1, 0)
-    prod = prod + dot(rounded[1], g_ref[:, 1].reshape(G, D), 1, 0)
+def image_sums_kernel(core_ref, got_hbm, g_hbm, mine_ref, theirs_ref, tok_ref, scr, got, guide, sems):
+    loads = []
+    for n in range(2):
+        for part in range(2):
+            some = pl.ds(16 * part, 16)
+            sem = sems.at[2 * n + part]
+            loads.append(pltpu.make_async_copy(got_hbm.at[some, n], got.at[n, some], sem))
+    last = pltpu.make_async_copy(g_hbm, guide, sems.at[4])
+    for copy in loads + [last]:
+        copy.start()
+    zero = jnp.zeros((40, G), F32)
+    sums = [None, None]
+    for n in range(2):
+
+        def add(s, pair, n=n):
+            terms = got[n, s].astype(F32)
+            first = terms[36:37, :] == 0.0
+            return pair[0] + jnp.where(first, terms, zero), pair[1] + jnp.where(first, zero, terms)
+
+        pair = (zero, zero)
+        for part in range(2):
+            loads[2 * n + part].wait()
+            pair = lax.fori_loop(16 * part, 16 * part + 16, add, pair)
+        sums[n] = pair
+    rounded = [jnp.concatenate([sums[0][m], sums[1][m]], axis=0).astype(BF16) for m in range(2)]
+    last.wait()
+    prod = dot(rounded[0], guide[:, 0].reshape(G, D), 1, 0)
+    prod = prod + dot(rounded[1], guide[:, 1].reshape(G, D), 1, 0)
     scr[...] = jnp.concatenate([prod, jnp.zeros((48, D), F32)], axis=0).T
     core = core_ref[0]
     for n in range(2):
@@ -163,114 +206,118 @@
 
 def image_sums(core, got, whole):
     vmem = pl.BlockSpec(memory_space=pltpu.VMEM)
+    hbm = pl.BlockSpec(memory_space=pl.ANY)
     return pl.pallas_call(
         image_sums_kernel,
-        in_specs=[pl.BlockSpec(memory_space=pltpu.SMEM), vmem, vmem],
+        in_specs=[pl.BlockSpec(memory_space=pltpu.SMEM), hbm, hbm],
         out_specs=[vmem] * 3,
         out_shape=[
             jax.ShapeDtypeStruct((ROWS, 128), F32),
             jax.ShapeDtypeStruct((ROWS, 128), F32),
             jax.ShapeDtypeStruct((G, 256), F32),
         ],
-        scratch_shapes=[pltpu.VMEM((D, 128), F32)],
+        scratch_shapes=[
+            pltpu.VMEM((D, 128), F32),
+            pltpu.VMEM((2, 32, 40, G), BF16),
+            pltpu.VMEM((32, 2, 16, D), BF16),
+            pltpu.SemaphoreType.DMA((5,)),
+        ],
         name="image_sums",
     )(core, got, whole)
 
 
-SLOTS = [(row, lane) for lane in range(512, D, 128) for row in range(8)]
-
-
-def fill_rest_kernel(send_ref, mine_ref, got_ref, tok_ref, ninth_ref, gain_ref, out_ref, scr):
-    scr[:, :, 384:512] = jnp.zeros((64, 8, 128), F32)
+def fill_rest_kernel(send_ref, mine_ref, got_ref, tok_ref, gain_ref, out_ref, scr):
+    scr[:, :, 512:EARLY] = jnp.zeros((64, 8, EARLY - 512), F32)
     total = mine_ref[...] + got_ref[...]
     high = total.astype(BF16)
     low = (total - high.astype(F32)).astype(BF16)
     want = eight_and_one(lax.broadcasted_iota(jnp.int32, (ROWS, ROWS), 0))
     order = (want == lax.broadcasted_iota(jnp.int32, (ROWS, ROWS), 1)).astype(BF16)
-    moved = [dot(order, x, 1, 0) for x in (high, low)]
+    moved = dot(order, jnp.concatenate([high, low], axis=1), 1, 0)
     tok = tok_ref[...].reshape(32, 16, 256)
+    for half in range(2):
+        lanes = slice(160 * half + 160, 160 * half + 320)
+        for n in range(2):
+            scr[32 * n : 32 * n + 32, :, lanes] = tok[:, 8 * half : 8 * half + 8, :160]
     for n in range(2):
-        scr[:, :, 80 * n : 80 * n + 80] = moved[n][:512].reshape(64, 8, 128)[:, :, :80]
-        for half in range(2):
-            lanes = slice(160 * half + 160, 160 * half + 320)
-            scr[32 * n : 32 * n + 32, :, lanes] = tok[:, 8 * half : 8 * half + 8, :160]
-    gain = gain_ref[...]
-    gain_high = gain.astype(BF16).astype(F32)
-    gains = jnp.concatenate([gain_high, gain - gain_high], axis=1)
-    for b, (row, lane) in enumerate(SLOTS):
-        if b < 18:
-            block = ninth_ref[:, 128 * b : 128 * b + 128]
-        elif b < 20:
-            block = moved[b - 18][512:]
-        elif b < 38:
-            block = jnp.broadcast_to(gains[:, 128 * (b - 20) : 128 * (b - 20) + 128], (64, 128))
-        else:
-            block = jnp.zeros((64, 128), F32)
-        scr[:, row, lane : lane + 128] = block
+        piece = moved[:, 128 * n : 128 * n + 80]
+        scr[:, :, 80 * n : 80 * n + 80] = piece[:512].reshape(64, 8, 80)
+        scr[:, 0, 480 + 80 * n : 560 + 80 * n] = piece[512:]
+    for b in range(14, 18):
+        row, lane = GAINS[b]
+        block = gain_ref[:, 128 * b : 128 * b + 128]
+        scr[:, row, lane : lane + 128] = jnp.broadcast_to(block, (64, 128))
     out_ref[:, 0] = scr[...].astype(BF16)
 
 
-def fill_rest(send, mine, got, tok, ninth, gain):
+def fill_rest(send, mine, got, tok, gain):
     vmem = pl.BlockSpec(memory_space=pltpu.VMEM)
     return pl.pallas_call(
         fill_rest_kernel,
         grid=(1,),
-        in_specs=[pl.BlockSpec(memory_space=pl.ANY)] + [vmem] * 5,
-        out_specs=pl.BlockSpec((64, 1, 8, D), lambda i: (0, 2, 0, 0)),
+        in_specs=[pl.BlockSpec(memory_space=pl.ANY)] + [vmem] * 4,
+        out_specs=pl.BlockSpec((64, 1, 8, EARLY), lambda i: (0, 2, 0, 0)),
         out_shape=jax.ShapeDtypeStruct((64, 3, 8, D), BF16),
-        scratch_shapes=[pltpu.VMEM((64, 8, D), F32)],
+        scratch_shapes=[pltpu.VMEM((64, 8, EARLY), F32)],
         input_output_aliases={0: 0},
         name="fill_rest",
-    )(send, mine, got, tok, ninth, gain)
-
-
-def finish_kernel(yl_ref, recv_ref, wk_hbm, wv_hbm, gw_ref, gg_ref, gain_ref, scr, wk, wv, sems):
-    copies = [
-        pltpu.make_async_copy(wk_hbm, wk, sems.at[0]),
-        pltpu.make_async_copy(wv_hbm, wv, sems.at[1]),
+    )(send, mine, got, tok, gain)
+
+
+def finish_kernel(
+    yl_ref, recv_hbm, wk_hbm, wv_hbm, gw_ref, gg_ref, gain_ref, tok, kv, recv, wk, wv, sems
+):
+    loads = []
+    for part in range(4):
+        some = pl.ds(16 * part, 16)
+        loads.append(pltpu.make_async_copy(recv_hbm.at[some], recv.at[some], sems.at[part]))
+    late = [
+        pltpu.make_async_copy(wk_hbm, wk, sems.at[4]),
+        pltpu.make_async_copy(wv_hbm, wv, sems.at[5]),
     ]
-    for copy in copies:
+    for copy in loads + late:
         copy.start()
 
     def add(j, sums):
-        return tuple(s + recv_ref[j, n].astype(F32) for n, s in enumerate(sums))
-
-    sums = lax.fori_loop(0, 64, add, tuple(jnp.zeros((8, D), F32) for _ in range(3)))
+        return tuple(s + recv[j, n].astype(F32) for n, s in enumerate(sums))
+
+    sums = tuple(jnp.zeros((8, D), F32) for _ in range(3))
+    for part in range(4):
+        loads[part].wait()
+        sums = lax.fori_loop(16 * part, 16 * part + 16, add, sums)
     gw_ref[:8, 0] = sums[0]
     gw_ref[:8, 3] = sums[1]
 
-    def slot(b):
-        row, lane = SLOTS[b]
+    def slot(place):
+        row, lane = place
         return sums[2][row : row + 1, lane : lane + 128]
 
     for b in range(18):
         at = 128 * (b % 9)
-        gw_ref[8:9, 3 * (b // 9), at : at + 128] = slot(b)
+        gw_ref[8:9, 3 * (b // 9), at : at + 128] = slot(SLOTS[b])
     for b in range(9):
-        gain_ref[b : b + 1] = slot(20 + b) + slot(29 + b)
+        gain_ref[b : b + 1] = slot(GAINS[b]) + slot(GAINS[9 + b])
     base = yl_ref[0] * 32
-    nines = [SLOTS[18], SLOTS[19]]
     for t in range(32):
         cols = slice(36 * t, 36 * t + 36)
-        x = recv_ref[t, 2, :, :256].astype(F32) + recv_ref[32 + t, 2, :, :256].astype(F32)
+        x = recv[t, 2, :, :EARLY].astype(F32) + recv[32 + t, 2, :, :EARLY].astype(F32)
         eight = x[:, :80] + x[:, 80:160]
-        one = jnp.zeros((1, 128), F32)
-        for row, lane in nines:
-            for j in (t, 32 + t):
-                one = one + recv_ref[j, 2, :, lane : lane + 128].astype(F32)[row : row + 1]
+        one = x[:1, 480:560] + x[:1, 560:640]
+        near = recv[base + t, 2, :, 128:512].astype(F32)
         for n in range(2):
-            gw_ref[:8, 1 + n, cols] = eight[:, 40 * n : 40 * n + 36]
-            gw_ref[8:9, 1 + n, cols] = one[:, 40 * n : 40 * n + 36]
-        near = recv_ref[base + t, 2, :, 128:512].astype(F32)
-        for half in range(2):
-            for m in range(2):
-                for n in range(2):
+            kv[n, :8, cols] = eight[:, 40 * n : 40 * n + 36]
+            kv[n, 8:9, cols] = one[:, 40 * n : 40 * n + 36]
+            for half in range(2):
+                for m in range(2):
                     lane = 32 + 160 * half + 80 * m + 40 * n
                     row = 16 * m + 8 * half
-                    scr[n, row : row + 8, cols] = near[:, lane : lane + 36]
-    for copy in copies:
+                    tok[n, row : row + 8, cols] = near[:, lane : lane + 36]
+    for n in range(2):
+        gw_ref[:8, 1 + n] = kv[n, :8]
+        gw_ref[8:9, 1 + n] = kv[n, 8:9]
+    for copy in late:
         copy.wait()
-    grad = dot(scr[0].astype(BF16), wk[...], 1, 1) + dot(scr[1].astype(BF16), wv[...], 1, 1)
+    grad = dot(tok[0].astype(BF16), wk[...], 1, 1) + dot(tok[1].astype(BF16), wv[...], 1, 1)
     gg_ref[...] = grad.astype(BF16)
 
 
@@ -279,7 +326,7 @@
     hbm = pl.BlockSpec(memory_space=pl.ANY)
     return pl.pallas_call(
         finish_kernel,
-        in_specs=[pl.BlockSpec(memory_space=pltpu.SMEM), vmem, hbm, hbm],
+        in_specs=[pl.BlockSpec(memory_space=pltpu.SMEM), hbm, hbm, hbm],
         out_specs=[vmem] * 3,
         out_shape=[
             jax.ShapeDtypeStruct((9, 4, D), F32),
@@ -288,9 +335,11 @@
         ],
         scratch_shapes=[
             pltpu.VMEM((2, 32, D), F32),
+            pltpu.VMEM((2, 16, D), F32),
+            pltpu.VMEM((64, 3, 8, D), BF16),
             pltpu.VMEM((D, D), BF16),
             pltpu.VMEM((D, D), BF16),
-            pltpu.SemaphoreType.DMA((2,)),
+            pltpu.SemaphoreType.DMA((6,)),
         ],
         name="finish",
     )(yl, recv, w_key, w_value)
@@ -299,9 +348,7 @@
 def on_device(tiles, tile_image, guide, gain, w_query, w_key, w_value, w_out, grad_out):
     core = lax.axis_index("c")
     yl = lax.axis_index("yl")
-    whole = lax.all_to_all(
-        jnp.broadcast_to(guide, (32, *guide.shape)), TILE_AXES, 0, 0, tiled=True
-    )
+    whole = lax.all_to_all(copies_of(guide), TILE_AXES, 0, 0, tiled=True)
     xf = tiles.astype(F32)
     rstd = lax.rsqrt(jnp.mean(xf * xf, axis=-1, keepdims=True) + 1e-06)
     normed = xf * rstd
@@ -319,16 +366,20 @@
 
     dq_got = lax.ppermute(dq, "c", SWAP)
     out_got = lax.ppermute(outv, "c", SWAP)
-    send, ninth = weight_parts(want, hid_rows, outv, out_got, dq, dq_got, grad_out, grad_got)
     dh = dot(dq, w_query, 1, 1)
     gain_part = jnp.sum(dh * normed, axis=0, keepdims=True)
     gain_part = gain_part + lax.ppermute(gain_part, "c", SWAP)
+    gain_high = lax.reduce_precision(gain_part, 8, 7)
+    gains = jnp.concatenate([gain_high, gain_part - gain_high], axis=1)
+    send = weight_parts(
+        want, hid_rows, outv, out_got, dq, dq_got, grad_out, grad_got, gains
+    )
     dn = dh * gain
     grad_tiles = (rstd * (dn - normed * jnp.mean(dn * normed, axis=-1, keepdims=True))).astype(BF16)
 
-    got, ninth, gain_part = lax.optimization_barrier((got, ninth, gain_part))
+    got, send = lax.optimization_barrier((got, send))
     mine, theirs, tok = image_sums(core[None], got, whole)
-    send = fill_rest(send, mine, lax.ppermute(theirs, "c", SWAP), tok, ninth, gain_part)
+    send = fill_rest(send, mine, lax.ppermute(theirs, "c", SWAP), tok, gains)
     recv = lax.all_to_all(send, CHIP_AXES, 0, 0, tiled=True)
     grad_weights, grad_guide, grad_gain = finish(yl[None], recv, w_key, w_value)
     grad_weights = grad_weights.transpose(1, 0, 2)

time: 186 us -> 182 us (0.978)
    pallas_call x1 -> x2, Pallas kernels: 6.33 us -> 9.69 us  [the longest x1 6.94 us: weight_parts(): pl.pallas_call(weight_parts_kernel, in_specs=[vmem] * 9, out_specs=vmem,...]
    all_to_all x1, waiting for transfers between devices: 20.8 us -> 17.6 us  [on_device(): got = lax.all_to_all(pay, TILE_AXES, 0, 0, tiled=True)]
    broadcast_in_dim x1 -> x0, local copies, waits for them, and re-layouts: 2.63 us -> none  [on_device(): jnp.broadcast_to(guide, (32, *guide.shape))]
  transfers between devices with their start and end apart: 9 -> 9, of which waited for: 4 -> 5; matrix products, arithmetic and copies ran while one was open for 9% -> 9% of each run, Pallas kernels for 3% -> 4%
where the time goes in v4:
time: 182 us; the launch traced here: 180 us
  waiting for transfers between devices  85 us (47%)
  Pallas kernels  45.4 us (25%)
  starting transfers between devices  30 us (16%)
  matrix products  11.2 us (6%)
  other arithmetic  5.33 us (3%)
    all_to_all x1, waiting for transfers between devices, on_device(): recv = lax.all_to_all(send, CHIP_AXES, 0, 0, tiled=True)  43.8 us
    pallas_call x1, Pallas kernels, attention(): pl.pallas_call(attention_kernel, in_specs=[pl.BlockSpec(memory_space=pltp...  21.6 us
    all_to_all x1, waiting for transfers between devices, on_device(): whole = lax.all_to_all(copies_of(guide), TILE_AXES, 0, 0, tiled=True)  20.1 us
    all_to_all x1, waiting for transfers between devices, on_device(): got = lax.all_to_all(pay, TILE_AXES, 0, 0, tiled=True)  17.6 us
    all_to_all x1, starting transfers between devices, on_device(): whole = lax.all_to_all(copies_of(guide), TILE_AXES, 0, 0, tiled=True)  11.3 us
    dot_general x4, matrix products, dot(): lax.dot_general(a, b, (((ca,), (cb,)), ((), ())), preferred_element_type=...  11.2 us
    all_to_all x1, starting transfers between devices, on_device(): recv = lax.all_to_all(send, CHIP_AXES, 0, 0, tiled=True)  9.14 us
    all_to_all x1, starting transfers between devices, on_device(): got = lax.all_to_all(pay, TILE_AXES, 0, 0, tiled=True)  8.37 us
  transfers between devices with their start and end apart: 9, of which 5 were waited for; matrix products, arithmetic and copies ran while one was open for 9% of the time, Pallas kernels for 4%

profile of v4, /device:TPU:2, one launch (start us, length us, event | category | flops | bytes accessed | tf_op | source)
XLA Modules:
  0.0 180.1 jit_solution(14181393435164730842)
XLA Ops:
  0.6 0.0 copy-start
  0.6 2.7 %copies_of_guide.1 = bf16[32,2,16,1152]{3,2,1,0:T(8,128)(2,1)} custom-call(bf16[2,16,1152]{2,1,0:T(8,128)(2,1)} %g_ref.2), custom_call_target="tpu_custom_call" | custom-call | tf_op jit(solution)/shard_map/copies_of_guide/pallas_call | solution.py:32
  3.4 0.0 copy-start.1
  3.4 0.0 copy-start.8
  3.4 11.3 %all-to-all-start = ((bf16[32,2,16,1152]{3,2,1,0:T(8,128)(2,1)}), bf16[32,2,16,1152]{3,2,1,0:T(8,128)(2,1)}, u32[]{:S(2)}, u32[]{:S(2)}) async-start(bf16[32,2,16,1152]{3,2,1,0:T(8,128)(2,1)} %copies_of_guide.1), calls=%async_computation | async-start | bytes 4718592 | tf_op jit(solution)/shard_map/all_to_all | solution.py:351
  14.7 0.0 copy-done.1
  14.7 0.2 fusion.13
  14.9 0.0 copy-done.8
  14.9 1.0 fusion.7
  16.0 0.0 collective-permute-start
  16.6 0.0 copy-done
  16.7 0.0 copy-start.2
  16.7 0.0 copy-start.9
  16.7 3.0 %convolution_convert_fusion.1.q_ref = bf16[256,1152]{1,0:T(8,128)(2,1)} fusion(bf16[256,1152]{1,0:T(8,128)(2,1)} %fusion.7, bf16[1152,1152]{1,0:T(8,128)(2,1)S(1)} %copy-done), kind=kOutput, calls=%fused_computation.3 | convolution fusion | flops 679772160 | bytes 3833856 | tf_op jit(solution)/shard_map/dot_general | solution.py:20
  19.7 0.0 copy-done.2
  19.7 0.0 copy-done.9
  19.7 1.9 %convolution_convert_fusion.d_ref = bf16[256,1152]{1,0:T(8,128)(2,1)} fusion(bf16[256,1152]{1,0:T(8,128)(2,1)S(1)} %copy-done.2, bf16[1152,1152]{1,0:T(8,128)(2,1)S(1)} %copy-done.9), kind=kOutput, calls=%fused_computation.2 | convolution fusion | flops 679772160 | bytes 3833856 | tf_op jit(solution)/shard_map/dot_general | solution.py:20
  21.6 0.0 collective-permute-done
  21.6 3.1 %fusion.6.hid_ref = bf16[576,512]{1,0:T(8,128)(2,1)} fusion(s32[576]{0:T(1024)S(1)} %fusion.44, bf16[256,1152]{1,0:T(8,128)(2,1)} %collective-permute-done, bf16[256,1152]{1,0:T(8,128)(2,1)} %fusion.7), kind=kOutput, calls=%fused_computation.11 | convolution fusion | flops 682795008 | bytes 1771776 | tf_op jit(solution)/shard_map/dot_general | solution.py:20
  24.7 20.1 %all-to-all-done.g_hbm = bf16[32,2,16,1152]{3,2,1,0:T(8,128)(2,1)} async-done(((bf16[32,2,16,1152]{3,2,1,0:T(8,128)(2,1)}), bf16[32,2,16,1152]{3,2,1,0:T(8,128)(2,1)}, u32[]{:S(2)}, u32[]{:S(2)}) %all-to-all-start) | async-done | bytes 2359328 | tf_op jit(solution)/shard_map/all_to_all | solution.py:351
  44.8 21.6 %attention.1 = (bf16[32,2,40,512]{3,2,1,0:T(8,128)(2,1)}, bf16[256,1152]{1,0:T(8,128)(2,1)}, bf16[256,1152]{1,0:T(8,128)(2,1)}) custom-call(s32[1]{0:T(128)S(6)} %copy.15.img_ref, bf16[32,2,16,1152]{3,2,1,0:T(8,128)(2,1)} %all-to-all-done.g_hbm, bf16[1152,1152]{1,0:T(8,128)(2,1)} %wk_hbm.3, bf16[1152,1152]{1,0:T(8,128)(2,1)} %wv_hbm.3, ...), custom_call_target="tpu_custom_call" | custom-call | tf_op jit(solution)/shard_map/attention/pallas_call | solution.py:91
  66.4 8.4 %all-to-all-start.1 = ((bf16[32,2,40,512]{3,2,1,0:T(8,128)(2,1)}), bf16[32,2,40,512]{3,2,1,0:T(8,128)(2,1)}, u32[]{:S(2)}, u32[]{:S(2)}) async-start(bf16[32,2,40,512]{3,2,1,0:T(8,128)(2,1)} %get-tuple-element.19), calls=%async_computation.1 | async-start | bytes 5242880 | tf_op jit(solution)/shard_map/all_to_all | solution.py:365
  74.8 0.1 collective-permute-start.3
  74.9 0.0 copy-start.4
  74.9 0.0 copy-start.3
  74.9 3.2 %fusion.12 = (f32[1152]{0:T(1024)S(1)}, f32[256]{0:T(256)S(1)}, f32[256,1152]{1,0:T(8,128)}) fusion(bf16[256,1152]{1,0:T(8,128)(2,1)S(1)} %copy-done.1, f32[256]{0:T(256)S(1)} %add_rsqrt_fusion, f32[1152]{0:T(1024)S(1)} %copy-done.8, bf16[256,1152]{1,0:T(8,128)(2,1)} %get-tuple-element.18.dq_ref, bf16[1152,1152]{1,0:T(8,128)(2,1)S(1)} %copy-done), kind=kOutput, calls=%fused_computation.17 | convolution fusion | flops 681540224 | bytes 5024768 | tf_op jit(solution)/shard_map/dot_general | solution.py:20
  78.1 0.5 collective-permute-start.4
  78.6 1.1 fusion.28.want_ref
  79.7 0.0 copy-done.4
  79.7 0.0 collective-permute-start.2
  79.7 0.0 copy-done.3
  79.7 0.5 collective-permute-start.1
  80.2 0.0 collective-permute-done.4
  80.2 0.6 pad_maximum_fusion.gain_ref
  80.8 0.0 collective-permute-done.3.g2_ref
  80.8 0.0 copy-start.5
  80.8 1.7 collective-permute-done.1.o2_ref
  82.5 0.0 copy-done.5
  82.5 0.0 copy-start.6
  82.5 0.8 copy-done.6
  83.3 0.0 collective-permute-done.2.dq2_ref
  83.3 6.9 %weight_parts.1.send_ref = bf16[64,3,8,1152]{3,2,1,0:T(8,128)(2,1)} custom-call(s32[576,1]{1,0:T(8,128)} %fusion.28.want_ref, bf16[576,512]{1,0:T(8,128)(2,1)} %fusion.6.hid_ref, bf16[256,1152]{1,0:T(8,128)(2,1)} %get-tuple-element.21.o_ref, bf16[256,1152]{1,0:T(8,128)(2,1)} %copy-done.6, bf16[256,1152]{1,0:T(8,128)(2,1)} %get-tuple-element.18.dq_ref, ...), custom_call_target="tpu_custom_call" | custom-call | tf_op jit(solution)/shard_map/weight_parts/pallas_call | solution.py:159
  90.3 17.6 %all-to-all-done.1.got_hbm = bf16[32,2,40,512]{3,2,1,0:T(8,128)(2,1)} async-done(((bf16[32,2,40,512]{3,2,1,0:T(8,128)(2,1)}), bf16[32,2,40,512]{3,2,1,0:T(8,128)(2,1)}, u32[]{:S(2)}, u32[]{:S(2)}) %all-to-all-start.1) | async-done | bytes 2621472 | tf_op jit(solution)/shard_map/all_to_all | solution.py:365
  107.8 4.6 %image_sums.1 = (f32[576,128]{1,0:T(8,128)}, f32[576,128]{1,0:T(8,128)}, f32[512,256]{1,0:T(8,128)}) custom-call(s32[1]{0:T(128)} %bitcast.1.core_ref, bf16[32,2,40,512]{3,2,1,0:T(8,128)(2,1)} %all-to-all-done.1.got_hbm, bf16[32,2,16,1152]{3,2,1,0:T(8,128)(2,1)} %all-to-all-done.g_hbm), custom_call_target="tpu_custom_call" | custom-call | tf_op jit(solution)/shard_map/image_sums/pallas_call | solution.py:210
  112.5 0.1 collective-permute-start.5
  112.6 1.8 collective-permute-done.5.got_ref
  114.3 0.0 copy-start.7
  114.3 0.7 copy-done.7
  115.1 2.9 %fill_rest.1 = bf16[64,3,8,1152]{3,2,1,0:T(8,128)(2,1)} custom-call(bf16[64,3,8,1152]{3,2,1,0:T(8,128)(2,1)} %weight_parts.1.send_ref, f32[576,128]{1,0:T(8,128)} %get-tuple-element.24.mine_ref, f32[576,128]{1,0:T(8,128)} %copy-done.7, f32[512,256]{1,0:T(8,128)} %get-tuple-element.26.tok_ref, ...), custom_call_target="tpu_custom_call", output_to_operand_aliasing={{}: (0, {})} | custom-call | tf_op jit(solution)/shard_map/fill_rest/pallas_call | solution.py:255
  118.0 9.1 %all-to-all-start.2 = ((bf16[64,3,8,1152]{3,2,1,0:T(8,128)(2,1)}), bf16[64,3,8,1152]{3,2,1,0:T(8,128)(2,1)}, u32[]{:S(2)}, u32[]{:S(2)}) async-start(bf16[64,3,8,1152]{3,2,1,0:T(8,128)(2,1)} %fill_rest.1), calls=%async_computation.2 | async-start | bytes 7077888 | tf_op jit(solution)/shard_map/all_to_all | solution.py:383
  127.1 2.4 %fusion.11 = bf16[256,1152]{1,0:T(8,128)(2,1)} fusion(bf16[256,1152]{1,0:T(8,128)(2,1)S(1)} %copy-done.1, f32[256,1152]{1,0:T(8,128)} %get-tuple-element.34, f32[256]{0:T(256)S(1)} %broadcast_multiply_fusion, f32[1152]{0:T(1024)S(1)} %copy-done.8, f32[256]{0:T(256)S(1)} %add_rsqrt_fusion), kind=kLoop, calls=%fused_computation.16 | loop fusion | flops 2064384 | bytes 2365952 | tf_op jit(solution)/shard_map/convert_element_type | solution.py:378
  129.5 43.8 %all-to-all-done.2.recv_hbm = bf16[64,3,8,1152]{3,2,1,0:T(8,128)(2,1)} async-done(((bf16[64,3,8,1152]{3,2,1,0:T(8,128)(2,1)}), bf16[64,3,8,1152]{3,2,1,0:T(8,128)(2,1)}, u32[]{:S(2)}, u32[]{:S(2)}) %all-to-all-start.2) | async-done | bytes 3538976 | tf_op jit(solution)/shard_map/all_to_all | solution.py:383
  173.3 6.7 %finish.1 = (f32[9,4,1152]{2,1,0:T(4,128)}, bf16[32,1152]{1,0:T(8,128)(2,1)}, f32[9,128]{1,0:T(8,128)}) custom-call(s32[1]{0:T(128)} %bitcast.yl_ref, bf16[64,3,8,1152]{3,2,1,0:T(8,128)(2,1)} %all-to-all-done.2.recv_hbm, bf16[1152,1152]{1,0:T(8,128)(2,1)} %wk_hbm.3, bf16[1152,1152]{1,0:T(8,128)(2,1)} %wv_hbm.3), custom_call_target="tpu_custom_call" | custom-call | tf_op jit(solution)/shard_map/finish/pallas_call | solution.py:327
  (5 shorter events, 0.0 us)
Async XLA Ops:
  0.6 16.0 %copy-start = (bf16[1152,1152]{1,0:T(8,128)(2,1)S(1)}, bf16[1152,1152]{1,0:T(8,128)(2,1)}, u32[]{:S(2)}) copy-start(bf16[1152,1152]{1,0:T(8,128)(2,1)} %param.13) | copy-start | bytes 7962628
  3.4 11.3 %copy-start.1 = (bf16[256,1152]{1,0:T(8,128)(2,1)S(1)}, bf16[256,1152]{1,0:T(8,128)(2,1)}, u32[]{:S(2)}) copy-start(bf16[256,1152]{1,0:T(8,128)(2,1)} %param.9) | copy-start | bytes 1769476
  3.4 11.5 %copy-start.8 = (f32[1152]{0:T(1024)S(1)}, f32[1152]{0:T(1024)}, u32[]{:S(2)}) copy-start(f32[1152]{0:T(1024)} %param.12) | copy-start | bytes 13828
  3.4 41.4 %all-to-all-start = ((bf16[32,2,16,1152]{3,2,1,0:T(8,128)(2,1)}), bf16[32,2,16,1152]{3,2,1,0:T(8,128)(2,1)}, u32[]{:S(2)}, u32[]{:S(2)}) async-start(bf16[32,2,16,1152]{3,2,1,0:T(8,128)(2,1)} %copies_of_guide.1), calls=%async_computation | async-start | bytes 4718592 | tf_op jit(solution)/shard_map/all_to_all | solution.py:351
  16.0 5.6 %collective-permute-start = (bf16[256,1152]{1,0:T(8,128)(2,1)}, bf16[256,1152]{1,0:T(8,128)(2,1)}, u32[]{:S(2)}, u32[]{:S(2)}) collective-permute-start(bf16[256,1152]{1,0:T(8,128)(2,1)} %fusion.7), channel_id=1, source_target_pairs={{0,32},{32,0},{1,33},{33,1},{2,34},{34,2},{3,35},{35,3},{4,36},{36... | collective-permute-start | bytes 1769480 | tf_op jit(solution)/shard_map/ppermute | solution.py:359
  16.7 3.1 %copy-start.2 = (bf16[256,1152]{1,0:T(8,128)(2,1)S(1)}, bf16[256,1152]{1,0:T(8,128)(2,1)}, u32[]{:S(2)}) copy-start(bf16[256,1152]{1,0:T(8,128)(2,1)} %g_ref.3) | copy-start | bytes 1769476
  16.7 3.1 %copy-start.9 = (bf16[1152,1152]{1,0:T(8,128)(2,1)S(1)}, bf16[1152,1152]{1,0:T(8,128)(2,1)}, u32[]{:S(2)}) copy-start(bf16[1152,1152]{1,0:T(8,128)(2,1)} %param.16) | copy-start | bytes 7962628
  66.4 41.5 %all-to-all-start.1 = ((bf16[32,2,40,512]{3,2,1,0:T(8,128)(2,1)}), bf16[32,2,40,512]{3,2,1,0:T(8,128)(2,1)}, u32[]{:S(2)}, u32[]{:S(2)}) async-start(bf16[32,2,40,512]{3,2,1,0:T(8,128)(2,1)} %get-tuple-element.19), calls=%async_computation.1 | async-start | bytes 5242880 | tf_op jit(solution)/shard_map/all_to_all | solution.py:365
  74.8 6.0 %collective-permute-start.3 = (bf16[256,1152]{1,0:T(8,128)(2,1)}, bf16[256,1152]{1,0:T(8,128)(2,1)S(1)}, u32[]{:S(2)}, u32[]{:S(2)}) collective-permute-start(bf16[256,1152]{1,0:T(8,128)(2,1)} %g_ref.3), channel_id=1, source_target_pairs={{0,32},{32,0},{1,33},{33,1},{2,34},{34,2},{3,35},{35,3},{4,36},{36... | collective-permute-start | bytes 1769480 | tf_op jit(solution)/shard_map/ppermute | solution.py:361
  74.9 4.8 %copy-start.4 = (bf16[256,1152]{1,0:T(8,128)(2,1)S(1)}, bf16[256,1152]{1,0:T(8,128)(2,1)}, u32[]{:S(2)}) copy-start(bf16[256,1152]{1,0:T(8,128)(2,1)} %get-tuple-element.18.dq_ref) | copy-start | bytes 1769476
  74.9 4.8 %copy-start.3 = (bf16[256,1152]{1,0:T(8,128)(2,1)S(1)}, bf16[256,1152]{1,0:T(8,128)(2,1)}, u32[]{:S(2)}) copy-start(bf16[256,1152]{1,0:T(8,128)(2,1)} %get-tuple-element.21.o_ref) | copy-start | bytes 1769476
  78.1 2.1 %collective-permute-start.4 = (f32[1,1152]{1,0:T(1,128)S(1)}, f32[1,1152]{1,0:T(1,128)S(1)}, u32[]{:S(2)}, u32[]{:S(2)}) collective-permute-start(f32[1,1152]{1,0:T(1,128)S(1)} %broadcast_in_dim.7), channel_id=1, source_target_pairs={{0,32},{32,0},{1,33},{33,1},{2,34},{34,2},{3,35},{35,3},{4,36},{36... | collective-permute-start | bytes 13832 | tf_op jit(solution)/shard_map/ppermute | solution.py:371
  79.7 3.7 %collective-permute-start.2 = (bf16[256,1152]{1,0:T(8,128)(2,1)S(1)}, bf16[256,1152]{1,0:T(8,128)(2,1)}, u32[]{:S(2)}, u32[]{:S(2)}) collective-permute-start(bf16[256,1152]{1,0:T(8,128)(2,1)S(1)} %copy-done.4), channel_id=1, source_target_pairs={{0,32},{32,0},{1,33},{33,1},{2,34},{34,2},{3,35},{35,3},{4,36},{36... | collective-permute-start | bytes 1769480 | tf_op jit(solution)/shard_map/ppermute | solution.py:367
  79.7 2.8 %collective-permute-start.1 = (bf16[256,1152]{1,0:T(8,128)(2,1)S(1)}, bf16[256,1152]{1,0:T(8,128)(2,1)S(1)}, u32[]{:S(2)}, u32[]{:S(2)}) collective-permute-start(bf16[256,1152]{1,0:T(8,128)(2,1)S(1)} %copy-done.3), channel_id=1, source_target_pairs={{0,32},{32,0},{1,33},{33,1},{2,34},{34,2},{3,35},{35,3},{4,36},{36... | collective-permute-start | bytes 1769480 | tf_op jit(solution)/shard_map/ppermute | solution.py:368
  80.8 1.7 copy-start.5
  82.5 0.8 copy-start.6
  112.5 1.9 %collective-permute-start.5 = (f32[576,128]{1,0:T(8,128)}, f32[576,128]{1,0:T(8,128)S(1)}, u32[]{:S(2)}, u32[]{:S(2)}) collective-permute-start(f32[576,128]{1,0:T(8,128)} %get-tuple-element.25), channel_id=1, source_target_pairs={{0,32},{32,0},{1,33},{33,1},{2,34},{34,2},{3,35},{35,3},{4,36},{36... | collective-permute-start | bytes 884744 | tf_op jit(solution)/shard_map/ppermute | solution.py:382
  114.3 0.7 copy-start.7
  118.0 55.4 %all-to-all-start.2 = ((bf16[64,3,8,1152]{3,2,1,0:T(8,128)(2,1)}), bf16[64,3,8,1152]{3,2,1,0:T(8,128)(2,1)}, u32[]{:S(2)}, u32[]{:S(2)}) async-start(bf16[64,3,8,1152]{3,2,1,0:T(8,128)(2,1)} %fill_rest.1), calls=%async_computation.2 | async-start | bytes 7077888 | tf_op jit(solution)/shard_map/all_to_all | solution.py:383

commit v5 on v4

--- a/solution.py
+++ b/solution.py
@@ -20,21 +20,18 @@
     return lax.dot_general(a, b, (((ca,), (cb,)), ((), ())), preferred_element_type=F32)
 
 
-def copies_kernel(g_ref, out, sems):
-    copies = [pltpu.make_async_copy(g_ref, out.at[i], sems.at[i]) for i in range(32)]
-    for copy in copies:
-        copy.start()
-    for copy in copies:
-        copy.wait()
+def copies_kernel(g_ref, out):
+    for i in range(32):
+        out[i] = g_ref[...]
 
 
 def copies_of(guide):
+    vmem = pl.BlockSpec(memory_space=pltpu.VMEM)
     return pl.pallas_call(
         copies_kernel,
-        in_specs=[pl.BlockSpec(memory_space=pltpu.VMEM)],
-        out_specs=pl.BlockSpec(memory_space=pl.ANY),
-        out_shape=jax.ShapeDtypeStruct((32, *guide.shape), guide.dtype),
-        scratch_shapes=[pltpu.SemaphoreType.DMA((32,))],
+        in_specs=[vmem],
+        out_specs=vmem,
+        out_shape=pltpu.VMEM((32, *guide.shape), guide.dtype),
         name="copies_of_guide",
     )(guide)
 
@@ -59,9 +56,20 @@
     scale = HD ** (-0.5)
     flag = jnp.full((4, G), img_ref[0], jnp.int32).astype(F32)
     stores = []
-    for h in range(HEADS):
-        cols = slice(h * HD, (h + 1) * HD)
-        q, d, k, v = q_ref[:, cols], d_ref[:, cols], k_scr[:, cols], v_scr[:, cols]
+    t = q_ref.shape[0]
+    lane = lax.broadcasted_iota(jnp.int32, (t, 2 * HD), 1)
+    none = jnp.zeros((t, 2 * HD), BF16)
+    for h in range(0, HEADS, 2):
+        cols = slice(h * HD, (h + 2) * HD)
+        k, v = k_scr[:, cols], v_scr[:, cols]
+
+        def both(x):
+            return jnp.concatenate([jnp.where(lane < HD, x, none), jnp.where(lane < HD, none, x)], axis=0)
+
+        def own(x):
+            return jnp.where(lane < HD, x[:t], x[t:]).astype(BF16)
+
+        q, d = both(q_ref[:, cols]), both(d_ref[:, cols])
         scores = dot(q, k, 1, 1) * scale
         dprob = dot(d, v, 1, 1)
         top = jnp.max(scores, axis=-1, keepdims=True)
@@ -71,14 +79,14 @@
         weighted = probs * dprob
         delta = jnp.sum(weighted, axis=-1, keepdims=True)
         ds = ((weighted - probs * delta) * scale).astype(BF16)
-        o_ref[:, cols] = dot(pb, v, 1, 0).astype(BF16)
-        dq_ref[:, cols] = dot(ds, k, 1, 0).astype(BF16)
+        o_ref[:, cols] = own(dot(pb, v, 1, 0))
+        dq_ref[:, cols] = own(dot(ds, k, 1, 0))
         for j, part in enumerate((dot(q, ds, 0, 0), dot(d, pb, 0, 0))):
-            for i in range(2):
+            for i in range(4):
                 rows = jnp.concatenate([part[36 * i : 36 * i + 36], flag], axis=0)
                 pay[2 * h + i, j] = rows.astype(BF16)
-        two = pl.ds(2 * h, 2)
-        stores.append(pltpu.make_async_copy(pay.at[two], pay_hbm.at[two], out_sems.at[h]))
+        some = pl.ds(2 * h, 4)
+        stores.append(pltpu.make_async_copy(pay.at[some], pay_hbm.at[some], out_sems.at[h // 2]))
         stores[-1].start()
     for copy in stores:
         copy.wait()
@@ -105,7 +113,7 @@
             pltpu.VMEM((G, D), BF16),
             pltpu.VMEM((32, 2, 40, G), BF16),
             pltpu.SemaphoreType.DMA((3,)),
-            pltpu.SemaphoreType.DMA((HEADS,)),
+            pltpu.SemaphoreType.DMA((HEADS // 2,)),
         ],
         name="attention",
     )(img, whole, w_key, w_value, q, d)

time: 182 us -> 185 us (1.016)
  local copies, waits for them, and re-layouts: 1.62 us -> 7.13 us
  waiting for transfers between devices: 85 us -> 83 us
  Pallas kernels: 45.4 us -> 43.5 us
    unnamed x20 -> x26, local copies, waits for them, and re-layouts: 1.61 us -> 7.13 us
  transfers between devices with their start and end apart: 9 -> 9, of which waited for: 5 -> 5; matrix products, arithmetic and copies ran while one was open for 9% -> 10% of each run, Pallas kernels for 4% -> 4%
where the time goes in v5:
time: 185 us; the launch traced here: 182 us
  waiting for transfers between devices  83 us (45%)
  Pallas kernels  43.5 us (24%)
  starting transfers between devices  29.8 us (16%)
  matrix products  12.6 us (7%)
  local copies, waits for them, and re-layouts  7.13 us (4%)
  other arithmetic  4.71 us (3%)
    all_to_all x1, waiting for transfers between devices, on_device(): recv = lax.all_to_all(send, CHIP_AXES, 0, 0, tiled=True)  43.4 us
    all_to_all x1, waiting for transfers between devices, on_device(): whole = lax.all_to_all(copies_of(guide), TILE_AXES, 0, 0, tiled=True)  20.4 us
    pallas_call x1, Pallas kernels, attention(): pl.pallas_call(attention_kernel, in_specs=[pl.BlockSpec(memory_space=pltp...  19.8 us
    all_to_all x1, waiting for transfers between devices, on_device(): got = lax.all_to_all(pay, TILE_AXES, 0, 0, tiled=True)  15.8 us
    dot_general x4, matrix products, dot(): lax.dot_general(a, b, (((ca,), (cb,)), ((), ())), preferred_element_type=...  12.6 us
    all_to_all x1, starting transfers between devices, on_device(): whole = lax.all_to_all(copies_of(guide), TILE_AXES, 0, 0, tiled=True)  11.2 us
    all_to_all x1, starting transfers between devices, on_device(): recv = lax.all_to_all(send, CHIP_AXES, 0, 0, tiled=True)  8.98 us
    all_to_all x1, starting transfers between devices, on_device(): got = lax.all_to_all(pay, TILE_AXES, 0, 0, tiled=True)  8.32 us
  transfers between devices with their start and end apart: 9, of which 5 were waited for; matrix products, arithmetic and copies ran while one was open for 10% of the time, Pallas kernels for 4%

profile of v5, /device:TPU:2, one launch (start us, length us, event | category | flops | bytes accessed | tf_op | source)
XLA Modules:
  0.0 182.3 jit_solution(14194742636861988138)
XLA Ops:
  0.6 2.5 %copies_of_guide.1 = bf16[32,2,16,1152]{3,2,1,0:T(8,128)(2,1)} custom-call(bf16[2,16,1152]{2,1,0:T(8,128)(2,1)} %g_ref.2), custom_call_target="tpu_custom_call" | custom-call | tf_op jit(solution)/shard_map/copies_of_guide/pallas_call | solution.py:30
  3.1 0.0 copy-start.3
  3.1 0.0 copy-start.11
  3.1 11.2 %all-to-all-start = ((bf16[32,2,16,1152]{3,2,1,0:T(8,128)(2,1)}), bf16[32,2,16,1152]{3,2,1,0:T(8,128)(2,1)S(1)}, u32[]{:S(2)}, u32[]{:S(2)}) async-start(bf16[32,2,16,1152]{3,2,1,0:T(8,128)(2,1)} %copies_of_guide.1), calls=%async_computation | async-start | bytes 4718592 | tf_op jit(solution)/shard_map/all_to_all | solution.py:359
  14.4 0.0 copy-done.3
  14.4 0.2 fusion.13
  14.6 0.0 copy-done.11
  14.6 0.2 fusion.7
  14.8 0.1 collective-permute-start
  15.6 0.0 copy-start.4
  15.6 0.0 copy-start.12
  15.6 3.7 %convolution_convert_fusion.1.q_ref = bf16[256,1152]{1,0:T(8,128)(2,1)} fusion(bf16[256,1152]{1,0:T(8,128)(2,1)S(1)} %fusion.7, bf16[1152,1152]{1,0:T(8,128)(2,1)} %param.13), kind=kOutput, calls=%fused_computation.3 | convolution fusion | flops 679772160 | bytes 3833856 | tf_op jit(solution)/shard_map/dot_general | solution.py:20
  19.3 0.0 copy-done.4
  19.3 0.0 copy-done.12
  19.3 1.9 %convolution_convert_fusion.d_ref = bf16[256,1152]{1,0:T(8,128)(2,1)} fusion(bf16[256,1152]{1,0:T(8,128)(2,1)S(1)} %copy-done.4, bf16[1152,1152]{1,0:T(8,128)(2,1)S(1)} %copy-done.12), kind=kOutput, calls=%fused_computation.2 | convolution fusion | flops 679772160 | bytes 3833856 | tf_op jit(solution)/shard_map/dot_general | solution.py:20
  21.2 0.0 collective-permute-done
  21.2 2.8 %fusion.6.hid_ref = bf16[576,512]{1,0:T(8,128)(2,1)} fusion(s32[576]{0:T(1024)S(1)} %fusion.44, bf16[256,1152]{1,0:T(8,128)(2,1)} %collective-permute-done, bf16[256,1152]{1,0:T(8,128)(2,1)S(1)} %fusion.7), kind=kOutput, calls=%fused_computation.11 | convolution fusion | flops 682795008 | bytes 1771776 | tf_op jit(solution)/shard_map/dot_general | solution.py:20
  24.0 20.4 %all-to-all-done.g_hbm = bf16[32,2,16,1152]{3,2,1,0:T(8,128)(2,1)S(1)} async-done(((bf16[32,2,16,1152]{3,2,1,0:T(8,128)(2,1)}), bf16[32,2,16,1152]{3,2,1,0:T(8,128)(2,1)S(1)}, u32[]{:S(2)}, u32[]{:S(2)}) %all-to-all-start) | async-done | bytes 2359328 | tf_op jit(solution)/shard_map/all_to_all | solution.py:359
  44.4 0.0 copy-start
  44.4 1.5 copy-done
  45.9 19.8 %attention.1 = (bf16[32,2,40,512]{3,2,1,0:T(8,128)(2,1)}, bf16[256,1152]{1,0:T(8,128)(2,1)}, bf16[256,1152]{1,0:T(8,128)(2,1)}) custom-call(s32[1]{0:T(128)S(6)} %copy.15.img_ref, bf16[32,2,16,1152]{3,2,1,0:T(8,128)(2,1)} %copy-done, bf16[1152,1152]{1,0:T(8,128)(2,1)} %wk_hbm.3, bf16[1152,1152]{1,0:T(8,128)(2,1)} %wv_hbm.3, ...), custom_call_target="tpu_custom_call" | custom-call | tf_op jit(solution)/shard_map/attention/pallas_call | solution.py:99
  65.7 8.3 %all-to-all-start.1 = ((bf16[32,2,40,512]{3,2,1,0:T(8,128)(2,1)}), bf16[32,2,40,512]{3,2,1,0:T(8,128)(2,1)S(1)}, u32[]{:S(2)}, u32[]{:S(2)}) async-start(bf16[32,2,40,512]{3,2,1,0:T(8,128)(2,1)} %get-tuple-element.19), calls=%async_computation.1 | async-start | bytes 5242880 | tf_op jit(solution)/shard_map/all_to_all | solution.py:373
  74.1 0.1 collective-permute-start.3
  74.2 0.0 copy-start.6
  74.2 0.0 copy-start.5
  74.2 4.2 %fusion.12 = (f32[1152]{0:T(1024)S(1)}, f32[256]{0:T(256)S(1)}, f32[256,1152]{1,0:T(8,128)}) fusion(bf16[256,1152]{1,0:T(8,128)(2,1)S(1)} %copy-done.3, f32[256]{0:T(256)S(1)} %add_rsqrt_fusion, f32[1152]{0:T(1024)S(1)} %copy-done.11, bf16[256,1152]{1,0:T(8,128)(2,1)} %get-tuple-element.18.dq_ref, bf16[1152,1152]{1,0:T(8,128)(2,1)} %param.13), kind=kOutput, calls=%fused_computation.17 | convolution fusion | flops 681540224 | bytes 5024768 | tf_op jit(solution)/shard_map/dot_general | solution.py:20
  78.4 0.5 collective-permute-start.4
  78.8 1.1 fusion.28.want_ref
  79.9 0.0 copy-done.6
  79.9 0.1 collective-permute-start.2
  80.0 0.0 copy-done.5
  80.0 0.5 collective-permute-start.1
  80.4 0.0 collective-permute-done.4
  80.4 0.6 pad_maximum_fusion.gain_ref
  81.0 0.0 collective-permute-done.3.g2_ref
  81.0 0.0 copy-start.7
  81.0 1.7 collective-permute-done.1.o2_ref
  82.7 0.0 copy-done.7
  82.7 0.0 copy-start.9
  82.8 0.8 copy-done.9
  83.6 0.0 collective-permute-done.2.dq2_ref
  83.6 0.0 copy-start.8
  83.6 0.8 copy-done.8
  84.4 6.9 %weight_parts.1.send_ref = bf16[64,3,8,1152]{3,2,1,0:T(8,128)(2,1)} custom-call(s32[576,1]{1,0:T(8,128)} %fusion.28.want_ref, bf16[576,512]{1,0:T(8,128)(2,1)} %fusion.6.hid_ref, bf16[256,1152]{1,0:T(8,128)(2,1)} %get-tuple-element.21.o_ref, bf16[256,1152]{1,0:T(8,128)(2,1)} %copy-done.9, bf16[256,1152]{1,0:T(8,128)(2,1)} %get-tuple-element.18.dq_ref, ...), custom_call_target="tpu_custom_call" | custom-call | tf_op jit(solution)/shard_map/weight_parts/pallas_call | solution.py:167
  91.3 15.8 %all-to-all-done.1.got_hbm = bf16[32,2,40,512]{3,2,1,0:T(8,128)(2,1)S(1)} async-done(((bf16[32,2,40,512]{3,2,1,0:T(8,128)(2,1)}), bf16[32,2,40,512]{3,2,1,0:T(8,128)(2,1)S(1)}, u32[]{:S(2)}, u32[]{:S(2)}) %all-to-all-start.1) | async-done | bytes 2621472 | tf_op jit(solution)/shard_map/all_to_all | solution.py:373
  107.1 0.0 copy-start.2
  107.1 1.5 copy-done.2
  108.6 4.6 %image_sums.1 = (f32[576,128]{1,0:T(8,128)}, f32[576,128]{1,0:T(8,128)}, f32[512,256]{1,0:T(8,128)}) custom-call(s32[1]{0:T(128)} %bitcast.1.core_ref, bf16[32,2,40,512]{3,2,1,0:T(8,128)(2,1)} %copy-done.2, bf16[32,2,16,1152]{3,2,1,0:T(8,128)(2,1)} %copy-done), custom_call_target="tpu_custom_call" | custom-call | tf_op jit(solution)/shard_map/image_sums/pallas_call | solution.py:218
  113.2 0.1 collective-permute-start.5
  113.3 1.8 collective-permute-done.5.got_ref
  115.1 0.0 copy-start.10
  115.1 0.7 copy-done.10
  115.8 2.9 %fill_rest.1 = bf16[64,3,8,1152]{3,2,1,0:T(8,128)(2,1)} custom-call(bf16[64,3,8,1152]{3,2,1,0:T(8,128)(2,1)} %weight_parts.1.send_ref, f32[576,128]{1,0:T(8,128)} %get-tuple-element.24.mine_ref, f32[576,128]{1,0:T(8,128)} %copy-done.10, f32[512,256]{1,0:T(8,128)} %get-tuple-element.26.tok_ref, ...), custom_call_target="tpu_custom_call", output_to_operand_aliasing={{}: (0, {})} | custom-call | tf_op jit(solution)/shard_map/fill_rest/pallas_call | solution.py:263
  118.7 9.0 %all-to-all-start.2 = ((bf16[64,3,8,1152]{3,2,1,0:T(8,128)(2,1)}), bf16[64,3,8,1152]{3,2,1,0:T(8,128)(2,1)S(1)}, u32[]{:S(2)}, u32[]{:S(2)}) async-start(bf16[64,3,8,1152]{3,2,1,0:T(8,128)(2,1)} %fill_rest.1), calls=%async_computation.2 | async-start | bytes 7077888 | tf_op jit(solution)/shard_map/all_to_all | solution.py:391
  127.7 2.6 %fusion.11 = bf16[256,1152]{1,0:T(8,128)(2,1)} fusion(bf16[256,1152]{1,0:T(8,128)(2,1)} %param.9, f32[256,1152]{1,0:T(8,128)} %get-tuple-element.34, f32[256]{0:T(256)S(1)} %broadcast_multiply_fusion, f32[1152]{0:T(1024)S(1)} %copy-done.11, f32[256]{0:T(256)S(1)} %add_rsqrt_fusion), kind=kLoop, calls=%fused_computation.16 | loop fusion | flops 2064384 | bytes 2365952 | tf_op jit(solution)/shard_map/convert_element_type | solution.py:386
  130.3 43.4 %all-to-all-done.2.recv_hbm = bf16[64,3,8,1152]{3,2,1,0:T(8,128)(2,1)S(1)} async-done(((bf16[64,3,8,1152]{3,2,1,0:T(8,128)(2,1)}), bf16[64,3,8,1152]{3,2,1,0:T(8,128)(2,1)S(1)}, u32[]{:S(2)}, u32[]{:S(2)}) %all-to-all-start.2) | async-done | bytes 3538976 | tf_op jit(solution)/shard_map/all_to_all | solution.py:391
  173.7 0.0 copy-start.1
  173.7 1.8 copy-done.1
  175.5 6.7 %finish.1 = (f32[9,4,1152]{2,1,0:T(4,128)}, bf16[32,1152]{1,0:T(8,128)(2,1)}, f32[9,128]{1,0:T(8,128)}) custom-call(s32[1]{0:T(128)} %bitcast.yl_ref, bf16[64,3,8,1152]{3,2,1,0:T(8,128)(2,1)} %copy-done.1, bf16[1152,1152]{1,0:T(8,128)(2,1)} %wk_hbm.3, bf16[1152,1152]{1,0:T(8,128)(2,1)} %wv_hbm.3), custom_call_target="tpu_custom_call" | custom-call | tf_op jit(solution)/shard_map/finish/pallas_call | solution.py:335
  (5 shorter events, 0.0 us)
Async XLA Ops:
  3.1 11.2 %copy-start.3 = (bf16[256,1152]{1,0:T(8,128)(2,1)S(1)}, bf16[256,1152]{1,0:T(8,128)(2,1)}, u32[]{:S(2)}) copy-start(bf16[256,1152]{1,0:T(8,128)(2,1)} %param.9) | copy-start | bytes 1769476
  3.1 11.5 %copy-start.11 = (f32[1152]{0:T(1024)S(1)}, f32[1152]{0:T(1024)}, u32[]{:S(2)}) copy-start(f32[1152]{0:T(1024)} %param.12) | copy-start | bytes 13828
  3.1 41.3 %all-to-all-start = ((bf16[32,2,16,1152]{3,2,1,0:T(8,128)(2,1)}), bf16[32,2,16,1152]{3,2,1,0:T(8,128)(2,1)S(1)}, u32[]{:S(2)}, u32[]{:S(2)}) async-start(bf16[32,2,16,1152]{3,2,1,0:T(8,128)(2,1)} %copies_of_guide.1), calls=%async_computation | async-start | bytes 4718592 | tf_op jit(solution)/shard_map/all_to_all | solution.py:359
  14.8 6.4 %collective-permute-start = (bf16[256,1152]{1,0:T(8,128)(2,1)S(1)}, bf16[256,1152]{1,0:T(8,128)(2,1)}, u32[]{:S(2)}, u32[]{:S(2)}) collective-permute-start(bf16[256,1152]{1,0:T(8,128)(2,1)S(1)} %fusion.7), channel_id=1, source_target_pairs={{0,32},{32,0},{1,33},{33,1},{2,34},{34,2},{3,35},{35,3},{4,36},{36... | collective-permute-start | bytes 1769480 | tf_op jit(solution)/shard_map/ppermute | solution.py:367
  15.6 3.7 %copy-start.4 = (bf16[256,1152]{1,0:T(8,128)(2,1)S(1)}, bf16[256,1152]{1,0:T(8,128)(2,1)}, u32[]{:S(2)}) copy-start(bf16[256,1152]{1,0:T(8,128)(2,1)} %g_ref.3) | copy-start | bytes 1769476
  15.6 3.7 %copy-start.12 = (bf16[1152,1152]{1,0:T(8,128)(2,1)S(1)}, bf16[1152,1152]{1,0:T(8,128)(2,1)}, u32[]{:S(2)}) copy-start(bf16[1152,1152]{1,0:T(8,128)(2,1)} %param.16) | copy-start | bytes 7962628
  44.4 1.5 copy-start
  65.7 41.4 %all-to-all-start.1 = ((bf16[32,2,40,512]{3,2,1,0:T(8,128)(2,1)}), bf16[32,2,40,512]{3,2,1,0:T(8,128)(2,1)S(1)}, u32[]{:S(2)}, u32[]{:S(2)}) async-start(bf16[32,2,40,512]{3,2,1,0:T(8,128)(2,1)} %get-tuple-element.19), calls=%async_computation.1 | async-start | bytes 5242880 | tf_op jit(solution)/shard_map/all_to_all | solution.py:373
  74.1 7.0 %collective-permute-start.3 = (bf16[256,1152]{1,0:T(8,128)(2,1)}, bf16[256,1152]{1,0:T(8,128)(2,1)S(1)}, u32[]{:S(2)}, u32[]{:S(2)}) collective-permute-start(bf16[256,1152]{1,0:T(8,128)(2,1)} %g_ref.3), channel_id=1, source_target_pairs={{0,32},{32,0},{1,33},{33,1},{2,34},{34,2},{3,35},{35,3},{4,36},{36... | collective-permute-start | bytes 1769480 | tf_op jit(solution)/shard_map/ppermute | solution.py:369
  74.2 5.7 %copy-start.6 = (bf16[256,1152]{1,0:T(8,128)(2,1)S(1)}, bf16[256,1152]{1,0:T(8,128)(2,1)}, u32[]{:S(2)}) copy-start(bf16[256,1152]{1,0:T(8,128)(2,1)} %get-tuple-element.18.dq_ref) | copy-start | bytes 1769476
  74.2 5.8 %copy-start.5 = (bf16[256,1152]{1,0:T(8,128)(2,1)S(1)}, bf16[256,1152]{1,0:T(8,128)(2,1)}, u32[]{:S(2)}) copy-start(bf16[256,1152]{1,0:T(8,128)(2,1)} %get-tuple-element.21.o_ref) | copy-start | bytes 1769476
  78.4 2.1 %collective-permute-start.4 = (f32[1,1152]{1,0:T(1,128)S(1)}, f32[1,1152]{1,0:T(1,128)S(1)}, u32[]{:S(2)}, u32[]{:S(2)}) collective-permute-start(f32[1,1152]{1,0:T(1,128)S(1)} %broadcast_in_dim.7), channel_id=1, source_target_pairs={{0,32},{32,0},{1,33},{33,1},{2,34},{34,2},{3,35},{35,3},{4,36},{36... | collective-permute-start | bytes 13832 | tf_op jit(solution)/shard_map/ppermute | solution.py:379
  79.9 3.7 %collective-permute-start.2 = (bf16[256,1152]{1,0:T(8,128)(2,1)S(1)}, bf16[256,1152]{1,0:T(8,128)(2,1)S(1)}, u32[]{:S(2)}, u32[]{:S(2)}) collective-permute-start(bf16[256,1152]{1,0:T(8,128)(2,1)S(1)} %copy-done.6), channel_id=1, source_target_pairs={{0,32},{32,0},{1,33},{33,1},{2,34},{34,2},{3,35},{35,3},{4,36},{36... | collective-permute-start | bytes 1769480 | tf_op jit(solution)/shard_map/ppermute | solution.py:375
  80.0 2.8 %collective-permute-start.1 = (bf16[256,1152]{1,0:T(8,128)(2,1)S(1)}, bf16[256,1152]{1,0:T(8,128)(2,1)S(1)}, u32[]{:S(2)}, u32[]{:S(2)}) collective-permute-start(bf16[256,1152]{1,0:T(8,128)(2,1)S(1)} %copy-done.5), channel_id=1, source_target_pairs={{0,32},{32,0},{1,33},{33,1},{2,34},{34,2},{3,35},{35,3},{4,36},{36... | collective-permute-start | bytes 1769480 | tf_op jit(solution)/shard_map/ppermute | solution.py:376
  81.0 1.7 copy-start.7
  82.7 0.8 copy-start.9
  83.6 0.8 copy-start.8
  107.1 1.5 copy-start.2
  113.2 1.9 %collective-permute-start.5 = (f32[576,128]{1,0:T(8,128)}, f32[576,128]{1,0:T(8,128)S(1)}, u32[]{:S(2)}, u32[]{:S(2)}) collective-permute-start(f32[576,128]{1,0:T(8,128)} %get-tuple-element.25), channel_id=1, source_target_pairs={{0,32},{32,0},{1,33},{33,1},{2,34},{34,2},{3,35},{35,3},{4,36},{36... | collective-permute-start | bytes 884744 | tf_op jit(solution)/shard_map/ppermute | solution.py:390
  115.1 0.7 copy-start.10
  118.7 55.0 %all-to-all-start.2 = ((bf16[64,3,8,1152]{3,2,1,0:T(8,128)(2,1)}), bf16[64,3,8,1152]{3,2,1,0:T(8,128)(2,1)S(1)}, u32[]{:S(2)}, u32[]{:S(2)}) async-start(bf16[64,3,8,1152]{3,2,1,0:T(8,128)(2,1)} %fill_rest.1), calls=%async_computation.2 | async-start | bytes 7077888 | tf_op jit(solution)/shard_map/all_to_all | solution.py:391
  173.7 1.8 copy-start.1

commit v6 on v5

--- a/solution.py
+++ b/solution.py
@@ -20,18 +20,21 @@
     return lax.dot_general(a, b, (((ca,), (cb,)), ((), ())), preferred_element_type=F32)
 
 
-def copies_kernel(g_ref, out):
-    for i in range(32):
-        out[i] = g_ref[...]
+def copies_kernel(g_ref, out, sems):
+    copies = [pltpu.make_async_copy(g_ref, out.at[i], sems.at[i]) for i in range(32)]
+    for copy in copies:
+        copy.start()
+    for copy in copies:
+        copy.wait()
 
 
 def copies_of(guide):
-    vmem = pl.BlockSpec(memory_space=pltpu.VMEM)
     return pl.pallas_call(
         copies_kernel,
-        in_specs=[vmem],
-        out_specs=vmem,
-        out_shape=pltpu.VMEM((32, *guide.shape), guide.dtype),
+        in_specs=[pl.BlockSpec(memory_space=pltpu.VMEM)],
+        out_specs=pl.BlockSpec(memory_space=pl.ANY),
+        out_shape=jax.ShapeDtypeStruct((32, *guide.shape), guide.dtype),
+        scratch_shapes=[pltpu.SemaphoreType.DMA((32,))],
         name="copies_of_guide",
     )(guide)
 
@@ -208,8 +211,8 @@
         for out, c in ((mine_ref, core), (theirs_ref, 1 - core)):
             start = pl.multiple_of(n * 576 + c * 288, 32)
             out[n * 288 : n * 288 + 288] = scr[pl.ds(start, 288), :]
-    both = jnp.concatenate([x.astype(F32) for x in rounded] + [jnp.zeros((96, G), F32)], axis=0)
-    tok_ref[...] = both.T
+    tok_ref[:80] = rounded[0]
+    tok_ref[80:] = rounded[1]
 
 
 def image_sums(core, got, whole):
@@ -222,7 +225,7 @@
         out_shape=[
             jax.ShapeDtypeStruct((ROWS, 128), F32),
             jax.ShapeDtypeStruct((ROWS, 128), F32),
-            jax.ShapeDtypeStruct((G, 256), F32),
+            jax.ShapeDtypeStruct((160, G), BF16),
         ],
         scratch_shapes=[
             pltpu.VMEM((D, 128), F32),
@@ -234,42 +237,58 @@
     )(core, got, whole)
 
 
-def fill_rest_kernel(send_ref, mine_ref, got_ref, tok_ref, gain_ref, out_ref, scr):
-    scr[:, :, 512:EARLY] = jnp.zeros((64, 8, EARLY - 512), F32)
+def fill_tokens_kernel(tok_ref, gain_ref, out_ref):
+    out_ref[:, :, 512:EARLY] = jnp.zeros((64, 8, EARLY - 512), F32)
+    rows = jnp.concatenate([tok_ref[...].astype(F32), jnp.zeros((96, G), F32)], axis=0)
+    tok = rows.T.reshape(32, 16, 256)
+    for half in range(2):
+        lanes = slice(160 * half + 160, 160 * half + 320)
+        for n in range(2):
+            out_ref[32 * n : 32 * n + 32, :, lanes] = tok[:, 8 * half : 8 * half + 8, :160]
+    for b in range(14, 18):
+        row, lane = GAINS[b]
+        block = gain_ref[:, 128 * b : 128 * b + 128]
+        out_ref[:, row, lane : lane + 128] = jnp.broadcast_to(block, (64, 128))
+
+
+def fill_tokens(tok, gain):
+    vmem = pl.BlockSpec(memory_space=pltpu.VMEM)
+    return pl.pallas_call(
+        fill_tokens_kernel,
+        in_specs=[vmem] * 2,
+        out_specs=vmem,
+        out_shape=jax.ShapeDtypeStruct((64, 8, EARLY), F32),
+        name="fill_tokens",
+    )(tok, gain)
+
+
+def fill_rest_kernel(send_ref, mine_ref, got_ref, part_ref, out_ref, scr):
     total = mine_ref[...] + got_ref[...]
     high = total.astype(BF16)
     low = (total - high.astype(F32)).astype(BF16)
     want = eight_and_one(lax.broadcasted_iota(jnp.int32, (ROWS, ROWS), 0))
     order = (want == lax.broadcasted_iota(jnp.int32, (ROWS, ROWS), 1)).astype(BF16)
     moved = dot(order, jnp.concatenate([high, low], axis=1), 1, 0)
-    tok = tok_ref[...].reshape(32, 16, 256)
-    for half in range(2):
-        lanes = slice(160 * half + 160, 160 * half + 320)
-        for n in range(2):
-            scr[32 * n : 32 * n + 32, :, lanes] = tok[:, 8 * half : 8 * half + 8, :160]
+    scr[...] = part_ref[...]
     for n in range(2):
         piece = moved[:, 128 * n : 128 * n + 80]
         scr[:, :, 80 * n : 80 * n + 80] = piece[:512].reshape(64, 8, 80)
         scr[:, 0, 480 + 80 * n : 560 + 80 * n] = piece[512:]
-    for b in range(14, 18):
-        row, lane = GAINS[b]
-        block = gain_ref[:, 128 * b : 128 * b + 128]
-        scr[:, row, lane : lane + 128] = jnp.broadcast_to(block, (64, 128))
     out_ref[:, 0] = scr[...].astype(BF16)
 
 
-def fill_rest(send, mine, got, tok, gain):
+def fill_rest(send, mine, got, part):
     vmem = pl.BlockSpec(memory_space=pltpu.VMEM)
     return pl.pallas_call(
         fill_rest_kernel,
         grid=(1,),
-        in_specs=[pl.BlockSpec(memory_space=pl.ANY)] + [vmem] * 4,
+        in_specs=[pl.BlockSpec(memory_space=pl.ANY)] + [vmem] * 3,
         out_specs=pl.BlockSpec((64, 1, 8, EARLY), lambda i: (0, 2, 0, 0)),
         out_shape=jax.ShapeDtypeStruct((64, 3, 8, D), BF16),
         scratch_shapes=[pltpu.VMEM((64, 8, EARLY), F32)],
         input_output_aliases={0: 0},
         name="fill_rest",
-    )(send, mine, got, tok, gain)
+    )(send, mine, got, part)
 
 
 def finish_kernel(
@@ -325,8 +344,8 @@
         gw_ref[8:9, 1 + n] = kv[n, 8:9]
     for copy in late:
         copy.wait()
-    grad = dot(tok[0].astype(BF16), wk[...], 1, 1) + dot(tok[1].astype(BF16), wv[...], 1, 1)
-    gg_ref[...] = grad.astype(BF16)
+    grad = dot(wk[...], tok[0].astype(BF16), 1, 1) + dot(wv[...], tok[1].astype(BF16), 1, 1)
+    gg_ref[...] = grad.T.astype(BF16)
 
 
 def finish(yl, recv, w_key, w_value):
@@ -387,7 +406,7 @@
 
     got, send = lax.optimization_barrier((got, send))
     mine, theirs, tok = image_sums(core[None], got, whole)
-    send = fill_rest(send, mine, lax.ppermute(theirs, "c", SWAP), tok, gains)
+    send = fill_rest(send, mine, lax.ppermute(theirs, "c", SWAP), fill_tokens(tok, gains))
     recv = lax.all_to_all(send, CHIP_AXES, 0, 0, tiled=True)
     grad_weights, grad_guide, grad_gain = finish(yl[None], recv, w_key, w_value)
     grad_weights = grad_weights.transpose(1, 0, 2)

time: 185 us -> 182 us (0.984); the launches traced: 182 us -> 181 us
  local copies, waits for them, and re-layouts: 7.13 us -> 1.59 us
  waiting for transfers between devices: 83 us -> 85.7 us
  Pallas kernels: 43.5 us -> 46.1 us
    unnamed x26 -> x20, local copies, waits for them, and re-layouts: 7.13 us -> 1.58 us
    all_to_all x1, waiting for transfers between devices: 43.4 us -> 46.2 us  [on_device(): recv = lax.all_to_all(send, CHIP_AXES, 0, 0, tiled=True)]
    pallas_call x1 -> x2, Pallas kernels: 2.49 us -> 5.07 us  [the longest x1 2.75 us: copies_of(): pl.pallas_call(copies_kernel, in_specs=[pl.BlockSpec(memory_space=pltpu.V...]
  transfers between devices with their start and end apart: 9 -> 9, of which waited for: 5 -> 4; matrix products, arithmetic and copies ran while one was open for 10% -> 9% of each run, Pallas kernels for 4% -> 5%
where the time goes in v6:
time: 182 us; the launch traced here: 181 us
  waiting for transfers between devices  85.7 us (47%)
  Pallas kernels  46.1 us (25%)
  starting transfers between devices  29.9 us (16%)
  matrix products  11.2 us (6%)
  other arithmetic  5.33 us (3%)
    all_to_all x1, waiting for transfers between devices, on_device(): recv = lax.all_to_all(send, CHIP_AXES, 0, 0, tiled=True)  46.2 us
    all_to_all x1, waiting for transfers between devices, on_device(): whole = lax.all_to_all(copies_of(guide), TILE_AXES, 0, 0, tiled=True)  20.1 us
    pallas_call x1, Pallas kernels, attention(): pl.pallas_call(attention_kernel, in_specs=[pl.BlockSpec(memory_space=pltp...  19.9 us
    all_to_all x1, waiting for transfers between devices, on_device(): got = lax.all_to_all(pay, TILE_AXES, 0, 0, tiled=True)  17.6 us
    all_to_all x1, starting transfers between devices, on_device(): whole = lax.all_to_all(copies_of(guide), TILE_AXES, 0, 0, tiled=True)  11.3 us
    dot_general x4, matrix products, dot(): lax.dot_general(a, b, (((ca,), (cb,)), ((), ())), preferred_element_type=...  11.2 us
    all_to_all x1, starting transfers between devices, on_device(): recv = lax.all_to_all(send, CHIP_AXES, 0, 0, tiled=True)  9.06 us
    all_to_all x1, starting transfers between devices, on_device(): got = lax.all_to_all(pay, TILE_AXES, 0, 0, tiled=True)  8.37 us
  transfers between devices with their start and end apart: 9, of which 4 were waited for; matrix products, arithmetic and copies ran while one was open for 9% of the time, Pallas kernels for 5%

profile of v6, /device:TPU:2, one launch (start us, length us, event | category | flops | bytes accessed | tf_op | source)
XLA Modules:
  0.0 181.3 jit_solution(12458863053375228169)
XLA Ops:
  0.6 0.0 copy-start
  0.6 2.7 %copies_of_guide.1 = bf16[32,2,16,1152]{3,2,1,0:T(8,128)(2,1)} custom-call(bf16[2,16,1152]{2,1,0:T(8,128)(2,1)} %g_ref.2), custom_call_target="tpu_custom_call" | custom-call | tf_op jit(solution)/shard_map/copies_of_guide/pallas_call | solution.py:32
  3.4 0.0 copy-start.1
  3.4 0.0 copy-start.8
  3.4 11.3 %all-to-all-start = ((bf16[32,2,16,1152]{3,2,1,0:T(8,128)(2,1)}), bf16[32,2,16,1152]{3,2,1,0:T(8,128)(2,1)}, u32[]{:S(2)}, u32[]{:S(2)}) async-start(bf16[32,2,16,1152]{3,2,1,0:T(8,128)(2,1)} %copies_of_guide.1), calls=%async_computation | async-start | bytes 4718592 | tf_op jit(solution)/shard_map/all_to_all | solution.py:378
  14.7 0.0 copy-done.1
  14.7 0.2 fusion.13
  14.9 0.0 copy-done.8
  14.9 1.0 fusion.7
  16.0 0.0 collective-permute-start
  16.6 0.0 copy-done
  16.7 0.0 copy-start.2
  16.7 0.0 copy-start.9
  16.7 3.0 %convolution_convert_fusion.1.q_ref = bf16[256,1152]{1,0:T(8,128)(2,1)} fusion(bf16[256,1152]{1,0:T(8,128)(2,1)} %fusion.7, bf16[1152,1152]{1,0:T(8,128)(2,1)S(1)} %copy-done), kind=kOutput, calls=%fused_computation.3 | convolution fusion | flops 679772160 | bytes 3833856 | tf_op jit(solution)/shard_map/dot_general | solution.py:20
  19.7 0.0 copy-done.2
  19.7 0.0 copy-done.9
  19.7 1.9 %convolution_convert_fusion.d_ref = bf16[256,1152]{1,0:T(8,128)(2,1)} fusion(bf16[256,1152]{1,0:T(8,128)(2,1)S(1)} %copy-done.2, bf16[1152,1152]{1,0:T(8,128)(2,1)S(1)} %copy-done.9), kind=kOutput, calls=%fused_computation.2 | convolution fusion | flops 679772160 | bytes 3833856 | tf_op jit(solution)/shard_map/dot_general | solution.py:20
  21.6 0.0 collective-permute-done
  21.6 3.1 %fusion.6.hid_ref = bf16[576,512]{1,0:T(8,128)(2,1)} fusion(s32[576]{0:T(1024)S(1)} %fusion.44, bf16[256,1152]{1,0:T(8,128)(2,1)} %collective-permute-done, bf16[256,1152]{1,0:T(8,128)(2,1)} %fusion.7), kind=kOutput, calls=%fused_computation.11 | convolution fusion | flops 682795008 | bytes 1771776 | tf_op jit(solution)/shard_map/dot_general | solution.py:20
  24.7 20.1 %all-to-all-done.g_hbm = bf16[32,2,16,1152]{3,2,1,0:T(8,128)(2,1)} async-done(((bf16[32,2,16,1152]{3,2,1,0:T(8,128)(2,1)}), bf16[32,2,16,1152]{3,2,1,0:T(8,128)(2,1)}, u32[]{:S(2)}, u32[]{:S(2)}) %all-to-all-start) | async-done | bytes 2359328 | tf_op jit(solution)/shard_map/all_to_all | solution.py:378
  44.8 19.9 %attention.1 = (bf16[32,2,40,512]{3,2,1,0:T(8,128)(2,1)}, bf16[256,1152]{1,0:T(8,128)(2,1)}, bf16[256,1152]{1,0:T(8,128)(2,1)}) custom-call(s32[1]{0:T(128)S(6)} %copy.15.img_ref, bf16[32,2,16,1152]{3,2,1,0:T(8,128)(2,1)} %all-to-all-done.g_hbm, bf16[1152,1152]{1,0:T(8,128)(2,1)} %wk_hbm.3, bf16[1152,1152]{1,0:T(8,128)(2,1)} %wv_hbm.3, ...), custom_call_target="tpu_custom_call" | custom-call | tf_op jit(solution)/shard_map/attention/pallas_call | solution.py:102
  64.7 8.4 %all-to-all-start.1 = ((bf16[32,2,40,512]{3,2,1,0:T(8,128)(2,1)}), bf16[32,2,40,512]{3,2,1,0:T(8,128)(2,1)}, u32[]{:S(2)}, u32[]{:S(2)}) async-start(bf16[32,2,40,512]{3,2,1,0:T(8,128)(2,1)} %get-tuple-element.19), calls=%async_computation.1 | async-start | bytes 5242880 | tf_op jit(solution)/shard_map/all_to_all | solution.py:392
  73.1 0.1 collective-permute-start.3
  73.2 0.0 copy-start.4
  73.2 0.0 copy-start.3
  73.2 3.2 %fusion.12 = (f32[1152]{0:T(1024)S(1)}, f32[256]{0:T(256)S(1)}, f32[256,1152]{1,0:T(8,128)}) fusion(bf16[256,1152]{1,0:T(8,128)(2,1)S(1)} %copy-done.1, f32[256]{0:T(256)S(1)} %add_rsqrt_fusion, f32[1152]{0:T(1024)S(1)} %copy-done.8, bf16[256,1152]{1,0:T(8,128)(2,1)} %get-tuple-element.18.dq_ref, bf16[1152,1152]{1,0:T(8,128)(2,1)S(1)} %copy-done), kind=kOutput, calls=%fused_computation.17 | convolution fusion | flops 681540224 | bytes 5024768 | tf_op jit(solution)/shard_map/dot_general | solution.py:20
  76.4 0.5 collective-permute-start.4
  76.9 1.1 fusion.28.want_ref
  77.9 0.0 copy-done.4
  77.9 0.0 collective-permute-start.2
  78.0 0.0 copy-done.3
  78.0 0.5 collective-permute-start.1
  78.5 0.0 collective-permute-done.4
  78.5 0.6 pad_maximum_fusion.gain_ref
  79.1 0.0 collective-permute-done.3.g2_ref
  79.1 0.0 copy-start.5
  79.1 1.7 collective-permute-done.1.o2_ref
  80.8 0.0 copy-done.5
  80.8 0.0 copy-start.6
  80.8 0.8 copy-done.6
  81.6 0.0 collective-permute-done.2.dq2_ref
  81.6 6.9 %weight_parts.1.send_ref = bf16[64,3,8,1152]{3,2,1,0:T(8,128)(2,1)} custom-call(s32[576,1]{1,0:T(8,128)} %fusion.28.want_ref, bf16[576,512]{1,0:T(8,128)(2,1)} %fusion.6.hid_ref, bf16[256,1152]{1,0:T(8,128)(2,1)} %get-tuple-element.21.o_ref, bf16[256,1152]{1,0:T(8,128)(2,1)} %copy-done.6, bf16[256,1152]{1,0:T(8,128)(2,1)} %get-tuple-element.18.dq_ref, ...), custom_call_target="tpu_custom_call" | custom-call | tf_op jit(solution)/shard_map/weight_parts/pallas_call | solution.py:170
  88.6 17.6 %all-to-all-done.1.got_hbm = bf16[32,2,40,512]{3,2,1,0:T(8,128)(2,1)} async-done(((bf16[32,2,40,512]{3,2,1,0:T(8,128)(2,1)}), bf16[32,2,40,512]{3,2,1,0:T(8,128)(2,1)}, u32[]{:S(2)}, u32[]{:S(2)}) %all-to-all-start.1) | async-done | bytes 2621472 | tf_op jit(solution)/shard_map/all_to_all | solution.py:392
  106.1 4.5 %image_sums.1 = (f32[576,128]{1,0:T(8,128)}, f32[576,128]{1,0:T(8,128)}, bf16[160,512]{1,0:T(8,128)(2,1)}) custom-call(s32[1]{0:T(128)} %bitcast.1.core_ref, bf16[32,2,40,512]{3,2,1,0:T(8,128)(2,1)} %all-to-all-done.1.got_hbm, bf16[32,2,16,1152]{3,2,1,0:T(8,128)(2,1)} %all-to-all-done.g_hbm), custom_call_target="tpu_custom_call" | custom-call | tf_op jit(solution)/shard_map/image_sums/pallas_call | solution.py:221
  110.6 0.1 collective-permute-start.5
  110.7 2.3 %fill_tokens.1.part_ref = f32[64,8,640]{2,1,0:T(8,128)} custom-call(bf16[160,512]{1,0:T(8,128)(2,1)} %get-tuple-element.26.tok_ref, f32[1,2304]{1,0:T(1,128)} %pad_maximum_fusion.gain_ref), custom_call_target="tpu_custom_call" | custom-call | tf_op jit(solution)/shard_map/fill_tokens/pallas_call | solution.py:256
  113.0 0.0 collective-permute-done.5.got_ref
  113.0 0.0 copy-start.7
  113.0 0.7 copy-done.7
  113.7 3.1 %fill_rest.1 = bf16[64,3,8,1152]{3,2,1,0:T(8,128)(2,1)} custom-call(bf16[64,3,8,1152]{3,2,1,0:T(8,128)(2,1)} %weight_parts.1.send_ref, f32[576,128]{1,0:T(8,128)} %get-tuple-element.24.mine_ref, f32[576,128]{1,0:T(8,128)} %copy-done.7, f32[64,8,640]{2,1,0:T(8,128)} %fill_tokens.1.part_ref), custom_call_target="tpu_custom_call", output_to_operand_aliasing={{}: (0, {})} | custom-call | tf_op jit(solution)/shard_map/fill_rest/pallas_call | solution.py:282
  116.9 9.1 %all-to-all-start.2 = ((bf16[64,3,8,1152]{3,2,1,0:T(8,128)(2,1)}), bf16[64,3,8,1152]{3,2,1,0:T(8,128)(2,1)}, u32[]{:S(2)}, u32[]{:S(2)}) async-start(bf16[64,3,8,1152]{3,2,1,0:T(8,128)(2,1)} %fill_rest.1), calls=%async_computation.2 | async-start | bytes 7077888 | tf_op jit(solution)/shard_map/all_to_all | solution.py:410
  125.9 2.4 %fusion.11 = bf16[256,1152]{1,0:T(8,128)(2,1)} fusion(bf16[256,1152]{1,0:T(8,128)(2,1)S(1)} %copy-done.1, f32[256,1152]{1,0:T(8,128)} %get-tuple-element.34, f32[256]{0:T(256)S(1)} %broadcast_multiply_fusion, f32[1152]{0:T(1024)S(1)} %copy-done.8, f32[256]{0:T(256)S(1)} %add_rsqrt_fusion), kind=kLoop, calls=%fused_computation.16 | loop fusion | flops 2064384 | bytes 2365952 | tf_op jit(solution)/shard_map/convert_element_type | solution.py:405
  128.3 46.2 %all-to-all-done.2.recv_hbm = bf16[64,3,8,1152]{3,2,1,0:T(8,128)(2,1)} async-done(((bf16[64,3,8,1152]{3,2,1,0:T(8,128)(2,1)}), bf16[64,3,8,1152]{3,2,1,0:T(8,128)(2,1)}, u32[]{:S(2)}, u32[]{:S(2)}) %all-to-all-start.2) | async-done | bytes 3538976 | tf_op jit(solution)/shard_map/all_to_all | solution.py:410
  174.6 6.6 %finish.1 = (f32[9,4,1152]{2,1,0:T(4,128)}, bf16[32,1152]{1,0:T(8,128)(2,1)}, f32[9,128]{1,0:T(8,128)}) custom-call(s32[1]{0:T(128)} %bitcast.yl_ref, bf16[64,3,8,1152]{3,2,1,0:T(8,128)(2,1)} %all-to-all-done.2.recv_hbm, bf16[1152,1152]{1,0:T(8,128)(2,1)} %wk_hbm.3, bf16[1152,1152]{1,0:T(8,128)(2,1)} %wv_hbm.3), custom_call_target="tpu_custom_call" | custom-call | tf_op jit(solution)/shard_map/finish/pallas_call | solution.py:354
  (5 shorter events, 0.0 us)
Async XLA Ops:
  0.6 16.0 %copy-start = (bf16[1152,1152]{1,0:T(8,128)(2,1)S(1)}, bf16[1152,1152]{1,0:T(8,128)(2,1)}, u32[]{:S(2)}) copy-start(bf16[1152,1152]{1,0:T(8,128)(2,1)} %param.13) | copy-start | bytes 7962628
  3.4 11.3 %copy-start.1 = (bf16[256,1152]{1,0:T(8,128)(2,1)S(1)}, bf16[256,1152]{1,0:T(8,128)(2,1)}, u32[]{:S(2)}) copy-start(bf16[256,1152]{1,0:T(8,128)(2,1)} %param.9) | copy-start | bytes 1769476
  3.4 11.5 %copy-start.8 = (f32[1152]{0:T(1024)S(1)}, f32[1152]{0:T(1024)}, u32[]{:S(2)}) copy-start(f32[1152]{0:T(1024)} %param.12) | copy-start | bytes 13828
  3.4 41.4 %all-to-all-start = ((bf16[32,2,16,1152]{3,2,1,0:T(8,128)(2,1)}), bf16[32,2,16,1152]{3,2,1,0:T(8,128)(2,1)}, u32[]{:S(2)}, u32[]{:S(2)}) async-start(bf16[32,2,16,1152]{3,2,1,0:T(8,128)(2,1)} %copies_of_guide.1), calls=%async_computation | async-start | bytes 4718592 | tf_op jit(solution)/shard_map/all_to_all | solution.py:378
  16.0 5.6 %collective-permute-start = (bf16[256,1152]{1,0:T(8,128)(2,1)}, bf16[256,1152]{1,0:T(8,128)(2,1)}, u32[]{:S(2)}, u32[]{:S(2)}) collective-permute-start(bf16[256,1152]{1,0:T(8,128)(2,1)} %fusion.7), channel_id=1, source_target_pairs={{0,32},{32,0},{1,33},{33,1},{2,34},{34,2},{3,35},{35,3},{4,36},{36... | collective-permute-start | bytes 1769480 | tf_op jit(solution)/shard_map/ppermute | solution.py:386
  16.7 3.1 %copy-start.2 = (bf16[256,1152]{1,0:T(8,128)(2,1)S(1)}, bf16[256,1152]{1,0:T(8,128)(2,1)}, u32[]{:S(2)}) copy-start(bf16[256,1152]{1,0:T(8,128)(2,1)} %g_ref.3) | copy-start | bytes 1769476
  16.7 3.1 %copy-start.9 = (bf16[1152,1152]{1,0:T(8,128)(2,1)S(1)}, bf16[1152,1152]{1,0:T(8,128)(2,1)}, u32[]{:S(2)}) copy-start(bf16[1152,1152]{1,0:T(8,128)(2,1)} %param.16) | copy-start | bytes 7962628
  64.7 41.5 %all-to-all-start.1 = ((bf16[32,2,40,512]{3,2,1,0:T(8,128)(2,1)}), bf16[32,2,40,512]{3,2,1,0:T(8,128)(2,1)}, u32[]{:S(2)}, u32[]{:S(2)}) async-start(bf16[32,2,40,512]{3,2,1,0:T(8,128)(2,1)} %get-tuple-element.19), calls=%async_computation.1 | async-start | bytes 5242880 | tf_op jit(solution)/shard_map/all_to_all | solution.py:392
  73.1 6.0 %collective-permute-start.3 = (bf16[256,1152]{1,0:T(8,128)(2,1)}, bf16[256,1152]{1,0:T(8,128)(2,1)S(1)}, u32[]{:S(2)}, u32[]{:S(2)}) collective-permute-start(bf16[256,1152]{1,0:T(8,128)(2,1)} %g_ref.3), channel_id=1, source_target_pairs={{0,32},{32,0},{1,33},{33,1},{2,34},{34,2},{3,35},{35,3},{4,36},{36... | collective-permute-start | bytes 1769480 | tf_op jit(solution)/shard_map/ppermute | solution.py:388
  73.2 4.8 %copy-start.4 = (bf16[256,1152]{1,0:T(8,128)(2,1)S(1)}, bf16[256,1152]{1,0:T(8,128)(2,1)}, u32[]{:S(2)}) copy-start(bf16[256,1152]{1,0:T(8,128)(2,1)} %get-tuple-element.18.dq_ref) | copy-start | bytes 1769476
  73.2 4.8 %copy-start.3 = (bf16[256,1152]{1,0:T(8,128)(2,1)S(1)}, bf16[256,1152]{1,0:T(8,128)(2,1)}, u32[]{:S(2)}) copy-start(bf16[256,1152]{1,0:T(8,128)(2,1)} %get-tuple-element.21.o_ref) | copy-start | bytes 1769476
  76.4 2.1 %collective-permute-start.4 = (f32[1,1152]{1,0:T(1,128)S(1)}, f32[1,1152]{1,0:T(1,128)S(1)}, u32[]{:S(2)}, u32[]{:S(2)}) collective-permute-start(f32[1,1152]{1,0:T(1,128)S(1)} %broadcast_in_dim.7), channel_id=1, source_target_pairs={{0,32},{32,0},{1,33},{33,1},{2,34},{34,2},{3,35},{35,3},{4,36},{36... | collective-permute-start | bytes 13832 | tf_op jit(solution)/shard_map/ppermute | solution.py:398
  77.9 3.7 %collective-permute-start.2 = (bf16[256,1152]{1,0:T(8,128)(2,1)S(1)}, bf16[256,1152]{1,0:T(8,128)(2,1)}, u32[]{:S(2)}, u32[]{:S(2)}) collective-permute-start(bf16[256,1152]{1,0:T(8,128)(2,1)S(1)} %copy-done.4), channel_id=1, source_target_pairs={{0,32},{32,0},{1,33},{33,1},{2,34},{34,2},{3,35},{35,3},{4,36},{36... | collective-permute-start | bytes 1769480 | tf_op jit(solution)/shard_map/ppermute | solution.py:394
  78.0 2.8 %collective-permute-start.1 = (bf16[256,1152]{1,0:T(8,128)(2,1)S(1)}, bf16[256,1152]{1,0:T(8,128)(2,1)S(1)}, u32[]{:S(2)}, u32[]{:S(2)}) collective-permute-start(bf16[256,1152]{1,0:T(8,128)(2,1)S(1)} %copy-done.3), channel_id=1, source_target_pairs={{0,32},{32,0},{1,33},{33,1},{2,34},{34,2},{3,35},{35,3},{4,36},{36... | collective-permute-start | bytes 1769480 | tf_op jit(solution)/shard_map/ppermute | solution.py:395
  79.1 1.7 copy-start.5
  80.8 0.8 copy-start.6
  110.6 2.4 %collective-permute-start.5 = (f32[576,128]{1,0:T(8,128)}, f32[576,128]{1,0:T(8,128)S(1)}, u32[]{:S(2)}, u32[]{:S(2)}) collective-permute-start(f32[576,128]{1,0:T(8,128)} %get-tuple-element.25), channel_id=1, source_target_pairs={{0,32},{32,0},{1,33},{33,1},{2,34},{34,2},{3,35},{35,3},{4,36},{36... | collective-permute-start | bytes 884744 | tf_op jit(solution)/shard_map/ppermute | solution.py:409
  113.0 0.7 copy-start.7
  116.9 57.7 %all-to-all-start.2 = ((bf16[64,3,8,1152]{3,2,1,0:T(8,128)(2,1)}), bf16[64,3,8,1152]{3,2,1,0:T(8,128)(2,1)}, u32[]{:S(2)}, u32[]{:S(2)}) async-start(bf16[64,3,8,1152]{3,2,1,0:T(8,128)(2,1)} %fill_rest.1), calls=%async_computation.2 | async-start | bytes 7077888 | tf_op jit(solution)/shard_map/all_to_all | solution.py:410

commit v7 on v5

--- a/solution.py
+++ b/solution.py
@@ -12,7 +12,6 @@
 F32 = jnp.float32
 BF16 = jnp.bfloat16
 TILE_AXES = ("x", "yh", "z")
-CHIP_AXES = ("yl", "x", "yh", "z")
 SWAP = [(0, 1), (1, 0)]
 
 
@@ -20,18 +19,21 @@
     return lax.dot_general(a, b, (((ca,), (cb,)), ((), ())), preferred_element_type=F32)
 
 
-def copies_kernel(g_ref, out):
-    for i in range(32):
-        out[i] = g_ref[...]
+def copies_kernel(g_ref, out, sems):
+    copies = [pltpu.make_async_copy(g_ref, out.at[i], sems.at[i]) for i in range(32)]
+    for copy in copies:
+        copy.start()
+    for copy in copies:
+        copy.wait()
 
 
 def copies_of(guide):
-    vmem = pl.BlockSpec(memory_space=pltpu.VMEM)
     return pl.pallas_call(
         copies_kernel,
-        in_specs=[vmem],
-        out_specs=vmem,
-        out_shape=pltpu.VMEM((32, *guide.shape), guide.dtype),
+        in_specs=[pl.BlockSpec(memory_space=pltpu.VMEM)],
+        out_specs=pl.BlockSpec(memory_space=pl.ANY),
+        out_shape=jax.ShapeDtypeStruct((32, *guide.shape), guide.dtype),
+        scratch_shapes=[pltpu.SemaphoreType.DMA((32,))],
         name="copies_of_guide",
     )(guide)
 
@@ -135,9 +137,11 @@
     return (want == lax.broadcasted_iota(jnp.int32, (want.shape[0], width), 1)).astype(BF16)
 
 
-EARLY = 640
-SLOTS = [(row, lane) for lane in range(EARLY, D, 128) for row in range(8)]
-GAINS = SLOTS[18:] + [(row, 512) for row in range(1, 5)]
+MISC = 4 * D
+LATE = 896
+WIDE = MISC + LATE + 768
+SLOTS = [(row, lane) for lane in range(LATE, LATE + 768, 128) for row in range(8)]
+GAINS = SLOTS[36:] + [(row, 640) for row in range(2, 8)]
 
 
 def weight_parts_kernel(
@@ -149,17 +153,19 @@
     o_rows = dot(one_hot(want_ref[...], D), o, 1, 1).astype(BF16)
     parts = (dot(hid_ref[...], dq, 1, 0), dot(o_rows, g, 1, 0))
     for m, part in enumerate(parts):
-        send_ref[:, m] = part[:512].reshape(64, 8, D).astype(BF16)
-        for b in range(9):
-            row, lane = SLOTS[9 * m + b]
-            at = lane - EARLY
-            scr[:, row, at : at + 128] = part[512:, 128 * b : 128 * b + 128]
-    for b in range(14):
+        for y in range(2):
+            at = (2 * y + m) * D
+            eight = part[256 * y : 256 * y + 256].reshape(32, 8, D)
+            send_ref[:, :, at : at + D] = eight.astype(BF16)
+            for b in range(9):
+                row, lane = SLOTS[9 * (2 * y + m) + b]
+                ninth = part[512 + 32 * y : 544 + 32 * y, 128 * b : 128 * b + 128]
+                scr[:, row, lane - LATE : lane - LATE + 128] = ninth
+    for b in range(12):
         row, lane = GAINS[b]
-        at = lane - EARLY
         block = gain_ref[:, 128 * b : 128 * b + 128]
-        scr[:, row, at : at + 128] = jnp.broadcast_to(block, (64, 128))
-    send_ref[:, 2, :, EARLY:] = scr[...].astype(BF16)
+        scr[:, row, lane - LATE : lane - LATE + 128] = jnp.broadcast_to(block, (32, 128))
+    send_ref[:, :, MISC + LATE :] = scr[...].astype(BF16)
 
 
 def weight_parts(*args):
@@ -168,8 +174,8 @@
         weight_parts_kernel,
         in_specs=[vmem] * 9,
         out_specs=vmem,
-        out_shape=jax.ShapeDtypeStruct((64, 3, 8, D), BF16),
-        scratch_shapes=[pltpu.VMEM((64, 8, D - EARLY), F32)],
+        out_shape=jax.ShapeDtypeStruct((32, 8, WIDE), BF16),
+        scratch_shapes=[pltpu.VMEM((32, 8, 768), F32)],
         name="weight_parts",
     )(*args)
 
@@ -208,8 +214,8 @@
         for out, c in ((mine_ref, core), (theirs_ref, 1 - core)):
             start = pl.multiple_of(n * 576 + c * 288, 32)
             out[n * 288 : n * 288 + 288] = scr[pl.ds(start, 288), :]
-    both = jnp.concatenate([x.astype(F32) for x in rounded] + [jnp.zeros((96, G), F32)], axis=0)
-    tok_ref[...] = both.T
+    tok_ref[:80] = rounded[0]
+    tok_ref[80:] = rounded[1]
 
 
 def image_sums(core, got, whole):
@@ -222,7 +228,7 @@
         out_shape=[
             jax.ShapeDtypeStruct((ROWS, 128), F32),
             jax.ShapeDtypeStruct((ROWS, 128), F32),
-            jax.ShapeDtypeStruct((G, 256), F32),
+            jax.ShapeDtypeStruct((160, G), BF16),
         ],
         scratch_shapes=[
             pltpu.VMEM((D, 128), F32),
@@ -234,123 +240,176 @@
     )(core, got, whole)
 
 
-def fill_rest_kernel(send_ref, mine_ref, got_ref, tok_ref, gain_ref, out_ref, scr):
-    scr[:, :, 512:EARLY] = jnp.zeros((64, 8, EARLY - 512), F32)
+def fill_rest_kernel(send_hbm, mine_ref, got_ref, tok_ref, gain_ref, out_hbm, scr, late, sem):
     total = mine_ref[...] + got_ref[...]
     high = total.astype(BF16)
     low = (total - high.astype(F32)).astype(BF16)
     want = eight_and_one(lax.broadcasted_iota(jnp.int32, (ROWS, ROWS), 0))
     order = (want == lax.broadcasted_iota(jnp.int32, (ROWS, ROWS), 1)).astype(BF16)
     moved = dot(order, jnp.concatenate([high, low], axis=1), 1, 0)
-    tok = tok_ref[...].reshape(32, 16, 256)
+    scr[:, :, 640:] = jnp.zeros((32, 8, LATE - 640), F32)
+    rows = jnp.concatenate([tok_ref[...].astype(F32), jnp.zeros((96, G), F32)], axis=0)
+    tok = rows.T.reshape(32, 16, 256)
     for half in range(2):
-        lanes = slice(160 * half + 160, 160 * half + 320)
+        scr[:, :, 160 * half : 160 * half + 160] = tok[:, 8 * half : 8 * half + 8, :160]
+    for y in range(2):
         for n in range(2):
-            scr[32 * n : 32 * n + 32, :, lanes] = tok[:, 8 * half : 8 * half + 8, :160]
-    for n in range(2):
-        piece = moved[:, 128 * n : 128 * n + 80]
-        scr[:, :, 80 * n : 80 * n + 80] = piece[:512].reshape(64, 8, 80)
-        scr[:, 0, 480 + 80 * n : 560 + 80 * n] = piece[512:]
-    for b in range(14, 18):
+            piece = moved[:, 128 * n : 128 * n + 80]
+            at = 320 + 160 * y + 80 * n
+            scr[:, :, at : at + 80] = piece[256 * y : 256 * y + 256].reshape(32, 8, 80)
+            scr[:, y, 640 + 80 * n : 720 + 80 * n] = piece[512 + 32 * y : 544 + 32 * y]
+    for b in range(12, 18):
         row, lane = GAINS[b]
         block = gain_ref[:, 128 * b : 128 * b + 128]
-        scr[:, row, lane : lane + 128] = jnp.broadcast_to(block, (64, 128))
-    out_ref[:, 0] = scr[...].astype(BF16)
+        scr[:, row, lane : lane + 128] = jnp.broadcast_to(block, (32, 128))
+    late[...] = scr[...].astype(BF16)
+    copy = pltpu.make_async_copy(late, out_hbm.at[:, :, pl.ds(MISC, LATE)], sem)
+    copy.start()
+    copy.wait()
 
 
 def fill_rest(send, mine, got, tok, gain):
     vmem = pl.BlockSpec(memory_space=pltpu.VMEM)
+    hbm = pl.BlockSpec(memory_space=pl.ANY)
     return pl.pallas_call(
         fill_rest_kernel,
-        grid=(1,),
-        in_specs=[pl.BlockSpec(memory_space=pl.ANY)] + [vmem] * 4,
-        out_specs=pl.BlockSpec((64, 1, 8, EARLY), lambda i: (0, 2, 0, 0)),
-        out_shape=jax.ShapeDtypeStruct((64, 3, 8, D), BF16),
-        scratch_shapes=[pltpu.VMEM((64, 8, EARLY), F32)],
+        in_specs=[hbm] + [vmem] * 4,
+        out_specs=hbm,
+        out_shape=jax.ShapeDtypeStruct((32, 8, WIDE), BF16),
+        scratch_shapes=[
+            pltpu.VMEM((32, 8, LATE), F32),
+            pltpu.VMEM((32, 8, LATE), BF16),
+            pltpu.SemaphoreType.DMA,
+        ],
         input_output_aliases={0: 0},
         name="fill_rest",
     )(send, mine, got, tok, gain)
 
 
-def finish_kernel(
-    yl_ref, recv_hbm, wk_hbm, wv_hbm, gw_ref, gg_ref, gain_ref, tok, kv, recv, wk, wv, sems
-):
+def group_sums_kernel(yl_ref, recv_hbm, keep_ref, give_ref, both, recv, sems):
     loads = []
     for part in range(4):
-        some = pl.ds(16 * part, 16)
+        some = pl.ds(8 * part, 8)
         loads.append(pltpu.make_async_copy(recv_hbm.at[some], recv.at[some], sems.at[part]))
-    late = [
-        pltpu.make_async_copy(wk_hbm, wk, sems.at[4]),
-        pltpu.make_async_copy(wv_hbm, wv, sems.at[5]),
-    ]
-    for copy in loads + late:
+    for copy in loads:
         copy.start()
-
-    def add(j, sums):
-        return tuple(s + recv[j, n].astype(F32) for n, s in enumerate(sums))
-
-    sums = tuple(jnp.zeros((8, D), F32) for _ in range(3))
+    sums = [None] * 4
     for part in range(4):
         loads[part].wait()
-        sums = lax.fori_loop(16 * part, 16 * part + 16, add, sums)
-    gw_ref[:8, 0] = sums[0]
-    gw_ref[:8, 3] = sums[1]
+    for n in range(4):
+
+        def add(t, total, n=n):
+            return total + recv[t, :, n * D : n * D + D].astype(F32)
+
+        sums[n] = lax.fori_loop(0, 32, add, jnp.zeros((8, D), F32))
+
+    def add_rest(t, total):
+        return total + recv[t, :, MISC + 640 :].astype(F32)
+
+    rest = lax.fori_loop(0, 32, add_rest, jnp.zeros((8, WIDE - MISC - 640), F32))
 
     def slot(place):
         row, lane = place
-        return sums[2][row : row + 1, lane : lane + 128]
-
-    for b in range(18):
-        at = 128 * (b % 9)
-        gw_ref[8:9, 3 * (b // 9), at : at + 128] = slot(SLOTS[b])
-    for b in range(9):
-        gain_ref[b : b + 1] = slot(GAINS[b]) + slot(GAINS[9 + b])
-    base = yl_ref[0] * 32
+        return rest[row : row + 1, lane - 640 : lane - 512]
+
+    for y in range(2):
+        for m in range(2):
+            both[y, 3 * m, :8] = sums[2 * y + m]
+            for b in range(9):
+                at = 128 * b
+                both[y, 3 * m, 8:9, at : at + 128] = slot(SLOTS[9 * (2 * y + m) + b])
+        for b in range(9):
+            at = 128 * b
+            both[y, 0, 9:10, at : at + 128] = slot(GAINS[b]) + slot(GAINS[9 + b])
     for t in range(32):
         cols = slice(36 * t, 36 * t + 36)
-        x = recv[t, 2, :, :EARLY].astype(F32) + recv[32 + t, 2, :, :EARLY].astype(F32)
-        eight = x[:, :80] + x[:, 80:160]
-        one = x[:1, 480:560] + x[:1, 560:640]
-        near = recv[base + t, 2, :, 128:512].astype(F32)
+        x = recv[t, :, MISC + 256 : MISC + LATE].astype(F32)
+        for y in range(2):
+            at = 64 + 160 * y
+            eight = x[:, at : at + 80] + x[:, at + 80 : at + 160]
+            one = x[y : y + 1, 384:464] + x[y : y + 1, 464:544]
+            for n in range(2):
+                both[y, 1 + n, :8, cols] = eight[:, 40 * n : 40 * n + 36]
+                both[y, 1 + n, 8:9, cols] = one[:, 40 * n : 40 * n + 36]
+    for out, y in ((keep_ref, yl_ref[0]), (give_ref, 1 - yl_ref[0])):
+        for m in range(4):
+            out[:, m] = both[y, m, :10]
+
+
+def group_sums(yl, recv):
+    vmem = pl.BlockSpec(memory_space=pltpu.VMEM)
+    return pl.pallas_call(
+        group_sums_kernel,
+        in_specs=[pl.BlockSpec(memory_space=pltpu.SMEM), pl.BlockSpec(memory_space=pl.ANY)],
+        out_specs=[vmem] * 2,
+        out_shape=[jax.ShapeDtypeStruct((10, 4, D), F32)] * 2,
+        scratch_shapes=[
+            pltpu.VMEM((2, 4, 16, D), F32),
+            pltpu.VMEM((32, 8, WIDE), BF16),
+            pltpu.SemaphoreType.DMA((4,)),
+        ],
+        name="group_sums",
+    )(yl, recv)
+
+
+def both_sums_kernel(keep_ref, got_ref, gw_ref, gain_ref):
+    gw_ref[...] = keep_ref[:9] + got_ref[:9]
+    gain = keep_ref[9, :1] + got_ref[9, :1]
+    for b in range(9):
+        gain_ref[b : b + 1] = gain[:, 128 * b : 128 * b + 128]
+
+
+def both_sums(keep, got):
+    vmem = pl.BlockSpec(memory_space=pltpu.VMEM)
+    return pl.pallas_call(
+        both_sums_kernel,
+        in_specs=[vmem] * 2,
+        out_specs=[vmem] * 2,
+        out_shape=[jax.ShapeDtypeStruct((9, 4, D), F32), jax.ShapeDtypeStruct((9, 128), F32)],
+        name="both_sums",
+    )(keep, got)
+
+
+def guide_grad_kernel(recv_hbm, wk_hbm, wv_hbm, gg_ref, tok, recv, wk, wv, sems):
+    copies = [
+        pltpu.make_async_copy(recv_hbm.at[:, :, pl.ds(MISC, 384)], recv, sems.at[0]),
+        pltpu.make_async_copy(wk_hbm, wk, sems.at[1]),
+        pltpu.make_async_copy(wv_hbm, wv, sems.at[2]),
+    ]
+    for copy in copies:
+        copy.start()
+    copies[0].wait()
+    for t in range(32):
+        near = recv[t].astype(F32)
         for n in range(2):
-            kv[n, :8, cols] = eight[:, 40 * n : 40 * n + 36]
-            kv[n, 8:9, cols] = one[:, 40 * n : 40 * n + 36]
             for half in range(2):
                 for m in range(2):
-                    lane = 32 + 160 * half + 80 * m + 40 * n
+                    lane = 160 * half + 80 * m + 40 * n
                     row = 16 * m + 8 * half
-                    tok[n, row : row + 8, cols] = near[:, lane : lane + 36]
-    for n in range(2):
-        gw_ref[:8, 1 + n] = kv[n, :8]
-        gw_ref[8:9, 1 + n] = kv[n, 8:9]
-    for copy in late:
-        copy.wait()
-    grad = dot(tok[0].astype(BF16), wk[...], 1, 1) + dot(tok[1].astype(BF16), wv[...], 1, 1)
-    gg_ref[...] = grad.astype(BF16)
-
-
-def finish(yl, recv, w_key, w_value):
-    vmem = pl.BlockSpec(memory_space=pltpu.VMEM)
+                    tok[n, row : row + 8, 36 * t : 36 * t + 36] = near[:, lane : lane + 36]
+    copies[1].wait()
+    grad = dot(wk[...], tok[0].astype(BF16), 1, 1)
+    copies[2].wait()
+    grad = grad + dot(wv[...], tok[1].astype(BF16), 1, 1)
+    gg_ref[...] = grad.T.astype(BF16)
+
+
+def guide_grad(recv, w_key, w_value):
     hbm = pl.BlockSpec(memory_space=pl.ANY)
     return pl.pallas_call(
-        finish_kernel,
-        in_specs=[pl.BlockSpec(memory_space=pltpu.SMEM), hbm, hbm, hbm],
-        out_specs=[vmem] * 3,
-        out_shape=[
-            jax.ShapeDtypeStruct((9, 4, D), F32),
-            jax.ShapeDtypeStruct((32, D), BF16),
-            jax.ShapeDtypeStruct((9, 128), F32),
-        ],
+        guide_grad_kernel,
+        in_specs=[hbm] * 3,
+        out_specs=pl.BlockSpec(memory_space=pltpu.VMEM),
+        out_shape=jax.ShapeDtypeStruct((32, D), BF16),
         scratch_shapes=[
             pltpu.VMEM((2, 32, D), F32),
-            pltpu.VMEM((2, 16, D), F32),
-            pltpu.VMEM((64, 3, 8, D), BF16),
+            pltpu.VMEM((32, 8, 384), BF16),
             pltpu.VMEM((D, D), BF16),
             pltpu.VMEM((D, D), BF16),
-            pltpu.SemaphoreType.DMA((6,)),
-        ],
-        name="finish",
-    )(yl, recv, w_key, w_value)
+            pltpu.SemaphoreType.DMA((3,)),
+        ],
+        name="guide_grad",
+    )(recv, w_key, w_value)
 
 
 def on_device(tiles, tile_image, guide, gain, w_query, w_key, w_value, w_out, grad_out):
@@ -388,10 +447,11 @@
     got, send = lax.optimization_barrier((got, send))
     mine, theirs, tok = image_sums(core[None], got, whole)
     send = fill_rest(send, mine, lax.ppermute(theirs, "c", SWAP), tok, gains)
-    recv = lax.all_to_all(send, CHIP_AXES, 0, 0, tiled=True)
-    grad_weights, grad_guide, grad_gain = finish(yl[None], recv, w_key, w_value)
-    grad_weights = grad_weights.transpose(1, 0, 2)
-    return (grad_tiles, grad_guide.reshape(guide.shape), grad_weights, grad_gain.reshape(D))
+    recv = lax.all_to_all(send, TILE_AXES, 0, 0, tiled=True)
+    keep, give = group_sums(yl[None], recv)
+    grad_weights, grad_gain = both_sums(keep, lax.ppermute(give, "yl", SWAP))
+    grad_guide = guide_grad(recv, w_key, w_value).reshape(guide.shape)
+    return (grad_tiles, grad_guide, grad_weights.transpose(1, 0, 2), grad_gain.reshape(D))
 
 
 def solution(mesh):

time: 185 us -> 184 us (level)
  Pallas kernels: 43.5 us -> 48.9 us
  local copies, waits for them, and re-layouts: 7.13 us -> 2.26 us
    pallas_call x3 -> x5, Pallas kernels: 12.1 us -> 17.9 us  [the longest x1 5.89 us: group_sums(): pl.pallas_call(group_sums_kernel, in_specs=[pl.BlockSpec(memory_space=plt...]
    unnamed x26 -> x22, local copies, waits for them, and re-layouts: 7.13 us -> 2.25 us
    all_to_all x1, waiting for transfers between devices: 43.4 us -> 40.6 us  [on_device(): recv = lax.all_to_all(send, TILE_AXES, 0, 0, tiled=True)]
    all_to_all x1, waiting for transfers between devices: 15.8 us -> 17.9 us  [on_device(): got = lax.all_to_all(pay, TILE_AXES, 0, 0, tiled=True)]
  transfers between devices with their start and end apart: 9 -> 10, of which waited for: 5 -> 5; matrix products, arithmetic and copies ran while one was open for 10% -> 9% of each run, Pallas kernels for 4% -> 6%
where the time goes in v7:
time: 184 us; the launch traced here: 181 us
  waiting for transfers between devices  82.2 us (45%)
  Pallas kernels  48.9 us (27%)
  starting transfers between devices  29.5 us (16%)
  matrix products  11.2 us (6%)
  other arithmetic  5.32 us (3%)
  local copies, waits for them, and re-layouts  2.26 us (1%)
    all_to_all x1, waiting for transfers between devices, on_device(): recv = lax.all_to_all(send, TILE_AXES, 0, 0, tiled=True)  40.6 us
    all_to_all x1, waiting for transfers between devices, on_device(): whole = lax.all_to_all(copies_of(guide), TILE_AXES, 0, 0, tiled=True)  20.1 us
    pallas_call x1, Pallas kernels, attention(): pl.pallas_call(attention_kernel, in_specs=[pl.BlockSpec(memory_space=pltp...  19.9 us
    all_to_all x1, waiting for transfers between devices, on_device(): got = lax.all_to_all(pay, TILE_AXES, 0, 0, tiled=True)  17.9 us
    all_to_all x1, starting transfers between devices, on_device(): whole = lax.all_to_all(copies_of(guide), TILE_AXES, 0, 0, tiled=True)  11.3 us
    dot_general x4, matrix products, dot(): lax.dot_general(a, b, (((ca,), (cb,)), ((), ())), preferred_element_type=...  11.2 us
    all_to_all x1, starting transfers between devices, on_device(): recv = lax.all_to_all(send, TILE_AXES, 0, 0, tiled=True)  8.63 us
    all_to_all x1, starting transfers between devices, on_device(): got = lax.all_to_all(pay, TILE_AXES, 0, 0, tiled=True)  8.37 us
  transfers between devices with their start and end apart: 10, of which 5 were waited for; matrix products, arithmetic and copies ran while one was open for 9% of the time, Pallas kernels for 6%

profile of v7, /device:TPU:2, one launch (start us, length us, event | category | flops | bytes accessed | tf_op | source)
XLA Modules:
  0.0 180.8 jit_solution(4443550280610665798)
XLA Ops:
  0.6 0.0 copy-start
  0.6 2.8 %copies_of_guide.1 = bf16[32,2,16,1152]{3,2,1,0:T(8,128)(2,1)} custom-call(bf16[2,16,1152]{2,1,0:T(8,128)(2,1)} %g_ref.2), custom_call_target="tpu_custom_call" | custom-call | tf_op jit(solution)/shard_map/copies_of_guide/pallas_call | solution.py:31
  3.4 0.0 copy-start.1
  3.4 0.0 copy-start.9
  3.4 11.3 %all-to-all-start = ((bf16[32,2,16,1152]{3,2,1,0:T(8,128)(2,1)}), bf16[32,2,16,1152]{3,2,1,0:T(8,128)(2,1)}, u32[]{:S(2)}, u32[]{:S(2)}) async-start(bf16[32,2,16,1152]{3,2,1,0:T(8,128)(2,1)} %copies_of_guide.1), calls=%async_computation | async-start | bytes 4718592 | tf_op jit(solution)/shard_map/all_to_all | solution.py:418
  14.7 0.0 copy-done.1
  14.7 0.2 fusion.13
  14.9 0.0 copy-done.9
  15.0 1.0 fusion.7
  16.0 0.0 collective-permute-start
  16.7 0.0 copy-done
  16.7 0.0 copy-start.2
  16.7 0.0 copy-start.10
  16.7 3.0 %convolution_convert_fusion.1.q_ref = bf16[256,1152]{1,0:T(8,128)(2,1)} fusion(bf16[256,1152]{1,0:T(8,128)(2,1)} %fusion.7, bf16[1152,1152]{1,0:T(8,128)(2,1)S(1)} %copy-done), kind=kOutput, calls=%fused_computation.3 | convolution fusion | flops 679772160 | bytes 3833856 | tf_op jit(solution)/shard_map/dot_general | solution.py:19
  19.7 0.0 copy-done.2
  19.7 0.0 copy-done.10
  19.7 1.9 %convolution_convert_fusion.d_ref = bf16[256,1152]{1,0:T(8,128)(2,1)} fusion(bf16[256,1152]{1,0:T(8,128)(2,1)S(1)} %copy-done.2, bf16[1152,1152]{1,0:T(8,128)(2,1)S(1)} %copy-done.10), kind=kOutput, calls=%fused_computation.2 | convolution fusion | flops 679772160 | bytes 3833856 | tf_op jit(solution)/shard_map/dot_general | solution.py:19
  21.6 0.0 collective-permute-done
  21.6 3.1 %fusion.6.hid_ref = bf16[576,512]{1,0:T(8,128)(2,1)} fusion(s32[576]{0:T(1024)S(1)} %fusion.44, bf16[256,1152]{1,0:T(8,128)(2,1)} %collective-permute-done, bf16[256,1152]{1,0:T(8,128)(2,1)} %fusion.7), kind=kOutput, calls=%fused_computation.11 | convolution fusion | flops 682795008 | bytes 1771776 | tf_op jit(solution)/shard_map/dot_general | solution.py:19
  24.7 20.1 %all-to-all-done.g_hbm = bf16[32,2,16,1152]{3,2,1,0:T(8,128)(2,1)} async-done(((bf16[32,2,16,1152]{3,2,1,0:T(8,128)(2,1)}), bf16[32,2,16,1152]{3,2,1,0:T(8,128)(2,1)}, u32[]{:S(2)}, u32[]{:S(2)}) %all-to-all-start) | async-done | bytes 2359328 | tf_op jit(solution)/shard_map/all_to_all | solution.py:418
  44.8 19.9 %attention.1 = (bf16[32,2,40,512]{3,2,1,0:T(8,128)(2,1)}, bf16[256,1152]{1,0:T(8,128)(2,1)}, bf16[256,1152]{1,0:T(8,128)(2,1)}) custom-call(s32[1]{0:T(128)S(6)} %copy.15.img_ref, bf16[32,2,16,1152]{3,2,1,0:T(8,128)(2,1)} %all-to-all-done.g_hbm, bf16[1152,1152]{1,0:T(8,128)(2,1)} %wk_hbm.3, bf16[1152,1152]{1,0:T(8,128)(2,1)} %wv_hbm.3, ...), custom_call_target="tpu_custom_call" | custom-call | tf_op jit(solution)/shard_map/attention/pallas_call | solution.py:101
  64.7 8.4 %all-to-all-start.1 = ((bf16[32,2,40,512]{3,2,1,0:T(8,128)(2,1)}), bf16[32,2,40,512]{3,2,1,0:T(8,128)(2,1)}, u32[]{:S(2)}, u32[]{:S(2)}) async-start(bf16[32,2,40,512]{3,2,1,0:T(8,128)(2,1)} %get-tuple-element.20), calls=%async_computation.1 | async-start | bytes 5242880 | tf_op jit(solution)/shard_map/all_to_all | solution.py:432
  73.1 0.1 collective-permute-start.3
  73.2 0.0 copy-start.4
  73.2 0.0 copy-start.3
  73.2 3.2 %fusion.12 = (f32[1152]{0:T(1024)S(1)}, f32[256]{0:T(256)S(1)}, f32[256,1152]{1,0:T(8,128)}) fusion(bf16[256,1152]{1,0:T(8,128)(2,1)S(1)} %copy-done.1, f32[256]{0:T(256)S(1)} %add_rsqrt_fusion, f32[1152]{0:T(1024)S(1)} %copy-done.9, bf16[256,1152]{1,0:T(8,128)(2,1)} %get-tuple-element.19.dq_ref, bf16[1152,1152]{1,0:T(8,128)(2,1)S(1)} %copy-done), kind=kOutput, calls=%fused_computation.17 | convolution fusion | flops 681540224 | bytes 5024768 | tf_op jit(solution)/shard_map/dot_general | solution.py:19
  76.5 0.5 collective-permute-start.4
  76.9 1.1 fusion.28.want_ref
  78.0 0.0 copy-done.4
  78.0 0.1 collective-permute-start.2
  78.1 0.0 copy-done.3
  78.1 0.5 collective-permute-start.1
  78.5 0.0 collective-permute-done.4
  78.5 0.6 pad_maximum_fusion.gain_ref
  79.2 0.0 collective-permute-done.3.g2_ref
  79.2 0.0 copy-start.5
  79.2 1.7 collective-permute-done.1.o2_ref
  80.9 0.0 copy-done.5
  80.9 0.0 copy-start.6
  80.9 0.8 copy-done.6
  81.7 0.0 collective-permute-done.2.dq2_ref
  81.7 6.6 %weight_parts.1.send_hbm = bf16[32,8,6272]{2,1,0:T(8,128)(2,1)} custom-call(s32[576,1]{1,0:T(8,128)} %fusion.28.want_ref, bf16[576,512]{1,0:T(8,128)(2,1)} %fusion.6.hid_ref, bf16[256,1152]{1,0:T(8,128)(2,1)} %get-tuple-element.22.o_ref, bf16[256,1152]{1,0:T(8,128)(2,1)} %copy-done.6, bf16[256,1152]{1,0:T(8,128)(2,1)} %get-tuple-element.19.dq_ref, ...), custom_call_target="tpu_custom_call" | custom-call | tf_op jit(solution)/shard_map/weight_parts/pallas_call | solution.py:173
  88.3 17.9 %all-to-all-done.1.got_hbm = bf16[32,2,40,512]{3,2,1,0:T(8,128)(2,1)} async-done(((bf16[32,2,40,512]{3,2,1,0:T(8,128)(2,1)}), bf16[32,2,40,512]{3,2,1,0:T(8,128)(2,1)}, u32[]{:S(2)}, u32[]{:S(2)}) %all-to-all-start.1) | async-done | bytes 2621472 | tf_op jit(solution)/shard_map/all_to_all | solution.py:432
  106.2 4.5 %image_sums.1 = (f32[576,128]{1,0:T(8,128)}, f32[576,128]{1,0:T(8,128)}, bf16[160,512]{1,0:T(8,128)(2,1)}) custom-call(s32[1]{0:T(128)} %bitcast.core_ref, bf16[32,2,40,512]{3,2,1,0:T(8,128)(2,1)} %all-to-all-done.1.got_hbm, bf16[32,2,16,1152]{3,2,1,0:T(8,128)(2,1)} %all-to-all-done.g_hbm), custom_call_target="tpu_custom_call" | custom-call | tf_op jit(solution)/shard_map/image_sums/pallas_call | solution.py:224
  110.7 0.1 collective-permute-start.5
  110.8 1.8 collective-permute-done.5.got_ref
  112.6 0.0 copy-start.7
  112.6 0.7 copy-done.7
  113.3 2.6 %fill_rest.1 = bf16[32,8,6272]{2,1,0:T(8,128)(2,1)} custom-call(bf16[32,8,6272]{2,1,0:T(8,128)(2,1)} %weight_parts.1.send_hbm, f32[576,128]{1,0:T(8,128)} %get-tuple-element.25.mine_ref, f32[576,128]{1,0:T(8,128)} %copy-done.7, bf16[160,512]{1,0:T(8,128)(2,1)} %get-tuple-element.27.tok_ref, ...), custom_call_target="tpu_custom_call", output_to_operand_aliasing={{}: (0, {})} | custom-call | tf_op jit(solution)/shard_map/fill_rest/pallas_call | solution.py:274
  115.9 8.6 %all-to-all-start.2 = ((bf16[32,8,6272]{2,1,0:T(8,128)(2,1)}), bf16[32,8,6272]{2,1,0:T(8,128)(2,1)}, u32[]{:S(2)}, u32[]{:S(2)}) async-start(bf16[32,8,6272]{2,1,0:T(8,128)(2,1)} %fill_rest.1), calls=%async_computation.2 | async-start | bytes 6422528 | tf_op jit(solution)/shard_map/all_to_all | solution.py:450
  124.6 40.6 %all-to-all-done.2.recv_hbm = bf16[32,8,6272]{2,1,0:T(8,128)(2,1)} async-done(((bf16[32,8,6272]{2,1,0:T(8,128)(2,1)}), bf16[32,8,6272]{2,1,0:T(8,128)(2,1)}, u32[]{:S(2)}, u32[]{:S(2)}) %all-to-all-start.2) | async-done | bytes 3211296 | tf_op jit(solution)/shard_map/all_to_all | solution.py:450
  165.1 5.9 %group_sums.1 = (f32[10,4,1152]{2,1,0:T(4,128)}, f32[10,4,1152]{2,1,0:T(4,128)}) custom-call(s32[1]{0:T(128)} %bitcast.2.yl_ref, bf16[32,8,6272]{2,1,0:T(8,128)(2,1)} %all-to-all-done.2.recv_hbm), custom_call_target="tpu_custom_call" | custom-call | tf_op jit(solution)/shard_map/group_sums/pallas_call | solution.py:341
  171.0 0.1 collective-permute-start.6
  171.1 2.4 %fusion.11 = bf16[256,1152]{1,0:T(8,128)(2,1)} fusion(bf16[256,1152]{1,0:T(8,128)(2,1)S(1)} %copy-done.1, f32[256,1152]{1,0:T(8,128)} %get-tuple-element.36, f32[256]{0:T(256)S(1)} %broadcast_multiply_fusion, f32[1152]{0:T(1024)S(1)} %copy-done.9, f32[256]{0:T(256)S(1)} %add_rsqrt_fusion), kind=kLoop, calls=%fused_computation.16 | loop fusion | flops 2064384 | bytes 2365952 | tf_op jit(solution)/shard_map/convert_element_type | solution.py:445
  173.5 4.9 %guide_grad.1 = bf16[32,1152]{1,0:T(8,128)(2,1)} custom-call(bf16[32,8,6272]{2,1,0:T(8,128)(2,1)} %all-to-all-done.2.recv_hbm, bf16[1152,1152]{1,0:T(8,128)(2,1)} %wk_hbm.3, bf16[1152,1152]{1,0:T(8,128)(2,1)} %wv_hbm.3), custom_call_target="tpu_custom_call" | custom-call | tf_op jit(solution)/shard_map/guide_grad/pallas_call | solution.py:399
  178.4 0.0 collective-permute-done.6.got_ref
  178.4 0.0 copy-start.8
  178.5 0.7 copy-done.8
  179.1 1.7 both_sums.1
  (5 shorter events, 0.0 us)
Async XLA Ops:
  0.6 16.0 %copy-start = (bf16[1152,1152]{1,0:T(8,128)(2,1)S(1)}, bf16[1152,1152]{1,0:T(8,128)(2,1)}, u32[]{:S(2)}) copy-start(bf16[1152,1152]{1,0:T(8,128)(2,1)} %param.13) | copy-start | bytes 7962628
  3.4 11.3 %copy-start.1 = (bf16[256,1152]{1,0:T(8,128)(2,1)S(1)}, bf16[256,1152]{1,0:T(8,128)(2,1)}, u32[]{:S(2)}) copy-start(bf16[256,1152]{1,0:T(8,128)(2,1)} %param.9) | copy-start | bytes 1769476
  3.4 11.5 %copy-start.9 = (f32[1152]{0:T(1024)S(1)}, f32[1152]{0:T(1024)}, u32[]{:S(2)}) copy-start(f32[1152]{0:T(1024)} %param.12) | copy-start | bytes 13828
  3.4 41.4 %all-to-all-start = ((bf16[32,2,16,1152]{3,2,1,0:T(8,128)(2,1)}), bf16[32,2,16,1152]{3,2,1,0:T(8,128)(2,1)}, u32[]{:S(2)}, u32[]{:S(2)}) async-start(bf16[32,2,16,1152]{3,2,1,0:T(8,128)(2,1)} %copies_of_guide.1), calls=%async_computation | async-start | bytes 4718592 | tf_op jit(solution)/shard_map/all_to_all | solution.py:418
  16.0 5.6 %collective-permute-start = (bf16[256,1152]{1,0:T(8,128)(2,1)}, bf16[256,1152]{1,0:T(8,128)(2,1)}, u32[]{:S(2)}, u32[]{:S(2)}) collective-permute-start(bf16[256,1152]{1,0:T(8,128)(2,1)} %fusion.7), channel_id=1, source_target_pairs={{0,32},{32,0},{1,33},{33,1},{2,34},{34,2},{3,35},{35,3},{4,36},{36... | collective-permute-start | bytes 1769480 | tf_op jit(solution)/shard_map/ppermute | solution.py:426
  16.7 3.1 %copy-start.2 = (bf16[256,1152]{1,0:T(8,128)(2,1)S(1)}, bf16[256,1152]{1,0:T(8,128)(2,1)}, u32[]{:S(2)}) copy-start(bf16[256,1152]{1,0:T(8,128)(2,1)} %g_ref.3) | copy-start | bytes 1769476
  16.7 3.1 %copy-start.10 = (bf16[1152,1152]{1,0:T(8,128)(2,1)S(1)}, bf16[1152,1152]{1,0:T(8,128)(2,1)}, u32[]{:S(2)}) copy-start(bf16[1152,1152]{1,0:T(8,128)(2,1)} %param.16) | copy-start | bytes 7962628
  64.7 41.5 %all-to-all-start.1 = ((bf16[32,2,40,512]{3,2,1,0:T(8,128)(2,1)}), bf16[32,2,40,512]{3,2,1,0:T(8,128)(2,1)}, u32[]{:S(2)}, u32[]{:S(2)}) async-start(bf16[32,2,40,512]{3,2,1,0:T(8,128)(2,1)} %get-tuple-element.20), calls=%async_computation.1 | async-start | bytes 5242880 | tf_op jit(solution)/shard_map/all_to_all | solution.py:432
  73.1 6.0 %collective-permute-start.3 = (bf16[256,1152]{1,0:T(8,128)(2,1)}, bf16[256,1152]{1,0:T(8,128)(2,1)S(1)}, u32[]{:S(2)}, u32[]{:S(2)}) collective-permute-start(bf16[256,1152]{1,0:T(8,128)(2,1)} %g_ref.3), channel_id=1, source_target_pairs={{0,32},{32,0},{1,33},{33,1},{2,34},{34,2},{3,35},{35,3},{4,36},{36... | collective-permute-start | bytes 1769480 | tf_op jit(solution)/shard_map/ppermute | solution.py:428
  73.2 4.8 %copy-start.4 = (bf16[256,1152]{1,0:T(8,128)(2,1)S(1)}, bf16[256,1152]{1,0:T(8,128)(2,1)}, u32[]{:S(2)}) copy-start(bf16[256,1152]{1,0:T(8,128)(2,1)} %get-tuple-element.19.dq_ref) | copy-start | bytes 1769476
  73.2 4.8 %copy-start.3 = (bf16[256,1152]{1,0:T(8,128)(2,1)S(1)}, bf16[256,1152]{1,0:T(8,128)(2,1)}, u32[]{:S(2)}) copy-start(bf16[256,1152]{1,0:T(8,128)(2,1)} %get-tuple-element.22.o_ref) | copy-start | bytes 1769476
  76.5 2.0 %collective-permute-start.4 = (f32[1,1152]{1,0:T(1,128)S(1)}, f32[1,1152]{1,0:T(1,128)S(1)}, u32[]{:S(2)}, u32[]{:S(2)}) collective-permute-start(f32[1,1152]{1,0:T(1,128)S(1)} %broadcast_in_dim.6), channel_id=1, source_target_pairs={{0,32},{32,0},{1,33},{33,1},{2,34},{34,2},{3,35},{35,3},{4,36},{36... | collective-permute-start | bytes 13832 | tf_op jit(solution)/shard_map/ppermute | solution.py:438
  78.0 3.7 %collective-permute-start.2 = (bf16[256,1152]{1,0:T(8,128)(2,1)S(1)}, bf16[256,1152]{1,0:T(8,128)(2,1)}, u32[]{:S(2)}, u32[]{:S(2)}) collective-permute-start(bf16[256,1152]{1,0:T(8,128)(2,1)S(1)} %copy-done.4), channel_id=1, source_target_pairs={{0,32},{32,0},{1,33},{33,1},{2,34},{34,2},{3,35},{35,3},{4,36},{36... | collective-permute-start | bytes 1769480 | tf_op jit(solution)/shard_map/ppermute | solution.py:434
  78.1 2.8 %collective-permute-start.1 = (bf16[256,1152]{1,0:T(8,128)(2,1)S(1)}, bf16[256,1152]{1,0:T(8,128)(2,1)S(1)}, u32[]{:S(2)}, u32[]{:S(2)}) collective-permute-start(bf16[256,1152]{1,0:T(8,128)(2,1)S(1)} %copy-done.3), channel_id=1, source_target_pairs={{0,32},{32,0},{1,33},{33,1},{2,34},{34,2},{3,35},{35,3},{4,36},{36... | collective-permute-start | bytes 1769480 | tf_op jit(solution)/shard_map/ppermute | solution.py:435
  79.2 1.7 copy-start.5
  80.9 0.8 copy-start.6
  110.7 1.9 %collective-permute-start.5 = (f32[576,128]{1,0:T(8,128)}, f32[576,128]{1,0:T(8,128)S(1)}, u32[]{:S(2)}, u32[]{:S(2)}) collective-permute-start(f32[576,128]{1,0:T(8,128)} %get-tuple-element.26), channel_id=1, source_target_pairs={{0,32},{32,0},{1,33},{33,1},{2,34},{34,2},{3,35},{35,3},{4,36},{36... | collective-permute-start | bytes 884744 | tf_op jit(solution)/shard_map/ppermute | solution.py:449
  112.6 0.7 copy-start.7
  115.9 49.2 %all-to-all-start.2 = ((bf16[32,8,6272]{2,1,0:T(8,128)(2,1)}), bf16[32,8,6272]{2,1,0:T(8,128)(2,1)}, u32[]{:S(2)}, u32[]{:S(2)}) async-start(bf16[32,8,6272]{2,1,0:T(8,128)(2,1)} %fill_rest.1), calls=%async_computation.2 | async-start | bytes 6422528 | tf_op jit(solution)/shard_map/all_to_all | solution.py:450
  171.0 7.4 %collective-permute-start.6 = (f32[10,4,1152]{2,1,0:T(4,128)}, f32[10,4,1152]{2,1,0:T(4,128)S(1)}, u32[]{:S(2)}, u32[]{:S(2)}) collective-permute-start(f32[10,4,1152]{2,1,0:T(4,128)} %get-tuple-element.29), channel_id=1, source_target_pairs={{0,64},{64,0},{1,65},{65,1},{2,66},{66,2},{3,67},{67,3},{4,68},{68... | collective-permute-start | bytes 552968 | tf_op jit(solution)/shard_map/ppermute | solution.py:452
  178.4 0.7 copy-start.8

commit v8 on v7

--- a/solution.py
+++ b/solution.py
@@ -293,20 +293,29 @@
         loads.append(pltpu.make_async_copy(recv_hbm.at[some], recv.at[some], sems.at[part]))
     for copy in loads:
         copy.start()
-    sums = [None] * 4
+    def add(t, totals):
+        sums = [x + recv[t, :, n * D : n * D + D].astype(F32) for n, x in enumerate(totals[:4])]
+        return (*sums, totals[4] + recv[t, :, MISC + 640 :].astype(F32))
+
+    def place_columns(t):
+        cols = slice(36 * t, 36 * t + 36)
+        x = recv[t, :, MISC + 256 : MISC + LATE].astype(F32)
+        for y in range(2):
+            at = 64 + 160 * y
+            eight = x[:, at : at + 80] + x[:, at + 80 : at + 160]
+            one = x[y : y + 1, 384:464] + x[y : y + 1, 464:544]
+            for n in range(2):
+                both[y, 1 + n, :8, cols] = eight[:, 40 * n : 40 * n + 36]
+                both[y, 1 + n, 8:9, cols] = one[:, 40 * n : 40 * n + 36]
+
+    sums = tuple(jnp.zeros((8, D), F32) for _ in range(4))
+    sums = (*sums, jnp.zeros((8, WIDE - MISC - 640), F32))
     for part in range(4):
         loads[part].wait()
-    for n in range(4):
-
-        def add(t, total, n=n):
-            return total + recv[t, :, n * D : n * D + D].astype(F32)
-
-        sums[n] = lax.fori_loop(0, 32, add, jnp.zeros((8, D), F32))
-
-    def add_rest(t, total):
-        return total + recv[t, :, MISC + 640 :].astype(F32)
-
-    rest = lax.fori_loop(0, 32, add_rest, jnp.zeros((8, WIDE - MISC - 640), F32))
+        sums = lax.fori_loop(8 * part, 8 * part + 8, add, sums)
+        for t in range(8 * part, 8 * part + 8):
+            place_columns(t)
+    rest = sums[4]
 
     def slot(place):
         row, lane = place
@@ -321,16 +330,6 @@
         for b in range(9):
             at = 128 * b
             both[y, 0, 9:10, at : at + 128] = slot(GAINS[b]) + slot(GAINS[9 + b])
-    for t in range(32):
-        cols = slice(36 * t, 36 * t + 36)
-        x = recv[t, :, MISC + 256 : MISC + LATE].astype(F32)
-        for y in range(2):
-            at = 64 + 160 * y
-            eight = x[:, at : at + 80] + x[:, at + 80 : at + 160]
-            one = x[y : y + 1, 384:464] + x[y : y + 1, 464:544]
-            for n in range(2):
-                both[y, 1 + n, :8, cols] = eight[:, 40 * n : 40 * n + 36]
-                both[y, 1 + n, 8:9, cols] = one[:, 40 * n : 40 * n + 36]
     for out, y in ((keep_ref, yl_ref[0]), (give_ref, 1 - yl_ref[0])):
         for m in range(4):
             out[:, m] = both[y, m, :10]
@@ -448,6 +447,7 @@
     mine, theirs, tok = image_sums(core[None], got, whole)
     send = fill_rest(send, mine, lax.ppermute(theirs, "c", SWAP), tok, gains)
     recv = lax.all_to_all(send, TILE_AXES, 0, 0, tiled=True)
+    recv, grad_tiles = lax.optimization_barrier((recv, grad_tiles))
     keep, give = group_sums(yl[None], recv)
     grad_weights, grad_gain = both_sums(keep, lax.ppermute(give, "yl", SWAP))
     grad_guide = guide_grad(recv, w_key, w_value).reshape(guide.shape)

time: 184 us -> 180 us (0.978)
  Pallas kernels: 48.9 us -> 46.5 us
    all_to_all x1, waiting for transfers between devices: 40.6 us -> 38.2 us  [on_device(): recv = lax.all_to_all(send, TILE_AXES, 0, 0, tiled=True)]
    pallas_call x1, Pallas kernels: 5.89 us -> 3.55 us  [group_sums(): pl.pallas_call(group_sums_kernel, in_specs=[pl.BlockSpec(memory_space=plt...]
  transfers between devices with their start and end apart: 10 -> 10, of which waited for: 5 -> 6; matrix products, arithmetic and copies ran while one was open for 9% -> 9% of each run, Pallas kernels for 6% -> 6%
where the time goes in v8:
time: 180 us; the launch traced here: 177 us
  waiting for transfers between devices  80.6 us (45%)
  Pallas kernels  46.5 us (26%)
  starting transfers between devices  29.5 us (16%)
  matrix products  11.2 us (6%)
  other arithmetic  5.32 us (3%)
  local copies, waits for them, and re-layouts  2.26 us (1%)
    all_to_all x1, waiting for transfers between devices, on_device(): recv = lax.all_to_all(send, TILE_AXES, 0, 0, tiled=True)  38.2 us
    all_to_all x1, waiting for transfers between devices, on_device(): whole = lax.all_to_all(copies_of(guide), TILE_AXES, 0, 0, tiled=True)  20.1 us
    pallas_call x1, Pallas kernels, attention(): pl.pallas_call(attention_kernel, in_specs=[pl.BlockSpec(memory_space=pltp...  19.9 us
    all_to_all x1, waiting for transfers between devices, on_device(): got = lax.all_to_all(pay, TILE_AXES, 0, 0, tiled=True)  17.9 us
    all_to_all x1, starting transfers between devices, on_device(): whole = lax.all_to_all(copies_of(guide), TILE_AXES, 0, 0, tiled=True)  11.3 us
    dot_general x4, matrix products, dot(): lax.dot_general(a, b, (((ca,), (cb,)), ((), ())), preferred_element_type=...  11.2 us
    all_to_all x1, starting transfers between devices, on_device(): recv = lax.all_to_all(send, TILE_AXES, 0, 0, tiled=True)  8.63 us
    all_to_all x1, starting transfers between devices, on_device(): got = lax.all_to_all(pay, TILE_AXES, 0, 0, tiled=True)  8.37 us
  transfers between devices with their start and end apart: 10, of which 6 were waited for; matrix products, arithmetic and copies ran while one was open for 9% of the time, Pallas kernels for 6%

profile of v8, /device:TPU:2, one launch (start us, length us, event | category | flops | bytes accessed | tf_op | source)
XLA Modules:
  0.0 176.9 jit_solution(10876683529569280080)
XLA Ops:
  0.6 0.0 copy-start
  0.6 2.8 %copies_of_guide.1 = bf16[32,2,16,1152]{3,2,1,0:T(8,128)(2,1)} custom-call(bf16[2,16,1152]{2,1,0:T(8,128)(2,1)} %g_ref.2), custom_call_target="tpu_custom_call" | custom-call | tf_op jit(solution)/shard_map/copies_of_guide/pallas_call | solution.py:31
  3.4 0.0 copy-start.1
  3.4 0.0 copy-start.9
  3.4 11.3 %all-to-all-start = ((bf16[32,2,16,1152]{3,2,1,0:T(8,128)(2,1)}), bf16[32,2,16,1152]{3,2,1,0:T(8,128)(2,1)}, u32[]{:S(2)}, u32[]{:S(2)}) async-start(bf16[32,2,16,1152]{3,2,1,0:T(8,128)(2,1)} %copies_of_guide.1), calls=%async_computation | async-start | bytes 4718592 | tf_op jit(solution)/shard_map/all_to_all | solution.py:417
  14.7 0.0 copy-done.1
  14.7 0.2 fusion.13
  14.9 0.0 copy-done.9
  15.0 1.0 fusion.7
  16.0 0.0 collective-permute-start
  16.7 0.0 copy-done
  16.7 0.0 copy-start.2
  16.7 0.0 copy-start.10
  16.7 3.0 %convolution_convert_fusion.1.q_ref = bf16[256,1152]{1,0:T(8,128)(2,1)} fusion(bf16[256,1152]{1,0:T(8,128)(2,1)} %fusion.7, bf16[1152,1152]{1,0:T(8,128)(2,1)S(1)} %copy-done), kind=kOutput, calls=%fused_computation.3 | convolution fusion | flops 679772160 | bytes 3833856 | tf_op jit(solution)/shard_map/dot_general | solution.py:19
  19.7 0.0 copy-done.2
  19.7 0.0 copy-done.10
  19.7 1.9 %convolution_convert_fusion.d_ref = bf16[256,1152]{1,0:T(8,128)(2,1)} fusion(bf16[256,1152]{1,0:T(8,128)(2,1)S(1)} %copy-done.2, bf16[1152,1152]{1,0:T(8,128)(2,1)S(1)} %copy-done.10), kind=kOutput, calls=%fused_computation.2 | convolution fusion | flops 679772160 | bytes 3833856 | tf_op jit(solution)/shard_map/dot_general | solution.py:19
  21.6 0.0 collective-permute-done
  21.6 3.1 %fusion.6.hid_ref = bf16[576,512]{1,0:T(8,128)(2,1)} fusion(s32[576]{0:T(1024)S(1)} %fusion.44, bf16[256,1152]{1,0:T(8,128)(2,1)} %collective-permute-done, bf16[256,1152]{1,0:T(8,128)(2,1)} %fusion.7), kind=kOutput, calls=%fused_computation.11 | convolution fusion | flops 682795008 | bytes 1771776 | tf_op jit(solution)/shard_map/dot_general | solution.py:19
  24.7 20.1 %all-to-all-done.g_hbm = bf16[32,2,16,1152]{3,2,1,0:T(8,128)(2,1)} async-done(((bf16[32,2,16,1152]{3,2,1,0:T(8,128)(2,1)}), bf16[32,2,16,1152]{3,2,1,0:T(8,128)(2,1)}, u32[]{:S(2)}, u32[]{:S(2)}) %all-to-all-start) | async-done | bytes 2359328 | tf_op jit(solution)/shard_map/all_to_all | solution.py:417
  44.8 19.9 %attention.1 = (bf16[32,2,40,512]{3,2,1,0:T(8,128)(2,1)}, bf16[256,1152]{1,0:T(8,128)(2,1)}, bf16[256,1152]{1,0:T(8,128)(2,1)}) custom-call(s32[1]{0:T(128)S(6)} %copy.15.img_ref, bf16[32,2,16,1152]{3,2,1,0:T(8,128)(2,1)} %all-to-all-done.g_hbm, bf16[1152,1152]{1,0:T(8,128)(2,1)} %wk_hbm.3, bf16[1152,1152]{1,0:T(8,128)(2,1)} %wv_hbm.3, ...), custom_call_target="tpu_custom_call" | custom-call | tf_op jit(solution)/shard_map/attention/pallas_call | solution.py:101
  64.7 8.4 %all-to-all-start.1 = ((bf16[32,2,40,512]{3,2,1,0:T(8,128)(2,1)}), bf16[32,2,40,512]{3,2,1,0:T(8,128)(2,1)}, u32[]{:S(2)}, u32[]{:S(2)}) async-start(bf16[32,2,40,512]{3,2,1,0:T(8,128)(2,1)} %get-tuple-element.21), calls=%async_computation.1 | async-start | bytes 5242880 | tf_op jit(solution)/shard_map/all_to_all | solution.py:431
  73.1 0.1 collective-permute-start.3
  73.2 0.0 copy-start.4
  73.2 0.0 copy-start.3
  73.2 3.2 %fusion.9 = (f32[256]{0:T(256)S(1)}, f32[1152]{0:T(1024)S(1)}, f32[256,1152]{1,0:T(8,128)}) fusion(bf16[256,1152]{1,0:T(8,128)(2,1)S(1)} %copy-done.1, f32[1152]{0:T(1024)S(1)} %copy-done.9, f32[256]{0:T(256)S(1)} %add_rsqrt_fusion, bf16[256,1152]{1,0:T(8,128)(2,1)} %get-tuple-element.24.dq_ref, bf16[1152,1152]{1,0:T(8,128)(2,1)S(1)} %copy-done), kind=kOutput, calls=%fused_computation.14 | convolution fusion | flops 681540224 | bytes 5024768 | tf_op jit(solution)/shard_map/dot_general | solution.py:19
  76.5 0.5 collective-permute-start.4
  76.9 1.1 fusion.28.want_ref
  78.0 0.0 copy-done.4
  78.0 0.1 collective-permute-start.2
  78.1 0.0 copy-done.3
  78.1 0.5 collective-permute-start.1
  78.5 0.0 collective-permute-done.4
  78.5 0.6 pad_maximum_fusion.gain_ref
  79.2 0.0 collective-permute-done.3.g2_ref
  79.2 0.0 copy-start.5
  79.2 1.7 collective-permute-done.1.o2_ref
  80.9 0.0 copy-done.5
  80.9 0.0 copy-start.6
  80.9 0.8 copy-done.6
  81.7 0.0 collective-permute-done.2.dq2_ref
  81.7 6.6 %weight_parts.1.send_hbm = bf16[32,8,6272]{2,1,0:T(8,128)(2,1)} custom-call(s32[576,1]{1,0:T(8,128)} %fusion.28.want_ref, bf16[576,512]{1,0:T(8,128)(2,1)} %fusion.6.hid_ref, bf16[256,1152]{1,0:T(8,128)(2,1)} %get-tuple-element.23.o_ref, bf16[256,1152]{1,0:T(8,128)(2,1)} %copy-done.6, bf16[256,1152]{1,0:T(8,128)(2,1)} %get-tuple-element.24.dq_ref, ...), custom_call_target="tpu_custom_call" | custom-call | tf_op jit(solution)/shard_map/weight_parts/pallas_call | solution.py:173
  88.3 17.9 %all-to-all-done.1.got_hbm = bf16[32,2,40,512]{3,2,1,0:T(8,128)(2,1)} async-done(((bf16[32,2,40,512]{3,2,1,0:T(8,128)(2,1)}), bf16[32,2,40,512]{3,2,1,0:T(8,128)(2,1)}, u32[]{:S(2)}, u32[]{:S(2)}) %all-to-all-start.1) | async-done | bytes 2621472 | tf_op jit(solution)/shard_map/all_to_all | solution.py:431
  106.2 4.5 %image_sums.1 = (f32[576,128]{1,0:T(8,128)}, f32[576,128]{1,0:T(8,128)}, bf16[160,512]{1,0:T(8,128)(2,1)}) custom-call(s32[1]{0:T(128)} %bitcast.core_ref, bf16[32,2,40,512]{3,2,1,0:T(8,128)(2,1)} %all-to-all-done.1.got_hbm, bf16[32,2,16,1152]{3,2,1,0:T(8,128)(2,1)} %all-to-all-done.g_hbm), custom_call_target="tpu_custom_call" | custom-call | tf_op jit(solution)/shard_map/image_sums/pallas_call | solution.py:224
  110.7 0.1 collective-permute-start.5
  110.8 1.8 %collective-permute-done.5.got_ref = f32[576,128]{1,0:T(8,128)S(1)} collective-permute-done((f32[576,128]{1,0:T(8,128)}, f32[576,128]{1,0:T(8,128)S(1)}, u32[]{:S(2)}, u32[]{:S(2)}) %collective-permute-start.5) | collective-permute-done | bytes 294944 | tf_op jit(solution)/shard_map/ppermute | solution.py:448
  112.6 0.0 copy-start.7
  112.6 0.7 copy-done.7
  113.3 2.6 %fill_rest.1 = bf16[32,8,6272]{2,1,0:T(8,128)(2,1)} custom-call(bf16[32,8,6272]{2,1,0:T(8,128)(2,1)} %weight_parts.1.send_hbm, f32[576,128]{1,0:T(8,128)} %get-tuple-element.27.mine_ref, f32[576,128]{1,0:T(8,128)} %copy-done.7, bf16[160,512]{1,0:T(8,128)(2,1)} %get-tuple-element.29.tok_ref, ...), custom_call_target="tpu_custom_call", output_to_operand_aliasing={{}: (0, {})} | custom-call | tf_op jit(solution)/shard_map/fill_rest/pallas_call | solution.py:274
  115.9 8.6 %all-to-all-start.2 = ((bf16[32,8,6272]{2,1,0:T(8,128)(2,1)}), bf16[32,8,6272]{2,1,0:T(8,128)(2,1)}, u32[]{:S(2)}, u32[]{:S(2)}) async-start(bf16[32,8,6272]{2,1,0:T(8,128)(2,1)} %fill_rest.1), calls=%async_computation.2 | async-start | bytes 6422528 | tf_op jit(solution)/shard_map/all_to_all | solution.py:449
  124.6 2.4 %fusion.12 = bf16[256,1152]{1,0:T(8,128)(2,1)} fusion(bf16[256,1152]{1,0:T(8,128)(2,1)S(1)} %copy-done.1, f32[256,1152]{1,0:T(8,128)} %get-tuple-element.40, f32[256]{0:T(256)S(1)} %broadcast_multiply_fusion, f32[1152]{0:T(1024)S(1)} %copy-done.9, f32[256]{0:T(256)S(1)} %add_rsqrt_fusion), kind=kLoop, calls=%fused_computation.17 | loop fusion | flops 2064384 | bytes 2365952 | tf_op jit(solution)/shard_map/convert_element_type | solution.py:444
  127.0 38.2 %all-to-all-done.2.recv_hbm = bf16[32,8,6272]{2,1,0:T(8,128)(2,1)} async-done(((bf16[32,8,6272]{2,1,0:T(8,128)(2,1)}), bf16[32,8,6272]{2,1,0:T(8,128)(2,1)}, u32[]{:S(2)}, u32[]{:S(2)}) %all-to-all-start.2) | async-done | bytes 3211296 | tf_op jit(solution)/shard_map/all_to_all | solution.py:449
  165.1 3.5 %group_sums.1 = (f32[10,4,1152]{2,1,0:T(4,128)}, f32[10,4,1152]{2,1,0:T(4,128)}) custom-call(s32[1]{0:T(128)} %bitcast.2.yl_ref, bf16[32,8,6272]{2,1,0:T(8,128)(2,1)} %all-to-all-done.2.recv_hbm), custom_call_target="tpu_custom_call" | custom-call | tf_op jit(solution)/shard_map/group_sums/pallas_call | solution.py:340
  168.7 0.1 collective-permute-start.6
  168.8 4.9 %guide_grad.1 = bf16[32,1152]{1,0:T(8,128)(2,1)} custom-call(bf16[32,8,6272]{2,1,0:T(8,128)(2,1)} %all-to-all-done.2.recv_hbm, bf16[1152,1152]{1,0:T(8,128)(2,1)} %wk_hbm.3, bf16[1152,1152]{1,0:T(8,128)(2,1)} %wv_hbm.3), custom_call_target="tpu_custom_call" | custom-call | tf_op jit(solution)/shard_map/guide_grad/pallas_call | solution.py:398
  173.7 0.8 collective-permute-done.6.got_ref
  174.5 0.0 copy-start.8
  174.5 0.7 copy-done.8
  175.2 1.7 both_sums.1
  (5 shorter events, 0.0 us)
Async XLA Ops:
  0.6 16.0 %copy-start = (bf16[1152,1152]{1,0:T(8,128)(2,1)S(1)}, bf16[1152,1152]{1,0:T(8,128)(2,1)}, u32[]{:S(2)}) copy-start(bf16[1152,1152]{1,0:T(8,128)(2,1)} %param.13) | copy-start | bytes 7962628
  3.4 11.3 %copy-start.1 = (bf16[256,1152]{1,0:T(8,128)(2,1)S(1)}, bf16[256,1152]{1,0:T(8,128)(2,1)}, u32[]{:S(2)}) copy-start(bf16[256,1152]{1,0:T(8,128)(2,1)} %param.9) | copy-start | bytes 1769476
  3.4 11.5 %copy-start.9 = (f32[1152]{0:T(1024)S(1)}, f32[1152]{0:T(1024)}, u32[]{:S(2)}) copy-start(f32[1152]{0:T(1024)} %param.12) | copy-start | bytes 13828
  3.4 41.4 %all-to-all-start = ((bf16[32,2,16,1152]{3,2,1,0:T(8,128)(2,1)}), bf16[32,2,16,1152]{3,2,1,0:T(8,128)(2,1)}, u32[]{:S(2)}, u32[]{:S(2)}) async-start(bf16[32,2,16,1152]{3,2,1,0:T(8,128)(2,1)} %copies_of_guide.1), calls=%async_computation | async-start | bytes 4718592 | tf_op jit(solution)/shard_map/all_to_all | solution.py:417
  16.0 5.6 %collective-permute-start = (bf16[256,1152]{1,0:T(8,128)(2,1)}, bf16[256,1152]{1,0:T(8,128)(2,1)}, u32[]{:S(2)}, u32[]{:S(2)}) collective-permute-start(bf16[256,1152]{1,0:T(8,128)(2,1)} %fusion.7), channel_id=1, source_target_pairs={{0,32},{32,0},{1,33},{33,1},{2,34},{34,2},{3,35},{35,3},{4,36},{36... | collective-permute-start | bytes 1769480 | tf_op jit(solution)/shard_map/ppermute | solution.py:425
  16.7 3.1 %copy-start.2 = (bf16[256,1152]{1,0:T(8,128)(2,1)S(1)}, bf16[256,1152]{1,0:T(8,128)(2,1)}, u32[]{:S(2)}) copy-start(bf16[256,1152]{1,0:T(8,128)(2,1)} %g_ref.3) | copy-start | bytes 1769476
  16.7 3.1 %copy-start.10 = (bf16[1152,1152]{1,0:T(8,128)(2,1)S(1)}, bf16[1152,1152]{1,0:T(8,128)(2,1)}, u32[]{:S(2)}) copy-start(bf16[1152,1152]{1,0:T(8,128)(2,1)} %param.16) | copy-start | bytes 7962628
  64.7 41.5 %all-to-all-start.1 = ((bf16[32,2,40,512]{3,2,1,0:T(8,128)(2,1)}), bf16[32,2,40,512]{3,2,1,0:T(8,128)(2,1)}, u32[]{:S(2)}, u32[]{:S(2)}) async-start(bf16[32,2,40,512]{3,2,1,0:T(8,128)(2,1)} %get-tuple-element.21), calls=%async_computation.1 | async-start | bytes 5242880 | tf_op jit(solution)/shard_map/all_to_all | solution.py:431
  73.1 6.0 %collective-permute-start.3 = (bf16[256,1152]{1,0:T(8,128)(2,1)}, bf16[256,1152]{1,0:T(8,128)(2,1)S(1)}, u32[]{:S(2)}, u32[]{:S(2)}) collective-permute-start(bf16[256,1152]{1,0:T(8,128)(2,1)} %g_ref.3), channel_id=1, source_target_pairs={{0,32},{32,0},{1,33},{33,1},{2,34},{34,2},{3,35},{35,3},{4,36},{36... | collective-permute-start | bytes 1769480 | tf_op jit(solution)/shard_map/ppermute | solution.py:427
  73.2 4.8 %copy-start.4 = (bf16[256,1152]{1,0:T(8,128)(2,1)S(1)}, bf16[256,1152]{1,0:T(8,128)(2,1)}, u32[]{:S(2)}) copy-start(bf16[256,1152]{1,0:T(8,128)(2,1)} %get-tuple-element.24.dq_ref) | copy-start | bytes 1769476
  73.2 4.8 %copy-start.3 = (bf16[256,1152]{1,0:T(8,128)(2,1)S(1)}, bf16[256,1152]{1,0:T(8,128)(2,1)}, u32[]{:S(2)}) copy-start(bf16[256,1152]{1,0:T(8,128)(2,1)} %get-tuple-element.23.o_ref) | copy-start | bytes 1769476
  76.5 2.0 %collective-permute-start.4 = (f32[1,1152]{1,0:T(1,128)S(1)}, f32[1,1152]{1,0:T(1,128)S(1)}, u32[]{:S(2)}, u32[]{:S(2)}) collective-permute-start(f32[1,1152]{1,0:T(1,128)S(1)} %broadcast_in_dim.6), channel_id=1, source_target_pairs={{0,32},{32,0},{1,33},{33,1},{2,34},{34,2},{3,35},{35,3},{4,36},{36... | collective-permute-start | bytes 13832 | tf_op jit(solution)/shard_map/ppermute | solution.py:437
  78.0 3.7 %collective-permute-start.2 = (bf16[256,1152]{1,0:T(8,128)(2,1)S(1)}, bf16[256,1152]{1,0:T(8,128)(2,1)}, u32[]{:S(2)}, u32[]{:S(2)}) collective-permute-start(bf16[256,1152]{1,0:T(8,128)(2,1)S(1)} %copy-done.4), channel_id=1, source_target_pairs={{0,32},{32,0},{1,33},{33,1},{2,34},{34,2},{3,35},{35,3},{4,36},{36... | collective-permute-start | bytes 1769480 | tf_op jit(solution)/shard_map/ppermute | solution.py:433
  78.1 2.8 %collective-permute-start.1 = (bf16[256,1152]{1,0:T(8,128)(2,1)S(1)}, bf16[256,1152]{1,0:T(8,128)(2,1)S(1)}, u32[]{:S(2)}, u32[]{:S(2)}) collective-permute-start(bf16[256,1152]{1,0:T(8,128)(2,1)S(1)} %copy-done.3), channel_id=1, source_target_pairs={{0,32},{32,0},{1,33},{33,1},{2,34},{34,2},{3,35},{35,3},{4,36},{36... | collective-permute-start | bytes 1769480 | tf_op jit(solution)/shard_map/ppermute | solution.py:434
  79.2 1.7 copy-start.5
  80.9 0.8 copy-start.6
  110.7 1.9 %collective-permute-start.5 = (f32[576,128]{1,0:T(8,128)}, f32[576,128]{1,0:T(8,128)S(1)}, u32[]{:S(2)}, u32[]{:S(2)}) collective-permute-start(f32[576,128]{1,0:T(8,128)} %get-tuple-element.28), channel_id=1, source_target_pairs={{0,32},{32,0},{1,33},{33,1},{2,34},{34,2},{3,35},{35,3},{4,36},{36... | collective-permute-start | bytes 884744 | tf_op jit(solution)/shard_map/ppermute | solution.py:448
  112.6 0.7 copy-start.7
  115.9 49.2 %all-to-all-start.2 = ((bf16[32,8,6272]{2,1,0:T(8,128)(2,1)}), bf16[32,8,6272]{2,1,0:T(8,128)(2,1)}, u32[]{:S(2)}, u32[]{:S(2)}) async-start(bf16[32,8,6272]{2,1,0:T(8,128)(2,1)} %fill_rest.1), calls=%async_computation.2 | async-start | bytes 6422528 | tf_op jit(solution)/shard_map/all_to_all | solution.py:449
  168.7 5.8 %collective-permute-start.6 = (f32[10,4,1152]{2,1,0:T(4,128)}, f32[10,4,1152]{2,1,0:T(4,128)S(1)}, u32[]{:S(2)}, u32[]{:S(2)}) collective-permute-start(f32[10,4,1152]{2,1,0:T(4,128)} %get-tuple-element.33), channel_id=1, source_target_pairs={{0,64},{64,0},{1,65},{65,1},{2,66},{66,2},{3,67},{67,3},{4,68},{68... | collective-permute-start | bytes 552968 | tf_op jit(solution)/shard_map/ppermute | solution.py:452
  174.5 0.7 copy-start.8

commit v9 on v8

--- a/solution.py
+++ b/solution.py
@@ -44,16 +44,19 @@
 ):
     loads = [
         pltpu.make_async_copy(g_hbm.at[:, img_ref[0]], guide, sems.at[0]),
-        pltpu.make_async_copy(wk_hbm, wk, sems.at[1]),
-        pltpu.make_async_copy(wv_hbm, wv, sems.at[2]),
+        pltpu.make_async_copy(wk_hbm.at[:, pl.ds(0, 512)], wk.at[:, pl.ds(0, 512)], sems.at[1]),
+        pltpu.make_async_copy(wk_hbm.at[:, pl.ds(512, 640)], wk.at[:, pl.ds(512, 640)], sems.at[2]),
+        pltpu.make_async_copy(wv_hbm, wv, sems.at[3]),
     ]
     for copy in loads:
         copy.start()
     loads[0].wait()
     tokens = guide[...].reshape(G, D)
     loads[1].wait()
-    k_scr[...] = dot(tokens, wk[...], 1, 0).astype(BF16)
+    k_scr[:, :512] = dot(tokens, wk[:, :512], 1, 0).astype(BF16)
     loads[2].wait()
+    k_scr[:, 512:] = dot(tokens, wk[:, 512:], 1, 0).astype(BF16)
+    loads[3].wait()
     v_scr[...] = dot(tokens, wv[...], 1, 0).astype(BF16)
     scale = HD ** (-0.5)
     flag = jnp.full((4, G), img_ref[0], jnp.int32).astype(F32)
@@ -114,7 +117,7 @@
             pltpu.VMEM((G, D), BF16),
             pltpu.VMEM((G, D), BF16),
             pltpu.VMEM((32, 2, 40, G), BF16),
-            pltpu.SemaphoreType.DMA((3,)),
+            pltpu.SemaphoreType.DMA((4,)),
             pltpu.SemaphoreType.DMA((HEADS // 2,)),
         ],
         name="attention",
@@ -286,7 +289,7 @@
     )(send, mine, got, tok, gain)
 
 
-def group_sums_kernel(yl_ref, recv_hbm, keep_ref, give_ref, both, recv, sems):
+def group_sums_kernel(yl_ref, recv_hbm, keep_ref, give_ref, gain_ref, both, recv, sems):
     loads = []
     for part in range(4):
         some = pl.ds(8 * part, 8)
@@ -327,12 +330,11 @@
             for b in range(9):
                 at = 128 * b
                 both[y, 3 * m, 8:9, at : at + 128] = slot(SLOTS[9 * (2 * y + m) + b])
-        for b in range(9):
-            at = 128 * b
-            both[y, 0, 9:10, at : at + 128] = slot(GAINS[b]) + slot(GAINS[9 + b])
+    for b in range(9):
+        gain_ref[b : b + 1] = slot(GAINS[b]) + slot(GAINS[9 + b])
     for out, y in ((keep_ref, yl_ref[0]), (give_ref, 1 - yl_ref[0])):
         for m in range(4):
-            out[:, m] = both[y, m, :10]
+            out[:, m] = both[y, m, :9]
 
 
 def group_sums(yl, recv):
@@ -340,8 +342,8 @@
     return pl.pallas_call(
         group_sums_kernel,
         in_specs=[pl.BlockSpec(memory_space=pltpu.SMEM), pl.BlockSpec(memory_space=pl.ANY)],
-        out_specs=[vmem] * 2,
-        out_shape=[jax.ShapeDtypeStruct((10, 4, D), F32)] * 2,
+        out_specs=[vmem] * 3,
+        out_shape=[jax.ShapeDtypeStruct((9, 4, D), F32)] * 2 + [jax.ShapeDtypeStruct((9, 128), F32)],
         scratch_shapes=[
             pltpu.VMEM((2, 4, 16, D), F32),
             pltpu.VMEM((32, 8, WIDE), BF16),
@@ -349,24 +351,6 @@
         ],
         name="group_sums",
     )(yl, recv)
-
-
-def both_sums_kernel(keep_ref, got_ref, gw_ref, gain_ref):
-    gw_ref[...] = keep_ref[:9] + got_ref[:9]
-    gain = keep_ref[9, :1] + got_ref[9, :1]
-    for b in range(9):
-        gain_ref[b : b + 1] = gain[:, 128 * b : 128 * b + 128]
-
-
-def both_sums(keep, got):
-    vmem = pl.BlockSpec(memory_space=pltpu.VMEM)
-    return pl.pallas_call(
-        both_sums_kernel,
-        in_specs=[vmem] * 2,
-        out_specs=[vmem] * 2,
-        out_shape=[jax.ShapeDtypeStruct((9, 4, D), F32), jax.ShapeDtypeStruct((9, 128), F32)],
-        name="both_sums",
-    )(keep, got)
 
 
 def guide_grad_kernel(recv_hbm, wk_hbm, wv_hbm, gg_ref, tok, recv, wk, wv, sems):
@@ -448,8 +432,9 @@
     send = fill_rest(send, mine, lax.ppermute(theirs, "c", SWAP), tok, gains)
     recv = lax.all_to_all(send, TILE_AXES, 0, 0, tiled=True)
     recv, grad_tiles = lax.optimization_barrier((recv, grad_tiles))
-    keep, give = group_sums(yl[None], recv)
-    grad_weights, grad_gain = both_sums(keep, lax.ppermute(give, "yl", SWAP))
+    keep, give, grad_gain = group_sums(yl[None], recv)
+    grad_weights = keep + lax.ppermute(give, "yl", SWAP)
+    grad_gain = grad_gain + lax.ppermute(grad_gain, "yl", SWAP)
     grad_guide = guide_grad(recv, w_key, w_value).reshape(guide.shape)
     return (grad_tiles, grad_guide, grad_weights.transpose(1, 0, 2), grad_gain.reshape(D))
 

time: 180 us -> 183 us (1.017)
  starting transfers between devices: 29.5 us -> 31.6 us
  Pallas kernels: 46.5 us -> 44.5 us
  waiting for transfers between devices: 80.6 us -> 82.6 us
    ppermute x1 -> x2, starting transfers between devices: 0.08 us -> 2.13 us  [the longest x1 2.05 us: on_device(): grad_weights = keep + lax.ppermute(give, 'yl', SWAP)]
    ppermute x1 -> x2, waiting for transfers between devices: 0.83 us -> 2.77 us  [the longest x1 2.76 us: on_device(): grad_weights = keep + lax.ppermute(give, 'yl', SWAP)]
  transfers between devices with their start and end apart: 10 -> 11, of which waited for: 6 -> 6; matrix products, arithmetic and copies ran while one was open for 9% -> 10% of each run, Pallas kernels for 6% -> 6%
where the time goes in v9:
time: 183 us; the launch traced here: 180 us
  waiting for transfers between devices  82.6 us (45%)
  Pallas kernels  44.5 us (24%)
  starting transfers between devices  31.6 us (17%)
  matrix products  11.2 us (6%)
  other arithmetic  6.65 us (4%)
    all_to_all x1, waiting for transfers between devices, on_device(): recv = lax.all_to_all(send, TILE_AXES, 0, 0, tiled=True)  38.2 us
    all_to_all x1, waiting for transfers between devices, on_device(): whole = lax.all_to_all(copies_of(guide), TILE_AXES, 0, 0, tiled=True)  20.2 us
    pallas_call x1, Pallas kernels, attention(): pl.pallas_call(attention_kernel, in_specs=[pl.BlockSpec(memory_space=pltp...  19.6 us
    all_to_all x1, waiting for transfers between devices, on_device(): got = lax.all_to_all(pay, TILE_AXES, 0, 0, tiled=True)  18 us
    all_to_all x1, starting transfers between devices, on_device(): whole = lax.all_to_all(copies_of(guide), TILE_AXES, 0, 0, tiled=True)  11.3 us
    dot_general x4, matrix products, dot(): lax.dot_general(a, b, (((ca,), (cb,)), ((), ())), preferred_element_type=...  11.2 us
    all_to_all x1, starting transfers between devices, on_device(): recv = lax.all_to_all(send, TILE_AXES, 0, 0, tiled=True)  8.63 us
    all_to_all x1, starting transfers between devices, on_device(): got = lax.all_to_all(pay, TILE_AXES, 0, 0, tiled=True)  8.37 us
  transfers between devices with their start and end apart: 11, of which 6 were waited for; matrix products, arithmetic and copies ran while one was open for 10% of the time, Pallas kernels for 6%

profile of v9, /device:TPU:2, one launch (start us, length us, event | category | flops | bytes accessed | tf_op | source)
XLA Modules:
  0.0 179.6 jit_solution(16083451977291983722)
XLA Ops:
  0.6 0.0 copy-start
  0.6 2.8 %copies_of_guide.1 = bf16[32,2,16,1152]{3,2,1,0:T(8,128)(2,1)} custom-call(bf16[2,16,1152]{2,1,0:T(8,128)(2,1)} %g_ref.2), custom_call_target="tpu_custom_call" | custom-call | tf_op jit(solution)/shard_map/copies_of_guide/pallas_call | solution.py:31
  3.4 0.0 copy-start.1
  3.4 0.0 copy-start.9
  3.4 11.3 %all-to-all-start = ((bf16[32,2,16,1152]{3,2,1,0:T(8,128)(2,1)}), bf16[32,2,16,1152]{3,2,1,0:T(8,128)(2,1)}, u32[]{:S(2)}, u32[]{:S(2)}) async-start(bf16[32,2,16,1152]{3,2,1,0:T(8,128)(2,1)} %copies_of_guide.1), calls=%async_computation | async-start | bytes 4718592 | tf_op jit(solution)/shard_map/all_to_all | solution.py:401
  14.7 0.0 copy-done.1
  14.7 0.2 fusion.13
  14.9 0.0 copy-done.9
  15.0 1.0 fusion.7
  16.0 0.0 collective-permute-start
  16.7 0.0 copy-done
  16.7 0.0 copy-start.2
  16.7 0.0 copy-start.11
  16.7 3.0 %convolution_convert_fusion.1.q_ref = bf16[256,1152]{1,0:T(8,128)(2,1)} fusion(bf16[256,1152]{1,0:T(8,128)(2,1)} %fusion.7, bf16[1152,1152]{1,0:T(8,128)(2,1)S(1)} %copy-done), kind=kOutput, calls=%fused_computation.3 | convolution fusion | flops 679772160 | bytes 3833856 | tf_op jit(solution)/shard_map/dot_general | solution.py:19
  19.7 0.0 copy-done.2
  19.7 0.0 copy-done.11
  19.7 1.9 %convolution_convert_fusion.d_ref = bf16[256,1152]{1,0:T(8,128)(2,1)} fusion(bf16[256,1152]{1,0:T(8,128)(2,1)S(1)} %copy-done.2, bf16[1152,1152]{1,0:T(8,128)(2,1)S(1)} %copy-done.11), kind=kOutput, calls=%fused_computation.2 | convolution fusion | flops 679772160 | bytes 3833856 | tf_op jit(solution)/shard_map/dot_general | solution.py:19
  21.6 0.0 collective-permute-done
  21.6 3.1 %fusion.6.hid_ref = bf16[576,512]{1,0:T(8,128)(2,1)} fusion(s32[576]{0:T(1024)S(1)} %fusion.44, bf16[256,1152]{1,0:T(8,128)(2,1)} %collective-permute-done, bf16[256,1152]{1,0:T(8,128)(2,1)} %fusion.7), kind=kOutput, calls=%fused_computation.11 | convolution fusion | flops 682795008 | bytes 1771776 | tf_op jit(solution)/shard_map/dot_general | solution.py:19
  24.7 20.2 %all-to-all-done.g_hbm = bf16[32,2,16,1152]{3,2,1,0:T(8,128)(2,1)} async-done(((bf16[32,2,16,1152]{3,2,1,0:T(8,128)(2,1)}), bf16[32,2,16,1152]{3,2,1,0:T(8,128)(2,1)}, u32[]{:S(2)}, u32[]{:S(2)}) %all-to-all-start) | async-done | bytes 2359328 | tf_op jit(solution)/shard_map/all_to_all | solution.py:401
  44.8 19.6 %attention.1 = (bf16[32,2,40,512]{3,2,1,0:T(8,128)(2,1)}, bf16[256,1152]{1,0:T(8,128)(2,1)}, bf16[256,1152]{1,0:T(8,128)(2,1)}) custom-call(s32[1]{0:T(128)S(6)} %copy.15.img_ref, bf16[32,2,16,1152]{3,2,1,0:T(8,128)(2,1)} %all-to-all-done.g_hbm, bf16[1152,1152]{1,0:T(8,128)(2,1)} %wk_hbm.3, bf16[1152,1152]{1,0:T(8,128)(2,1)} %wv_hbm.3, ...), custom_call_target="tpu_custom_call" | custom-call | tf_op jit(solution)/shard_map/attention/pallas_call | solution.py:104
  64.4 8.4 %all-to-all-start.1 = ((bf16[32,2,40,512]{3,2,1,0:T(8,128)(2,1)}), bf16[32,2,40,512]{3,2,1,0:T(8,128)(2,1)}, u32[]{:S(2)}, u32[]{:S(2)}) async-start(bf16[32,2,40,512]{3,2,1,0:T(8,128)(2,1)} %get-tuple-element.20), calls=%async_computation.1 | async-start | bytes 5242880 | tf_op jit(solution)/shard_map/all_to_all | solution.py:415
  72.8 0.1 collective-permute-start.3
  72.9 0.0 copy-start.4
  72.9 0.0 copy-start.3
  72.9 3.2 %fusion.9 = (f32[256]{0:T(256)S(1)}, f32[1152]{0:T(1024)S(1)}, f32[256,1152]{1,0:T(8,128)}) fusion(bf16[256,1152]{1,0:T(8,128)(2,1)S(1)} %copy-done.1, f32[1152]{0:T(1024)S(1)} %copy-done.9, f32[256]{0:T(256)S(1)} %add_rsqrt_fusion, bf16[256,1152]{1,0:T(8,128)(2,1)} %get-tuple-element.23.dq_ref, bf16[1152,1152]{1,0:T(8,128)(2,1)S(1)} %copy-done), kind=kOutput, calls=%fused_computation.14 | convolution fusion | flops 681540224 | bytes 5024768 | tf_op jit(solution)/shard_map/dot_general | solution.py:19
  76.1 0.5 collective-permute-start.4
  76.6 1.1 fusion.28.want_ref
  77.7 0.0 copy-done.4
  77.7 0.0 collective-permute-start.2
  77.7 0.0 copy-done.3
  77.7 0.5 collective-permute-start.1
  78.2 0.0 collective-permute-done.4
  78.2 0.6 pad_maximum_fusion.gain_ref
  78.8 0.0 collective-permute-done.3.g2_ref
  78.8 0.0 copy-start.5
  78.8 1.7 collective-permute-done.1.o2_ref
  80.5 0.0 copy-done.5
  80.5 0.8 copy-done.6
  81.4 0.0 collective-permute-done.2.dq2_ref
  81.4 6.6 %weight_parts.1.send_hbm = bf16[32,8,6272]{2,1,0:T(8,128)(2,1)} custom-call(s32[576,1]{1,0:T(8,128)} %fusion.28.want_ref, bf16[576,512]{1,0:T(8,128)(2,1)} %fusion.6.hid_ref, bf16[256,1152]{1,0:T(8,128)(2,1)} %get-tuple-element.22.o_ref, bf16[256,1152]{1,0:T(8,128)(2,1)} %copy-done.6, bf16[256,1152]{1,0:T(8,128)(2,1)} %get-tuple-element.23.dq_ref, ...), custom_call_target="tpu_custom_call" | custom-call | tf_op jit(solution)/shard_map/weight_parts/pallas_call | solution.py:176
  87.9 18.0 %all-to-all-done.1.got_hbm = bf16[32,2,40,512]{3,2,1,0:T(8,128)(2,1)} async-done(((bf16[32,2,40,512]{3,2,1,0:T(8,128)(2,1)}), bf16[32,2,40,512]{3,2,1,0:T(8,128)(2,1)}, u32[]{:S(2)}, u32[]{:S(2)}) %all-to-all-start.1) | async-done | bytes 2621472 | tf_op jit(solution)/shard_map/all_to_all | solution.py:415
  105.9 4.5 %image_sums.1 = (f32[576,128]{1,0:T(8,128)}, f32[576,128]{1,0:T(8,128)}, bf16[160,512]{1,0:T(8,128)(2,1)}) custom-call(s32[1]{0:T(128)} %bitcast.core_ref, bf16[32,2,40,512]{3,2,1,0:T(8,128)(2,1)} %all-to-all-done.1.got_hbm, bf16[32,2,16,1152]{3,2,1,0:T(8,128)(2,1)} %all-to-all-done.g_hbm), custom_call_target="tpu_custom_call" | custom-call | tf_op jit(solution)/shard_map/image_sums/pallas_call | solution.py:227
  110.4 0.1 collective-permute-start.5
  110.5 1.8 collective-permute-done.5.got_ref
  112.3 0.7 copy-done.7
  113.0 2.6 %fill_rest.1 = bf16[32,8,6272]{2,1,0:T(8,128)(2,1)} custom-call(bf16[32,8,6272]{2,1,0:T(8,128)(2,1)} %weight_parts.1.send_hbm, f32[576,128]{1,0:T(8,128)} %get-tuple-element.26.mine_ref, f32[576,128]{1,0:T(8,128)} %copy-done.7, bf16[160,512]{1,0:T(8,128)(2,1)} %get-tuple-element.28.tok_ref, ...), custom_call_target="tpu_custom_call", output_to_operand_aliasing={{}: (0, {})} | custom-call | tf_op jit(solution)/shard_map/fill_rest/pallas_call | solution.py:277
  115.6 8.6 %all-to-all-start.2 = ((bf16[32,8,6272]{2,1,0:T(8,128)(2,1)}), bf16[32,8,6272]{2,1,0:T(8,128)(2,1)}, u32[]{:S(2)}, u32[]{:S(2)}) async-start(bf16[32,8,6272]{2,1,0:T(8,128)(2,1)} %fill_rest.1), calls=%async_computation.2 | async-start | bytes 6422528 | tf_op jit(solution)/shard_map/all_to_all | solution.py:433
  124.3 2.4 %fusion.12 = bf16[256,1152]{1,0:T(8,128)(2,1)} fusion(bf16[256,1152]{1,0:T(8,128)(2,1)S(1)} %copy-done.1, f32[256,1152]{1,0:T(8,128)} %get-tuple-element.38, f32[256]{0:T(256)S(1)} %broadcast_multiply_fusion, f32[1152]{0:T(1024)S(1)} %copy-done.9, f32[256]{0:T(256)S(1)} %add_rsqrt_fusion), kind=kLoop, calls=%fused_computation.17 | loop fusion | flops 2064384 | bytes 2365952 | tf_op jit(solution)/shard_map/convert_element_type | solution.py:428
  126.7 38.2 %all-to-all-done.2.recv_hbm = bf16[32,8,6272]{2,1,0:T(8,128)(2,1)} async-done(((bf16[32,8,6272]{2,1,0:T(8,128)(2,1)}), bf16[32,8,6272]{2,1,0:T(8,128)(2,1)}, u32[]{:S(2)}, u32[]{:S(2)}) %all-to-all-start.2) | async-done | bytes 3211296 | tf_op jit(solution)/shard_map/all_to_all | solution.py:433
  164.9 3.5 %group_sums.1 = (f32[9,4,1152]{2,1,0:T(4,128)}, f32[9,4,1152]{2,1,0:T(4,128)}, f32[9,128]{1,0:T(8,128)}) custom-call(s32[1]{0:T(128)} %bitcast.2.yl_ref, bf16[32,8,6272]{2,1,0:T(8,128)(2,1)} %all-to-all-done.2.recv_hbm), custom_call_target="tpu_custom_call" | custom-call | tf_op jit(solution)/shard_map/group_sums/pallas_call | solution.py:342
  168.4 0.0 copy-start.12
  168.4 0.0 copy-start.10
  168.4 0.0 copy-start.8
  168.4 0.1 collective-permute-start.7
  168.5 4.9 %guide_grad.1 = bf16[32,1152]{1,0:T(8,128)(2,1)} custom-call(bf16[32,8,6272]{2,1,0:T(8,128)(2,1)} %all-to-all-done.2.recv_hbm, bf16[1152,1152]{1,0:T(8,128)(2,1)} %wk_hbm.3, bf16[1152,1152]{1,0:T(8,128)(2,1)} %wv_hbm.3), custom_call_target="tpu_custom_call" | custom-call | tf_op jit(solution)/shard_map/guide_grad/pallas_call | solution.py:382
  173.5 0.0 copy-done.12
  173.5 2.0 %collective-permute-start.6 = (f32[9,4,1152]{2,1,0:T(4,128)S(1)}, f32[9,4,1152]{2,1,0:T(4,128)S(1)}, u32[]{:S(2)}, u32[]{:S(2)}) collective-permute-start(f32[9,4,1152]{2,1,0:T(4,128)S(1)} %copy-done.12), channel_id=1, source_target_pairs={{0,64},{64,0},{1,65},{65,1},{2,66},{66,2},{3,67},{67,3},{4,68},{68... | collective-permute-start | bytes 497672 | tf_op jit(solution)/shard_map/ppermute | solution.py:436
  175.5 0.0 collective-permute-done.7
  175.5 0.0 copy-done.10
  175.5 0.6 add_bitcast_fusion.1
  176.1 2.8 %collective-permute-done.6 = f32[9,4,1152]{2,1,0:T(4,128)S(1)} collective-permute-done((f32[9,4,1152]{2,1,0:T(4,128)S(1)}, f32[9,4,1152]{2,1,0:T(4,128)S(1)}, u32[]{:S(2)}, u32[]{:S(2)}) %collective-permute-start.6) | collective-permute-done | bytes 165920 | tf_op jit(solution)/shard_map/ppermute | solution.py:436
  178.9 0.0 copy-done.8
  178.9 0.7 add_bitcast_fusion
  (7 shorter events, 0.0 us)
Async XLA Ops:
  0.6 16.0 %copy-start = (bf16[1152,1152]{1,0:T(8,128)(2,1)S(1)}, bf16[1152,1152]{1,0:T(8,128)(2,1)}, u32[]{:S(2)}) copy-start(bf16[1152,1152]{1,0:T(8,128)(2,1)} %param.13) | copy-start | bytes 7962628
  3.4 11.3 %copy-start.1 = (bf16[256,1152]{1,0:T(8,128)(2,1)S(1)}, bf16[256,1152]{1,0:T(8,128)(2,1)}, u32[]{:S(2)}) copy-start(bf16[256,1152]{1,0:T(8,128)(2,1)} %param.9) | copy-start | bytes 1769476
  3.4 11.5 %copy-start.9 = (f32[1152]{0:T(1024)S(1)}, f32[1152]{0:T(1024)}, u32[]{:S(2)}) copy-start(f32[1152]{0:T(1024)} %param.12) | copy-start | bytes 13828
  3.4 41.4 %all-to-all-start = ((bf16[32,2,16,1152]{3,2,1,0:T(8,128)(2,1)}), bf16[32,2,16,1152]{3,2,1,0:T(8,128)(2,1)}, u32[]{:S(2)}, u32[]{:S(2)}) async-start(bf16[32,2,16,1152]{3,2,1,0:T(8,128)(2,1)} %copies_of_guide.1), calls=%async_computation | async-start | bytes 4718592 | tf_op jit(solution)/shard_map/all_to_all | solution.py:401
  16.0 5.6 %collective-permute-start = (bf16[256,1152]{1,0:T(8,128)(2,1)}, bf16[256,1152]{1,0:T(8,128)(2,1)}, u32[]{:S(2)}, u32[]{:S(2)}) collective-permute-start(bf16[256,1152]{1,0:T(8,128)(2,1)} %fusion.7), channel_id=1, source_target_pairs={{0,32},{32,0},{1,33},{33,1},{2,34},{34,2},{3,35},{35,3},{4,36},{36... | collective-permute-start | bytes 1769480 | tf_op jit(solution)/shard_map/ppermute | solution.py:409
  16.7 3.1 %copy-start.2 = (bf16[256,1152]{1,0:T(8,128)(2,1)S(1)}, bf16[256,1152]{1,0:T(8,128)(2,1)}, u32[]{:S(2)}) copy-start(bf16[256,1152]{1,0:T(8,128)(2,1)} %g_ref.3) | copy-start | bytes 1769476
  16.7 3.0 %copy-start.11 = (bf16[1152,1152]{1,0:T(8,128)(2,1)S(1)}, bf16[1152,1152]{1,0:T(8,128)(2,1)}, u32[]{:S(2)}) copy-start(bf16[1152,1152]{1,0:T(8,128)(2,1)} %param.16) | copy-start | bytes 7962628
  64.4 41.5 %all-to-all-start.1 = ((bf16[32,2,40,512]{3,2,1,0:T(8,128)(2,1)}), bf16[32,2,40,512]{3,2,1,0:T(8,128)(2,1)}, u32[]{:S(2)}, u32[]{:S(2)}) async-start(bf16[32,2,40,512]{3,2,1,0:T(8,128)(2,1)} %get-tuple-element.20), calls=%async_computation.1 | async-start | bytes 5242880 | tf_op jit(solution)/shard_map/all_to_all | solution.py:415
  72.8 6.0 %collective-permute-start.3 = (bf16[256,1152]{1,0:T(8,128)(2,1)}, bf16[256,1152]{1,0:T(8,128)(2,1)S(1)}, u32[]{:S(2)}, u32[]{:S(2)}) collective-permute-start(bf16[256,1152]{1,0:T(8,128)(2,1)} %g_ref.3), channel_id=1, source_target_pairs={{0,32},{32,0},{1,33},{33,1},{2,34},{34,2},{3,35},{35,3},{4,36},{36... | collective-permute-start | bytes 1769480 | tf_op jit(solution)/shard_map/ppermute | solution.py:411
  72.9 4.8 %copy-start.4 = (bf16[256,1152]{1,0:T(8,128)(2,1)S(1)}, bf16[256,1152]{1,0:T(8,128)(2,1)}, u32[]{:S(2)}) copy-start(bf16[256,1152]{1,0:T(8,128)(2,1)} %get-tuple-element.23.dq_ref) | copy-start | bytes 1769476
  72.9 4.8 %copy-start.3 = (bf16[256,1152]{1,0:T(8,128)(2,1)S(1)}, bf16[256,1152]{1,0:T(8,128)(2,1)}, u32[]{:S(2)}) copy-start(bf16[256,1152]{1,0:T(8,128)(2,1)} %get-tuple-element.22.o_ref) | copy-start | bytes 1769476
  76.1 2.1 %collective-permute-start.4 = (f32[1,1152]{1,0:T(1,128)S(1)}, f32[1,1152]{1,0:T(1,128)S(1)}, u32[]{:S(2)}, u32[]{:S(2)}) collective-permute-start(f32[1,1152]{1,0:T(1,128)S(1)} %broadcast_in_dim.6), channel_id=1, source_target_pairs={{0,32},{32,0},{1,33},{33,1},{2,34},{34,2},{3,35},{35,3},{4,36},{36... | collective-permute-start | bytes 13832 | tf_op jit(solution)/shard_map/ppermute | solution.py:421
  77.7 3.7 %collective-permute-start.2 = (bf16[256,1152]{1,0:T(8,128)(2,1)S(1)}, bf16[256,1152]{1,0:T(8,128)(2,1)}, u32[]{:S(2)}, u32[]{:S(2)}) collective-permute-start(bf16[256,1152]{1,0:T(8,128)(2,1)S(1)} %copy-done.4), channel_id=1, source_target_pairs={{0,32},{32,0},{1,33},{33,1},{2,34},{34,2},{3,35},{35,3},{4,36},{36... | collective-permute-start | bytes 1769480 | tf_op jit(solution)/shard_map/ppermute | solution.py:417
  77.7 2.8 %collective-permute-start.1 = (bf16[256,1152]{1,0:T(8,128)(2,1)S(1)}, bf16[256,1152]{1,0:T(8,128)(2,1)S(1)}, u32[]{:S(2)}, u32[]{:S(2)}) collective-permute-start(bf16[256,1152]{1,0:T(8,128)(2,1)S(1)} %copy-done.3), channel_id=1, source_target_pairs={{0,32},{32,0},{1,33},{33,1},{2,34},{34,2},{3,35},{35,3},{4,36},{36... | collective-permute-start | bytes 1769480 | tf_op jit(solution)/shard_map/ppermute | solution.py:418
  78.8 1.7 copy-start.5
  80.5 0.8 copy-start.6
  110.4 1.9 %collective-permute-start.5 = (f32[576,128]{1,0:T(8,128)}, f32[576,128]{1,0:T(8,128)S(1)}, u32[]{:S(2)}, u32[]{:S(2)}) collective-permute-start(f32[576,128]{1,0:T(8,128)} %get-tuple-element.27), channel_id=1, source_target_pairs={{0,32},{32,0},{1,33},{33,1},{2,34},{34,2},{3,35},{35,3},{4,36},{36... | collective-permute-start | bytes 884744 | tf_op jit(solution)/shard_map/ppermute | solution.py:432
  112.3 0.7 copy-start.7
  115.6 49.2 %all-to-all-start.2 = ((bf16[32,8,6272]{2,1,0:T(8,128)(2,1)}), bf16[32,8,6272]{2,1,0:T(8,128)(2,1)}, u32[]{:S(2)}, u32[]{:S(2)}) async-start(bf16[32,8,6272]{2,1,0:T(8,128)(2,1)} %fill_rest.1), calls=%async_computation.2 | async-start | bytes 6422528 | tf_op jit(solution)/shard_map/all_to_all | solution.py:433
  168.4 5.1 %copy-start.12 = (f32[9,4,1152]{2,1,0:T(4,128)S(1)}, f32[9,4,1152]{2,1,0:T(4,128)}, u32[]{:S(2)}) copy-start(f32[9,4,1152]{2,1,0:T(4,128)} %get-tuple-element.32) | copy-start | bytes 497668
  168.4 7.1 %copy-start.10 = (f32[9,128]{1,0:T(8,128)S(1)}, f32[9,128]{1,0:T(8,128)}, u32[]{:S(2)}) copy-start(f32[9,128]{1,0:T(8,128)} %get-tuple-element.33) | copy-start | bytes 13828
  168.4 10.5 %copy-start.8 = (f32[9,4,1152]{2,1,0:T(4,128)S(1)}, f32[9,4,1152]{2,1,0:T(4,128)}, u32[]{:S(2)}) copy-start(f32[9,4,1152]{2,1,0:T(4,128)} %get-tuple-element.31) | copy-start | bytes 497668
  168.4 7.1 %collective-permute-start.7 = (f32[9,128]{1,0:T(8,128)}, f32[9,128]{1,0:T(8,128)S(1)}, u32[]{:S(2)}, u32[]{:S(2)}) collective-permute-start(f32[9,128]{1,0:T(8,128)} %get-tuple-element.33), channel_id=1, source_target_pairs={{0,64},{64,0},{1,65},{65,1},{2,66},{66,2},{3,67},{67,3},{4,68},{68... | collective-permute-start | bytes 13832 | tf_op jit(solution)/shard_map/ppermute | solution.py:437
  173.5 5.4 %collective-permute-start.6 = (f32[9,4,1152]{2,1,0:T(4,128)S(1)}, f32[9,4,1152]{2,1,0:T(4,128)S(1)}, u32[]{:S(2)}, u32[]{:S(2)}) collective-permute-start(f32[9,4,1152]{2,1,0:T(4,128)S(1)} %copy-done.12), channel_id=1, source_target_pairs={{0,64},{64,0},{1,65},{65,1},{2,66},{66,2},{3,67},{67,3},{4,68},{68... | collective-permute-start | bytes 497672 | tf_op jit(solution)/shard_map/ppermute | solution.py:436

commit v10 on v9

--- a/solution.py
+++ b/solution.py
@@ -4,6 +4,7 @@
 from jax.experimental import pallas as pl
 from jax.experimental.pallas import tpu as pltpu
 from jax.sharding import Mesh, PartitionSpec as P
+
 
 HEADS = 16
 HD = 72
@@ -296,6 +297,7 @@
         loads.append(pltpu.make_async_copy(recv_hbm.at[some], recv.at[some], sems.at[part]))
     for copy in loads:
         copy.start()
+
     def add(t, totals):
         sums = [x + recv[t, :, n * D : n * D + D].astype(F32) for n, x in enumerate(totals[:4])]
         return (*sums, totals[4] + recv[t, :, MISC + 640 :].astype(F32))
@@ -419,6 +421,7 @@
     dh = dot(dq, w_query, 1, 1)
     gain_part = jnp.sum(dh * normed, axis=0, keepdims=True)
     gain_part = gain_part + lax.ppermute(gain_part, "c", SWAP)
+    gain_part = gain_part + lax.ppermute(gain_part, "yl", SWAP)
     gain_high = lax.reduce_precision(gain_part, 8, 7)
     gains = jnp.concatenate([gain_high, gain_part - gain_high], axis=1)
     send = weight_parts(
@@ -433,9 +436,9 @@
     recv = lax.all_to_all(send, TILE_AXES, 0, 0, tiled=True)
     recv, grad_tiles = lax.optimization_barrier((recv, grad_tiles))
     keep, give, grad_gain = group_sums(yl[None], recv)
-    grad_weights = keep + lax.ppermute(give, "yl", SWAP)
-    grad_gain = grad_gain + lax.ppermute(grad_gain, "yl", SWAP)
+    got = lax.ppermute(give, "yl", SWAP)
     grad_guide = guide_grad(recv, w_key, w_value).reshape(guide.shape)
+    grad_weights = keep + got
     return (grad_tiles, grad_guide, grad_weights.transpose(1, 0, 2), grad_gain.reshape(D))
 
 

time: 183 us -> 185 us (1.011)
  starting transfers between devices: 31.6 us -> 35.4 us
    all_to_all x1, waiting for transfers between devices: 18 us -> 0.01 us  [on_device(): got = lax.all_to_all(pay, TILE_AXES, 0, 0, tiled=True)]
    ppermute x2, waiting for transfers between devices: 2.77 us -> 20.7 us  [the longest x1 20.7 us: on_device(): gain_part = gain_part + lax.ppermute(gain_part, 'yl', SWAP)]
    all_to_all x1, starting transfers between devices: 8.63 us -> 12.5 us  [on_device(): recv = lax.all_to_all(send, TILE_AXES, 0, 0, tiled=True)]
  transfers between devices with their start and end apart: 11 -> 11, of which waited for: 6 -> 5; matrix products, arithmetic and copies ran while one was open for 10% -> 9% of each run, Pallas kernels for 6% -> 6%
where the time goes in v10:
time: 185 us; the launch traced here: 183 us
  waiting for transfers between devices  81.4 us (44%)
  Pallas kernels  44.5 us (24%)
  starting transfers between devices  35.4 us (19%)
  matrix products  11.2 us (6%)
  other arithmetic  6.05 us (3%)
  local copies, waits for them, and re-layouts  2.42 us (1%)
    all_to_all x1, waiting for transfers between devices, on_device(): recv = lax.all_to_all(send, TILE_AXES, 0, 0, tiled=True)  38.2 us
    ppermute x1, waiting for transfers between devices, on_device(): gain_part = gain_part + lax.ppermute(gain_part, 'yl', SWAP)  20.7 us
    all_to_all x1, waiting for transfers between devices, on_device(): whole = lax.all_to_all(copies_of(guide), TILE_AXES, 0, 0, tiled=True)  20.1 us
    pallas_call x1, Pallas kernels, attention(): pl.pallas_call(attention_kernel, in_specs=[pl.BlockSpec(memory_space=pltp...  19.6 us
    all_to_all x1, starting transfers between devices, on_device(): recv = lax.all_to_all(send, TILE_AXES, 0, 0, tiled=True)  12.5 us
    all_to_all x1, starting transfers between devices, on_device(): whole = lax.all_to_all(copies_of(guide), TILE_AXES, 0, 0, tiled=True)  11.3 us
    dot_general x4, matrix products, dot(): lax.dot_general(a, b, (((ca,), (cb,)), ((), ())), preferred_element_type=...  11.2 us
    all_to_all x1, starting transfers between devices, on_device(): got = lax.all_to_all(pay, TILE_AXES, 0, 0, tiled=True)  8.36 us
  transfers between devices with their start and end apart: 11, of which 5 were waited for; matrix products, arithmetic and copies ran while one was open for 9% of the time, Pallas kernels for 6%

profile of v10, /device:TPU:2, one launch (start us, length us, event | category | flops | bytes accessed | tf_op | source)
XLA Modules:
  0.0 182.6 jit_solution(12751633622566006659)
XLA Ops:
  0.6 0.0 copy-start
  0.6 2.8 %copies_of_guide.1 = bf16[32,2,16,1152]{3,2,1,0:T(8,128)(2,1)} custom-call(bf16[2,16,1152]{2,1,0:T(8,128)(2,1)} %g_ref.2), custom_call_target="tpu_custom_call" | custom-call | tf_op jit(solution)/shard_map/copies_of_guide/pallas_call | solution.py:32
  3.4 0.0 copy-start.1
  3.4 0.0 copy-start.10
  3.4 11.3 %all-to-all-start = ((bf16[32,2,16,1152]{3,2,1,0:T(8,128)(2,1)}), bf16[32,2,16,1152]{3,2,1,0:T(8,128)(2,1)}, u32[]{:S(2)}, u32[]{:S(2)}) async-start(bf16[32,2,16,1152]{3,2,1,0:T(8,128)(2,1)} %copies_of_guide.1), calls=%async_computation | async-start | bytes 4718592 | tf_op jit(solution)/shard_map/all_to_all | solution.py:403
  14.7 0.0 copy-done.1
  14.7 0.2 fusion.13
  15.0 0.0 copy-done.10
  15.0 1.0 fusion.7
  16.0 0.0 collective-permute-start
  16.7 0.0 copy-done
  16.7 0.0 copy-start.2
  16.7 0.0 copy-start.11
  16.7 3.0 %convolution_convert_fusion.1.q_ref = bf16[256,1152]{1,0:T(8,128)(2,1)} fusion(bf16[256,1152]{1,0:T(8,128)(2,1)} %fusion.7, bf16[1152,1152]{1,0:T(8,128)(2,1)S(1)} %copy-done), kind=kOutput, calls=%fused_computation.3 | convolution fusion | flops 679772160 | bytes 3833856 | tf_op jit(solution)/shard_map/dot_general | solution.py:20
  19.7 0.0 copy-done.2
  19.7 0.0 copy-done.11
  19.7 1.9 %convolution_convert_fusion.d_ref = bf16[256,1152]{1,0:T(8,128)(2,1)} fusion(bf16[256,1152]{1,0:T(8,128)(2,1)S(1)} %copy-done.2, bf16[1152,1152]{1,0:T(8,128)(2,1)S(1)} %copy-done.11), kind=kOutput, calls=%fused_computation.2 | convolution fusion | flops 679772160 | bytes 3833856 | tf_op jit(solution)/shard_map/dot_general | solution.py:20
  21.6 0.0 collective-permute-done
  21.6 3.1 %fusion.6.hid_ref = bf16[576,512]{1,0:T(8,128)(2,1)} fusion(s32[576]{0:T(1024)S(1)} %fusion.44, bf16[256,1152]{1,0:T(8,128)(2,1)} %collective-permute-done, bf16[256,1152]{1,0:T(8,128)(2,1)} %fusion.7), kind=kOutput, calls=%fused_computation.11 | convolution fusion | flops 682795008 | bytes 1771776 | tf_op jit(solution)/shard_map/dot_general | solution.py:20
  24.7 20.1 %all-to-all-done.g_hbm = bf16[32,2,16,1152]{3,2,1,0:T(8,128)(2,1)} async-done(((bf16[32,2,16,1152]{3,2,1,0:T(8,128)(2,1)}), bf16[32,2,16,1152]{3,2,1,0:T(8,128)(2,1)}, u32[]{:S(2)}, u32[]{:S(2)}) %all-to-all-start) | async-done | bytes 2359328 | tf_op jit(solution)/shard_map/all_to_all | solution.py:403
  44.8 19.6 %attention.1 = (bf16[32,2,40,512]{3,2,1,0:T(8,128)(2,1)}, bf16[256,1152]{1,0:T(8,128)(2,1)}, bf16[256,1152]{1,0:T(8,128)(2,1)}) custom-call(s32[1]{0:T(128)S(6)} %copy.15.img_ref, bf16[32,2,16,1152]{3,2,1,0:T(8,128)(2,1)} %all-to-all-done.g_hbm, bf16[1152,1152]{1,0:T(8,128)(2,1)} %wk_hbm.3, bf16[1152,1152]{1,0:T(8,128)(2,1)} %wv_hbm.3, ...), custom_call_target="tpu_custom_call" | custom-call | tf_op jit(solution)/shard_map/attention/pallas_call | solution.py:105
  64.5 8.4 %all-to-all-start.1 = ((bf16[32,2,40,512]{3,2,1,0:T(8,128)(2,1)}), bf16[32,2,40,512]{3,2,1,0:T(8,128)(2,1)}, u32[]{:S(2)}, u32[]{:S(2)}) async-start(bf16[32,2,40,512]{3,2,1,0:T(8,128)(2,1)} %get-tuple-element.20), calls=%async_computation.1 | async-start | bytes 5242880 | tf_op jit(solution)/shard_map/all_to_all | solution.py:417
  72.8 0.0 copy-start.3
  72.8 0.0 copy-start.5
  72.9 0.0 copy-start.4
  72.9 3.2 %fusion.9 = (f32[256]{0:T(256)S(1)}, f32[1152]{0:T(1024)S(1)}, f32[256,1152]{1,0:T(8,128)}) fusion(bf16[256,1152]{1,0:T(8,128)(2,1)S(1)} %copy-done.1, f32[1152]{0:T(1024)S(1)} %copy-done.10, f32[256]{0:T(256)S(1)} %add_rsqrt_fusion, bf16[256,1152]{1,0:T(8,128)(2,1)} %get-tuple-element.23.dq_ref, bf16[1152,1152]{1,0:T(8,128)(2,1)S(1)} %copy-done), kind=kOutput, calls=%fused_computation.14 | convolution fusion | flops 681540224 | bytes 5024768 | tf_op jit(solution)/shard_map/dot_general | solution.py:20
  76.1 0.0 collective-permute-start.4
  76.1 0.0 copy-done.3
  76.1 0.5 collective-permute-start.3
  76.6 0.7 collective-permute-done.4
  77.3 0.6 collective-permute-start.5
  77.9 1.1 fusion.28.want_ref
  79.0 0.0 copy-done.5
  79.0 0.0 collective-permute-start.2
  79.0 0.0 copy-done.4
  79.0 0.5 collective-permute-start.1
  79.5 20.7 %collective-permute-done.5 = f32[1,1152]{1,0:T(1,128)S(1)} collective-permute-done((f32[1,1152]{1,0:T(1,128)S(1)}, f32[1,1152]{1,0:T(1,128)S(1)}, u32[]{:S(2)}, u32[]{:S(2)}) %collective-permute-start.5) | collective-permute-done | bytes 4640 | tf_op jit(solution)/shard_map/ppermute | solution.py:424
  100.2 0.6 pad_maximum_fusion.gain_ref
  100.8 0.0 collective-permute-done.3.g2_ref
  100.8 0.0 copy-start.6
  100.8 0.0 collective-permute-done.1.o2_ref
  100.8 0.8 copy-done.6
  101.6 0.0 copy-start.7
  101.6 0.8 copy-done.7
  102.5 0.0 collective-permute-done.2.dq2_ref
  102.5 6.6 %weight_parts.1.send_hbm = bf16[32,8,6272]{2,1,0:T(8,128)(2,1)} custom-call(s32[576,1]{1,0:T(8,128)} %fusion.28.want_ref, bf16[576,512]{1,0:T(8,128)(2,1)} %fusion.6.hid_ref, bf16[256,1152]{1,0:T(8,128)(2,1)} %get-tuple-element.22.o_ref, bf16[256,1152]{1,0:T(8,128)(2,1)} %copy-done.7, bf16[256,1152]{1,0:T(8,128)(2,1)} %get-tuple-element.23.dq_ref, ...), custom_call_target="tpu_custom_call" | custom-call | tf_op jit(solution)/shard_map/weight_parts/pallas_call | solution.py:177
  109.0 0.0 all-to-all-done.1.got_hbm
  109.0 4.5 %image_sums.1 = (f32[576,128]{1,0:T(8,128)}, f32[576,128]{1,0:T(8,128)}, bf16[160,512]{1,0:T(8,128)(2,1)}) custom-call(s32[1]{0:T(128)} %bitcast.core_ref, bf16[32,2,40,512]{3,2,1,0:T(8,128)(2,1)} %all-to-all-done.1.got_hbm, bf16[32,2,16,1152]{3,2,1,0:T(8,128)(2,1)} %all-to-all-done.g_hbm), custom_call_target="tpu_custom_call" | custom-call | tf_op jit(solution)/shard_map/image_sums/pallas_call | solution.py:228
  113.5 0.1 collective-permute-start.6
  113.6 1.8 collective-permute-done.6.got_ref
  115.4 0.0 copy-start.8
  115.4 0.7 copy-done.8
  116.1 2.6 %fill_rest.1 = bf16[32,8,6272]{2,1,0:T(8,128)(2,1)} custom-call(bf16[32,8,6272]{2,1,0:T(8,128)(2,1)} %weight_parts.1.send_hbm, f32[576,128]{1,0:T(8,128)} %get-tuple-element.26.mine_ref, f32[576,128]{1,0:T(8,128)} %copy-done.8, bf16[160,512]{1,0:T(8,128)(2,1)} %get-tuple-element.28.tok_ref, ...), custom_call_target="tpu_custom_call", output_to_operand_aliasing={{}: (0, {})} | custom-call | tf_op jit(solution)/shard_map/fill_rest/pallas_call | solution.py:278
  118.8 12.5 %all-to-all-start.2 = ((bf16[32,8,6272]{2,1,0:T(8,128)(2,1)}), bf16[32,8,6272]{2,1,0:T(8,128)(2,1)}, u32[]{:S(2)}, u32[]{:S(2)}) async-start(bf16[32,8,6272]{2,1,0:T(8,128)(2,1)} %fill_rest.1), calls=%async_computation.2 | async-start | bytes 6422528 | tf_op jit(solution)/shard_map/all_to_all | solution.py:436
  131.3 2.4 %fusion.12 = bf16[256,1152]{1,0:T(8,128)(2,1)} fusion(bf16[256,1152]{1,0:T(8,128)(2,1)S(1)} %copy-done.1, f32[256,1152]{1,0:T(8,128)} %get-tuple-element.38, f32[256]{0:T(256)S(1)} %broadcast_multiply_fusion, f32[1152]{0:T(1024)S(1)} %copy-done.10, f32[256]{0:T(256)S(1)} %add_rsqrt_fusion), kind=kLoop, calls=%fused_computation.17 | loop fusion | flops 2064384 | bytes 2365952 | tf_op jit(solution)/shard_map/convert_element_type | solution.py:431
  133.7 38.2 %all-to-all-done.2.recv_hbm = bf16[32,8,6272]{2,1,0:T(8,128)(2,1)} async-done(((bf16[32,8,6272]{2,1,0:T(8,128)(2,1)}), bf16[32,8,6272]{2,1,0:T(8,128)(2,1)}, u32[]{:S(2)}, u32[]{:S(2)}) %all-to-all-start.2) | async-done | bytes 3211296 | tf_op jit(solution)/shard_map/all_to_all | solution.py:436
  171.9 3.5 %group_sums.1 = (f32[9,4,1152]{2,1,0:T(4,128)}, f32[9,4,1152]{2,1,0:T(4,128)}, f32[9,128]{1,0:T(8,128)}) custom-call(s32[1]{0:T(128)} %bitcast.2.yl_ref, bf16[32,8,6272]{2,1,0:T(8,128)(2,1)} %all-to-all-done.2.recv_hbm), custom_call_target="tpu_custom_call" | custom-call | tf_op jit(solution)/shard_map/group_sums/pallas_call | solution.py:344
  175.4 0.0 copy-start.9
  175.4 1.5 collective-permute-start.7
  176.9 4.9 %guide_grad.1 = bf16[32,1152]{1,0:T(8,128)(2,1)} custom-call(bf16[32,8,6272]{2,1,0:T(8,128)(2,1)} %all-to-all-done.2.recv_hbm, bf16[1152,1152]{1,0:T(8,128)(2,1)} %wk_hbm.3, bf16[1152,1152]{1,0:T(8,128)(2,1)} %wv_hbm.3), custom_call_target="tpu_custom_call" | custom-call | tf_op jit(solution)/shard_map/guide_grad/pallas_call | solution.py:384
  181.8 0.0 collective-permute-done.7
  181.8 0.0 copy-done.9
  181.8 0.7 add_bitcast_fusion
  (6 shorter events, 0.1 us)
Async XLA Ops:
  0.6 16.0 %copy-start = (bf16[1152,1152]{1,0:T(8,128)(2,1)S(1)}, bf16[1152,1152]{1,0:T(8,128)(2,1)}, u32[]{:S(2)}) copy-start(bf16[1152,1152]{1,0:T(8,128)(2,1)} %param.13) | copy-start | bytes 7962628
  3.4 11.3 %copy-start.1 = (bf16[256,1152]{1,0:T(8,128)(2,1)S(1)}, bf16[256,1152]{1,0:T(8,128)(2,1)}, u32[]{:S(2)}) copy-start(bf16[256,1152]{1,0:T(8,128)(2,1)} %param.9) | copy-start | bytes 1769476
  3.4 11.5 %copy-start.10 = (f32[1152]{0:T(1024)S(1)}, f32[1152]{0:T(1024)}, u32[]{:S(2)}) copy-start(f32[1152]{0:T(1024)} %param.12) | copy-start | bytes 13828
  3.4 41.4 %all-to-all-start = ((bf16[32,2,16,1152]{3,2,1,0:T(8,128)(2,1)}), bf16[32,2,16,1152]{3,2,1,0:T(8,128)(2,1)}, u32[]{:S(2)}, u32[]{:S(2)}) async-start(bf16[32,2,16,1152]{3,2,1,0:T(8,128)(2,1)} %copies_of_guide.1), calls=%async_computation | async-start | bytes 4718592 | tf_op jit(solution)/shard_map/all_to_all | solution.py:403
  16.0 5.6 %collective-permute-start = (bf16[256,1152]{1,0:T(8,128)(2,1)}, bf16[256,1152]{1,0:T(8,128)(2,1)}, u32[]{:S(2)}, u32[]{:S(2)}) collective-permute-start(bf16[256,1152]{1,0:T(8,128)(2,1)} %fusion.7), channel_id=1, source_target_pairs={{0,32},{32,0},{1,33},{33,1},{2,34},{34,2},{3,35},{35,3},{4,36},{36... | collective-permute-start | bytes 1769480 | tf_op jit(solution)/shard_map/ppermute | solution.py:411
  16.7 3.1 %copy-start.2 = (bf16[256,1152]{1,0:T(8,128)(2,1)S(1)}, bf16[256,1152]{1,0:T(8,128)(2,1)}, u32[]{:S(2)}) copy-start(bf16[256,1152]{1,0:T(8,128)(2,1)} %g_ref.3) | copy-start | bytes 1769476
  16.7 3.0 %copy-start.11 = (bf16[1152,1152]{1,0:T(8,128)(2,1)S(1)}, bf16[1152,1152]{1,0:T(8,128)(2,1)}, u32[]{:S(2)}) copy-start(bf16[1152,1152]{1,0:T(8,128)(2,1)} %param.16) | copy-start | bytes 7962628
  64.5 44.6 %all-to-all-start.1 = ((bf16[32,2,40,512]{3,2,1,0:T(8,128)(2,1)}), bf16[32,2,40,512]{3,2,1,0:T(8,128)(2,1)}, u32[]{:S(2)}, u32[]{:S(2)}) async-start(bf16[32,2,40,512]{3,2,1,0:T(8,128)(2,1)} %get-tuple-element.20), calls=%async_computation.1 | async-start | bytes 5242880 | tf_op jit(solution)/shard_map/all_to_all | solution.py:417
  72.8 3.3 %copy-start.3 = (bf16[256,1152]{1,0:T(8,128)(2,1)S(1)}, bf16[256,1152]{1,0:T(8,128)(2,1)}, u32[]{:S(2)}) copy-start(bf16[256,1152]{1,0:T(8,128)(2,1)} %g_ref.3) | copy-start | bytes 1769476
  72.8 6.2 %copy-start.5 = (bf16[256,1152]{1,0:T(8,128)(2,1)S(1)}, bf16[256,1152]{1,0:T(8,128)(2,1)}, u32[]{:S(2)}) copy-start(bf16[256,1152]{1,0:T(8,128)(2,1)} %get-tuple-element.23.dq_ref) | copy-start | bytes 1769476
  72.9 6.2 %copy-start.4 = (bf16[256,1152]{1,0:T(8,128)(2,1)S(1)}, bf16[256,1152]{1,0:T(8,128)(2,1)}, u32[]{:S(2)}) copy-start(bf16[256,1152]{1,0:T(8,128)(2,1)} %get-tuple-element.22.o_ref) | copy-start | bytes 1769476
  76.1 1.2 collective-permute-start.4
  76.1 24.7 %collective-permute-start.3 = (bf16[256,1152]{1,0:T(8,128)(2,1)S(1)}, bf16[256,1152]{1,0:T(8,128)(2,1)S(1)}, u32[]{:S(2)}, u32[]{:S(2)}) collective-permute-start(bf16[256,1152]{1,0:T(8,128)(2,1)S(1)} %copy-done.3), channel_id=1, source_target_pairs={{0,32},{32,0},{1,33},{33,1},{2,34},{34,2},{3,35},{35,3},{4,36},{36... | collective-permute-start | bytes 1769480 | tf_op jit(solution)/shard_map/ppermute | solution.py:413
  77.3 22.9 %collective-permute-start.5 = (f32[1,1152]{1,0:T(1,128)S(1)}, f32[1,1152]{1,0:T(1,128)S(1)}, u32[]{:S(2)}, u32[]{:S(2)}) collective-permute-start(f32[1,1152]{1,0:T(1,128)S(1)} %reshape_add_fusion), channel_id=1, source_target_pairs={{0,64},{64,0},{1,65},{65,1},{2,66},{66,2},{3,67},{67,3},{4,68},{68... | collective-permute-start | bytes 13832 | tf_op jit(solution)/shard_map/ppermute | solution.py:424
  79.0 23.4 %collective-permute-start.2 = (bf16[256,1152]{1,0:T(8,128)(2,1)S(1)}, bf16[256,1152]{1,0:T(8,128)(2,1)}, u32[]{:S(2)}, u32[]{:S(2)}) collective-permute-start(bf16[256,1152]{1,0:T(8,128)(2,1)S(1)} %copy-done.5), channel_id=1, source_target_pairs={{0,32},{32,0},{1,33},{33,1},{2,34},{34,2},{3,35},{35,3},{4,36},{36... | collective-permute-start | bytes 1769480 | tf_op jit(solution)/shard_map/ppermute | solution.py:419
  79.0 21.8 %collective-permute-start.1 = (bf16[256,1152]{1,0:T(8,128)(2,1)S(1)}, bf16[256,1152]{1,0:T(8,128)(2,1)S(1)}, u32[]{:S(2)}, u32[]{:S(2)}) collective-permute-start(bf16[256,1152]{1,0:T(8,128)(2,1)S(1)} %copy-done.4), channel_id=1, source_target_pairs={{0,32},{32,0},{1,33},{33,1},{2,34},{34,2},{3,35},{35,3},{4,36},{36... | collective-permute-start | bytes 1769480 | tf_op jit(solution)/shard_map/ppermute | solution.py:420
  100.8 0.8 copy-start.6
  101.6 0.8 copy-start.7
  113.5 1.9 %collective-permute-start.6 = (f32[576,128]{1,0:T(8,128)}, f32[576,128]{1,0:T(8,128)S(1)}, u32[]{:S(2)}, u32[]{:S(2)}) collective-permute-start(f32[576,128]{1,0:T(8,128)} %get-tuple-element.27), channel_id=1, source_target_pairs={{0,32},{32,0},{1,33},{33,1},{2,34},{34,2},{3,35},{35,3},{4,36},{36... | collective-permute-start | bytes 884744 | tf_op jit(solution)/shard_map/ppermute | solution.py:435
  115.4 0.7 copy-start.8
  118.8 53.1 %all-to-all-start.2 = ((bf16[32,8,6272]{2,1,0:T(8,128)(2,1)}), bf16[32,8,6272]{2,1,0:T(8,128)(2,1)}, u32[]{:S(2)}, u32[]{:S(2)}) async-start(bf16[32,8,6272]{2,1,0:T(8,128)(2,1)} %fill_rest.1), calls=%async_computation.2 | async-start | bytes 6422528 | tf_op jit(solution)/shard_map/all_to_all | solution.py:436
  175.4 6.5 %copy-start.9 = (f32[9,4,1152]{2,1,0:T(4,128)S(1)}, f32[9,4,1152]{2,1,0:T(4,128)}, u32[]{:S(2)}) copy-start(f32[9,4,1152]{2,1,0:T(4,128)} %get-tuple-element.31) | copy-start | bytes 497668
  175.4 6.4 %collective-permute-start.7 = (f32[9,4,1152]{2,1,0:T(4,128)}, f32[9,4,1152]{2,1,0:T(4,128)S(1)}, u32[]{:S(2)}, u32[]{:S(2)}) collective-permute-start(f32[9,4,1152]{2,1,0:T(4,128)} %get-tuple-element.32), channel_id=1, source_target_pairs={{0,64},{64,0},{1,65},{65,1},{2,66},{66,2},{3,67},{67,3},{4,68},{68... | collective-permute-start | bytes 497672 | tf_op jit(solution)/shard_map/ppermute | solution.py:439
